TPU v7x, 32 devices: a whole 2x2x4 slice. The times are simulated.
32 devices in a mesh: dp: 16 (over z, x, core), seq: 2 (over y).
Axes of the slice: x: 2, y: 2, z: 4, core: 2. Of those that a mesh axis runs over, the one named last changes fastest.
Arguments:
- hidden_in: bfloat16 [4, 16, 512, 768], P(None, 'dp', 'seq'), may hold values from -6 to 6
- segment_ids: int32 [4, 16, 512], P(None, 'dp', 'seq'), may hold values from 0 to 31, as said below
- segment_counts: int32 [4, 16, 32], P(None, 'dp'), may hold values from 1 to 481, as said below
- pooled_grad: float32 [4, 16, 32, 768], P(None, 'dp'), may hold values from -96 to 96
- qkv_weight: bfloat16 [768, 2304], replicated, may hold values from -0.21875 to 0.21875
- query_bias: float32 [768], replicated, may hold values from -3 to 3
- value_bias: float32 [768], replicated, may hold values from -3 to 3
- out_weight: bfloat16 [768, 768], replicated, may hold values from -1.25 to 1.25
- out_bias: float32 [768], replicated, may hold values from -2.5 to 2.5
- norm1_gain: float32 [768], replicated, may hold values from 0.4 to 1.6
- norm1_shift: float32 [768], replicated, may hold values from -2.5 to 2.5
- up_weight: bfloat16 [768, 3072], replicated, may hold values from -0.21875 to 0.21875
- up_bias: float32 [3072], replicated, may hold values from -3 to 3
- down_weight: bfloat16 [3072, 768], replicated, may hold values from -0.15625 to 0.15625
- down_bias: float32 [768], replicated, may hold values from -2.5 to 2.5
- norm2_gain: float32 [768], replicated, may hold values from 0.4 to 1.6
- norm2_shift: float32 [768], replicated, may hold values from -2.5 to 2.5
Outputs:
- pooled: float32 [4, 16, 32, 768], P(None, 'dp')
- grad_input: bfloat16 [4, 16, 512, 768], P(None, 'dp', 'seq')
- grad_qkv_weight: float32 [768, 2304], replicated
- grad_query_bias: float32 [768], replicated
- grad_value_bias: float32 [768], replicated
- grad_out_weight: float32 [768, 768], replicated
- grad_out_bias: float32 [768], replicated
- grad_norm1_gain: float32 [768], replicated
- grad_norm1_shift: float32 [768], replicated
- grad_up_weight: float32 [768, 3072], replicated
- grad_up_bias: float32 [3072], replicated
- grad_down_weight: float32 [3072, 768], replicated
- grad_down_bias: float32 [768], replicated
- grad_norm2_gain: float32 [768], replicated
- grad_norm2_shift: float32 [768], replicated
Inputs may be any that keep to these rules, and one draw needn't show every extreme that they name: `segment_ids`: along a row the segment numbers never fall; every row of 512 positions holds exactly 32 segments, none empty. `segment_counts`: for each row, the number of positions that segment_ids gives each segment, in order of segment number; they sum to 512.
All inputs are finite; a program needn't handle non-finite values.
Results may differ from a plain program's by a relative error of at most 0.009.
Values may be sent and summed in bfloat16 or wider, within the bound.
No kernel may reach another device: no remote copies, remote signals or barrier semaphores. Data moves between devices by JAX's collectives and lax.ppermute only.
A program may use at most 256 MiB of HBM per device.

v0:
```python
import jax
import jax.numpy as jnp
from jax import lax
from jax.sharding import PartitionSpec as P

D = 768
HEADS = 12
HEAD_DIM = 64
FF = 3072
SEGS = 32


NORM_EPS = 1e-05
MASK_FILL = -1e30


def for_sending(value):
    return jax.tree.map(lambda a: a.astype(jnp.bfloat16) if a.dtype == jnp.float32 else a, value)


def norm_forward(total_in, gain_vec, shift_vec):
    row_mean = jnp.mean(total_in, axis=-1, keepdims=True)
    centered = total_in - row_mean
    inv_std = lax.rsqrt(jnp.mean(centered * centered, axis=-1, keepdims=True) + NORM_EPS)
    normed = centered * inv_std
    return (normed * gain_vec + shift_vec, normed, inv_std)


def norm_backward(grad_in, normed, inv_std, gain_vec):
    scaled = grad_in * gain_vec
    inner_part = (
        scaled
        - jnp.mean(scaled, axis=-1, keepdims=True)
        - normed * jnp.mean(scaled * normed, axis=-1, keepdims=True)
    )
    return (inner_part * inv_std, jnp.sum(grad_in * normed, axis=0), jnp.sum(grad_in, axis=0))


def gelu_exact(values_in):
    return jax.nn.gelu(values_in, approximate=False)


def weight_grad(left_arg, right_arg):
    return jnp.einsum("nd,nf->df", left_arg, right_arg, preferred_element_type=jnp.float32)


def back_product(grad_low, weight_mat):
    return jnp.einsum("nf,df->nd", grad_low, weight_mat, preferred_element_type=jnp.float32)


def key_segments(seg_counts, length):
    bounds = jnp.cumsum(seg_counts, axis=-1)
    positions = lax.broadcasted_iota(jnp.int32, (seg_counts.shape[0], length), 1)
    return jnp.sum((positions[:, :, None] >= bounds[:, None, :-1]).astype(jnp.int32), axis=-1)


def masked_scores(queries, keys_heads, query_ids, key_ids, score_scale):
    raw_scores = (
        jnp.einsum("rqhd,rkhd->rhqk", queries, keys_heads, preferred_element_type=jnp.float32)
        * score_scale
    )
    same_seg = query_ids[:, None, :, None] == key_ids[:, None, None, :]
    return jnp.where(same_seg, raw_scores, MASK_FILL)


def local(
    hidden_in,
    segment_ids,
    segment_counts,
    pooled_grad,
    qkv_weight,
    query_bias,
    value_bias,
    out_weight,
    out_bias,
    norm1_gain,
    norm1_shift,
    up_weight,
    up_bias,
    down_weight,
    down_bias,
    norm2_gain,
    norm2_shift,
):
    length = hidden_in.shape[2] * lax.axis_size("seq")
    local_micro = hidden_in.shape[0]
    row_count = hidden_in.shape[1]
    piece_len = hidden_in.shape[2]
    token_count = row_count * piece_len
    score_scale = HEAD_DIM ** (-0.5)
    shift_qkv = jnp.concatenate([query_bias, jnp.zeros((D,), jnp.float32), value_bias])
    seg_range = jnp.arange(SEGS, dtype=jnp.int32)
    totals = None
    pooled_parts = []
    input_parts = []
    for micro_idx in range(local_micro):
        flat_in = hidden_in[micro_idx].reshape(token_count, D)
        seg_counts = segment_counts[micro_idx]
        key_ids = key_segments(seg_counts, length)
        query_ids = segment_ids[micro_idx]
        qkv_proj = (
            jnp.dot(flat_in, qkv_weight, preferred_element_type=jnp.float32) + shift_qkv
        ).astype(jnp.bfloat16)
        queries = qkv_proj[:, :D].reshape(row_count, piece_len, HEADS, HEAD_DIM)
        keys_own = qkv_proj[:, D : 2 * D].reshape(row_count, piece_len, D)
        values_own = qkv_proj[:, 2 * D :].reshape(row_count, piece_len, D)
        keys_all, values_all = (
            lax.all_gather(keys_own, "seq", axis=1, tiled=True),
            lax.all_gather(values_own, "seq", axis=1, tiled=True),
        )
        keys_heads = keys_all.reshape(row_count, length, HEADS, HEAD_DIM)
        values_heads = values_all.reshape(row_count, length, HEADS, HEAD_DIM)
        scores = masked_scores(queries, keys_heads, query_ids, key_ids, score_scale)
        row_max = jnp.max(scores, axis=-1, keepdims=True)
        exps_raw = jnp.exp(scores - row_max)
        total_e = jnp.sum(exps_raw, axis=-1, keepdims=True)
        log_total = row_max + jnp.log(total_e)
        probs_low = (exps_raw / total_e).astype(jnp.bfloat16)
        context = (
            jnp.einsum(
                "rhqk,rkhd->rqhd", probs_low, values_heads, preferred_element_type=jnp.float32
            )
            .reshape(token_count, D)
            .astype(jnp.bfloat16)
        )
        attn_out = jnp.dot(context, out_weight, preferred_element_type=jnp.float32) + out_bias
        mid_out, normed1, inv_std1 = norm_forward(
            flat_in.astype(jnp.float32) + attn_out, norm1_gain, norm1_shift
        )
        mid_low = mid_out.astype(jnp.bfloat16)
        up_pre = jnp.dot(mid_low, up_weight, preferred_element_type=jnp.float32) + up_bias
        act_low = gelu_exact(up_pre).astype(jnp.bfloat16)
        down_out = jnp.dot(act_low, down_weight, preferred_element_type=jnp.float32) + down_bias
        normed_out, normed2, inv_std2 = norm_forward(mid_out + down_out, norm2_gain, norm2_shift)
        member = (query_ids[..., None] == seg_range).astype(jnp.float32)
        partial_value = jnp.einsum(
            "rts,rtd->rsd",
            member,
            normed_out.reshape(row_count, piece_len, D),
            precision=lax.Precision.HIGHEST,
        )
        seg_sums = lax.psum(partial_value.astype(jnp.bfloat16), "seq").astype(jnp.float32)
        seg_size = seg_counts.astype(jnp.float32)[..., None]
        pooled_parts.append(seg_sums / seg_size)
        grad_out = jnp.einsum(
            "rts,rsd->rtd",
            member,
            pooled_grad[micro_idx] / seg_size,
            precision=lax.Precision.HIGHEST,
        ).reshape(token_count, D)
        grad_h2, grad_gain2, grad_shift2 = norm_backward(grad_out, normed2, inv_std2, norm2_gain)
        grad_down_low = grad_h2.astype(jnp.bfloat16)
        grad_down_w = weight_grad(act_low, grad_down_low)
        grad_down_b = jnp.sum(grad_down_low.astype(jnp.float32), axis=0)
        grad_act = back_product(grad_down_low, down_weight)
        gelu_unused, gelu_pull = jax.vjp(gelu_exact, up_pre)
        grad_up_low = gelu_pull(grad_act)[0].astype(jnp.bfloat16)
        grad_up_w = weight_grad(mid_low, grad_up_low)
        grad_up_b = jnp.sum(grad_up_low.astype(jnp.float32), axis=0)
        grad_mid = grad_h2 + back_product(grad_up_low, up_weight)
        grad_h1, grad_gain1, grad_shift1 = norm_backward(grad_mid, normed1, inv_std1, norm1_gain)
        grad_attn_low = grad_h1.astype(jnp.bfloat16)
        grad_out_w = weight_grad(context, grad_attn_low)
        grad_out_b = jnp.sum(grad_attn_low.astype(jnp.float32), axis=0)
        grad_context = (
            back_product(grad_attn_low, out_weight)
            .astype(jnp.bfloat16)
            .reshape(row_count, piece_len, HEADS, HEAD_DIM)
        )
        probs_back = jnp.exp(
            masked_scores(queries, keys_heads, query_ids, key_ids, score_scale) - log_total
        )
        probs_back_low = probs_back.astype(jnp.bfloat16)
        grad_probs = jnp.einsum(
            "rqhd,rkhd->rhqk", grad_context, values_heads, preferred_element_type=jnp.float32
        )
        grad_scores = (
            probs_back * (grad_probs - jnp.sum(probs_back * grad_probs, axis=-1, keepdims=True))
        ).astype(jnp.bfloat16)
        grad_queries = (
            jnp.einsum(
                "rhqk,rkhd->rqhd", grad_scores, keys_heads, preferred_element_type=jnp.float32
            )
            * score_scale
        )
        grad_keys = (
            jnp.einsum("rhqk,rqhd->rkhd", grad_scores, queries, preferred_element_type=jnp.float32)
            * score_scale
        )
        grad_values = jnp.einsum(
            "rhqk,rqhd->rkhd", probs_back_low, grad_context, preferred_element_type=jnp.float32
        )
        grad_keys_own, grad_values_own = (
            lax.psum_scatter(
                grad_keys.reshape(row_count, length, D).astype(jnp.bfloat16),
                "seq",
                scatter_dimension=1,
                tiled=True,
            ).astype(jnp.float32),
            lax.psum_scatter(
                grad_values.reshape(row_count, length, D).astype(jnp.bfloat16),
                "seq",
                scatter_dimension=1,
                tiled=True,
            ).astype(jnp.float32),
        )
        grad_qkv = jnp.concatenate(
            [
                grad_queries.reshape(token_count, D),
                grad_keys_own.reshape(token_count, D),
                grad_values_own.reshape(token_count, D),
            ],
            axis=1,
        ).astype(jnp.bfloat16)
        grad_qkv_w = weight_grad(flat_in, grad_qkv)
        grad_qkv_f = grad_qkv.astype(jnp.float32)
        grad_query_b = jnp.sum(grad_qkv_f[:, :D], axis=0)
        grad_value_b = jnp.sum(grad_qkv_f[:, 2 * D :], axis=0)
        grad_flat = grad_h1 + back_product(grad_qkv, qkv_weight)
        input_parts.append(grad_flat.astype(jnp.bfloat16).reshape(row_count, piece_len, D))
        small_grads = jnp.concatenate(
            [
                grad_query_b,
                grad_value_b,
                grad_out_b,
                grad_gain1,
                grad_shift1,
                grad_up_b,
                grad_down_b,
                grad_gain2,
                grad_shift2,
            ]
        )
        local_grads = (
            grad_qkv_w.reshape(-1),
            grad_out_w.reshape(-1),
            grad_up_w.reshape(-1),
            grad_down_w.reshape(-1),
            small_grads,
        )
        totals = (
            local_grads if totals is None else tuple((a + b for a, b in zip(totals, local_grads)))
        )
    totals = lax.psum_scatter(totals, ("dp", "seq"), scatter_dimension=0, tiled=True)
    whole_grads = jax.tree.map(
        lambda part, own: part.astype(own.dtype),
        lax.all_gather(for_sending(totals), ("dp", "seq"), axis=0, tiled=True),
        totals,
    )
    small_all = whole_grads[4]
    pooled_local = jnp.stack(pooled_parts, axis=0)
    input_local = jnp.stack(input_parts, axis=0)
    return (
        pooled_local,
        input_local,
        whole_grads[0].reshape(D, 3 * D),
        small_all[0:D],
        small_all[D : 2 * D],
        whole_grads[1].reshape(D, D),
        small_all[2 * D : 3 * D],
        small_all[3 * D : 4 * D],
        small_all[4 * D : 5 * D],
        whole_grads[2].reshape(D, FF),
        small_all[5 * D : 5 * D + FF],
        whole_grads[3].reshape(FF, D),
        small_all[5 * D + FF : 6 * D + FF],
        small_all[6 * D + FF : 7 * D + FF],
        small_all[7 * D + FF : 8 * D + FF],
    )


def solution(mesh):
    in_specs = (
        P(None, "dp", "seq", None),
        P(None, "dp", "seq"),
        P(None, "dp", None),
        P(None, "dp", None, None),
        P(),
        P(),
        P(),
        P(),
        P(),
        P(),
        P(),
        P(),
        P(),
        P(),
        P(),
        P(),
        P(),
    )
    out_specs = (
        P(None, "dp", None, None),
        P(None, "dp", "seq", None),
        P(),
        P(),
        P(),
        P(),
        P(),
        P(),
        P(),
        P(),
        P(),
        P(),
        P(),
        P(),
        P(),
    )
    return jax.shard_map(local, mesh=mesh, in_specs=in_specs, out_specs=out_specs, check_vma=False)
```

profile of v0, /device:TPU:0, one launch (start us, length us, event | category | flops | bytes accessed | tf_op | source)
XLA Modules:
  0.0 1245.3 jit_solution(11774226197422313115)
XLA Ops:
  18.8 13.0 %all-gather.6 = bf16[512,768]{1,0:T(8,128)(2,1)} all-gather(bf16[256,768]{1,0:T(8,128)(2,1)S(1)} %get-tuple-element.99), channel_id=8, replica_groups=mesh['dp'=16,'seq'=2] {'seq'}, dimensions={0}, use_global_device_ids=true | all-gather | bytes 1179648 | tf_op jit(solution)/shard_map/all_gather | solution.py:109
  36.0 13.0 %all-gather.7 = bf16[512,768]{1,0:T(8,128)(2,1)} all-gather(bf16[256,768]{1,0:T(8,128)(2,1)} %get-tuple-element.97), channel_id=9, replica_groups=mesh['dp'=16,'seq'=2] {'seq'}, dimensions={0}, use_global_device_ids=true | all-gather | bytes 1179648 | tf_op jit(solution)/shard_map/all_gather | solution.py:108
  63.6 11.0 multiply_convert_fusion.4
  78.9 10.1 all-gather.4
  93.3 10.9 all-gather.5
  108.8 2.5 fusion.241
  118.9 11.1 multiply_convert_fusion.5
  134.2 8.8 all-gather.2
  147.2 9.3 all-gather.3
  160.7 2.5 fusion.244
  170.8 11.1 multiply_convert_fusion.6
  186.2 8.5 all-gather
  199.0 9.9 all-gather.1
  213.0 2.5 fusion.247
  223.1 11.1 multiply_convert_fusion.7
  244.5 2.7 convert_reduce_fusion.2
  250.7 2.7 convert_reduce_fusion.3
  256.8 2.7 convert_reduce_fusion.1
  263.0 2.9 convert_reduce_fusion
  266.0 3.5 convert_reduce_fusion.11
  276.0 4.8 fusion.58
  280.9 5.2 multiply_reduce_fusion.1
  286.1 3.9 multiply_convert_fusion.1
  293.4 2.8 convolution_convert_fusion.3
  298.9 5.0 fusion.52
  303.9 5.2 multiply_reduce_fusion.3
  309.2 3.7 multiply_convert_fusion.3
  316.3 2.8 convolution_convert_fusion.2
  321.7 5.0 fusion.55
  326.8 5.2 multiply_reduce_fusion.2
  332.0 3.7 multiply_convert_fusion.2
  339.1 2.8 convolution_convert_fusion
  344.5 5.3 fusion.61
  349.9 5.3 multiply_reduce_fusion
  355.1 3.7 multiply_convert_fusion
  372.1 4.2 fusion.79
  386.4 5.3 fusion.219
  391.7 5.3 fusion.225
  397.1 5.2 fusion.222
  402.3 5.1 fusion.189
  407.5 5.1 fusion.207
  412.6 5.3 fusion.198
  419.8 3.2 add.473
  423.1 11.9 add_bitcast_fusion
  435.0 5.9 copy.115
  441.0 14.7 %add_add_fusion = f32[3072,768]{1,0:T(8,128)} fusion(f32[3072,768]{1,0:T(8,128)} %fusion.189, f32[3072,768]{1,0:T(8,128)} %fusion.207, f32[3072,768]{1,0:T(8,128)} %fusion.198, bf16[256,3072]{1,0:T(8,128)(2,1)S(1)} %copy-done.78, f32[256,768]{1,0:T(8,128)S(1)} %copy-done.67), kind=kOutput, calls=%fused_computation | convolution fusion | flops 1215234048 | bytes 40108032 | tf_op jit(solution)/shard_map/nd,nf->df/dot_general | solution.py:44
  455.7 10.8 add.481
  466.4 5.5 fusion.106
  473.6 5.5 fusion.112
  480.7 5.4 fusion.109
  487.7 3.0 fusion.213
  490.7 11.5 add_bitcast_fusion.1
  502.2 8.0 copy.114
  510.2 8.1 add.466
  524.1 456.5 %all-reduce.12 = (bf16[1769472]{0:T(1024)(128)(2,1)}, bf16[9216]{0:T(1024)(128)(2,1)}, bf16[589824]{0:T(1024)(128)(2,1)}, bf16[2359296]{0:T(1024)(128)(2,1)}, bf16[2359296]{0:T(1024)(128)(2,1)}) all-reduce(f32[1769472]{0:T(1024)} %add.466, f32[9216]{0:T(1024)} %add_add_fusion.2, ...), channel_id=18, replica_groups=mesh['dp'=16,'seq'=2] {'dp','seq'}, use_global_device_ids=true, to_apply=%region_64.65.clone | all-reduce | flops 7087104 | bytes 42522624
  992.4 39.4 %all-reduce = bf16[9216]{0:T(1024)(128)(2,1)} all-reduce(bf16[9216]{0:T(1024)(128)(2,1)} %dynamic-update-slice), channel_id=1, replica_groups=mesh['dp'=16,'seq'=2] {'dp','seq'}, use_global_device_ids=true, to_apply=%add | all-reduce | flops 9216 | bytes 36864
  1033.1 2.8 fusion.84
  1042.0 3.4 reshape.1601
  1045.4 52.0 %all-gather.13.cloned.1.call-done = bf16[1769472]{0:T(1024)(128)(2,1)} async-done(((bf16[55296]{0:T(1024)(128)(2,1)}), bf16[1769472]{0:T(1024)(128)(2,1)}) %all-gather.13.cloned.1.call-update) | async-done | bytes 3538960 | tf_op jit(solution)/shard_map/all_gather | solution.py:247
  1097.3 7.9 reshape.1599
  1105.3 57.9 %all-gather.17.cloned.1.call-done = bf16[2359296]{0:T(1024)(128)(2,1)} async-done(((bf16[73728]{0:T(1024)(128)(2,1)}), bf16[2359296]{0:T(1024)(128)(2,1)}) %all-gather.17.cloned.1.call-update) | async-done | bytes 4718608 | tf_op jit(solution)/shard_map/all_gather | solution.py:247
  1163.2 8.7 reshape.1603
  1171.9 56.7 %all-gather.19.cloned.1.call-done = bf16[2359296]{0:T(1024)(128)(2,1)} async-done(((bf16[73728]{0:T(1024)(128)(2,1)}), bf16[2359296]{0:T(1024)(128)(2,1)}) %all-gather.19.cloned.1.call-update) | async-done | bytes 4718608 | tf_op jit(solution)/shard_map/all_gather | solution.py:247
  1228.6 10.0 reshape.1605
  (722 shorter events, 189.2 us)
Async XLA Ops:
  7.2 459.2 %reduce-scatter.19.cloned.1.call-start = ((), (), s32[]{:S(2)}) async-start(), calls=%async_computation.13 | async-start | bytes 1179648 | tf_op jit(solution)/shard_map/reduce_scatter | solution.py:200
  18.8 32.5 %copy-start.206 = (s32[4,1,32]{2,1,0:T(1,128)S(1)}, s32[4,1,32]{2,1,0:T(1,128)}, u32[]{:S(2)}) copy-start(s32[4,1,32]{2,1,0:T(1,128)} %param.19) | copy-start | bytes 1540
  18.8 33.5 %copy-start.190 = (s32[4,1,256]{2,1,0:T(1,128)S(1)}, s32[4,1,256]{2,1,0:T(1,128)}, u32[]{:S(2)}) copy-start(s32[4,1,256]{2,1,0:T(1,128)} %param.18) | copy-start | bytes 12292
  52.8 55.8 %copy-start.147 = (s32[1,1,256]{2,1,0:T(1,128)}, s32[1,1,256]{2,1,0:T(1,128)S(1)}, u32[]{:S(2)}) copy-start(s32[1,1,256]{2,1,0:T(1,128)S(1)} %get-tuple-element.143) | copy-start | bytes 3076
  56.0 7.5 slice-start.8
  61.4 13.2 %copy-start.108 = (bf16[12,64,256]{2,1,0:T(8,128)(2,1)}, bf16[12,64,256]{2,1,0:T(8,128)(2,1)S(1)}, u32[]{:S(2)}) copy-start(bf16[12,64,256]{2,1,0:T(8,128)(2,1)S(1)} %fusion.80) | copy-start | bytes 1179652
  61.5 13.2 %slice-start = ((s8[4718592]{0:T(1024)(128)(4,1)}), s8[4194304]{0:T(1024)(128)(4,1)S(1)}, s32[]{:S(2)}) async-start(s8[4718592]{0:T(1024)(128)(4,1)} %bitcast.410), calls=%async_computation.21 | async-start | bytes 8388608
  63.2 11.4 copy-start.30
  63.3 11.4 copy-start.157
  63.6 11.1 copy-start.178
  63.6 11.1 slice-start.1
  63.6 11.1 copy-start.215
  76.2 164.9 %copy-start.131 = (f32[256]{0:T(256)}, f32[256]{0:T(256)S(1)}, u32[]{:S(2)}) copy-start(f32[256]{0:T(256)S(1)} %broadcast_multiply_fusion.16) | copy-start | bytes 3076
  111.4 7.5 slice-start.10
  116.8 13.2 %copy-start.103 = (bf16[12,64,256]{2,1,0:T(8,128)(2,1)}, bf16[12,64,256]{2,1,0:T(8,128)(2,1)S(1)}, u32[]{:S(2)}) copy-start(bf16[12,64,256]{2,1,0:T(8,128)(2,1)S(1)} %fusion.81) | copy-start | bytes 1179652
  116.8 13.2 %slice-start.2 = ((s8[4718592]{0:T(1024)(128)(4,1)}), s8[4194304]{0:T(1024)(128)(4,1)S(1)}, s32[]{:S(2)}) async-start(s8[4718592]{0:T(1024)(128)(4,1)} %bitcast.412), calls=%async_computation.23 | async-start | bytes 8388608
  118.6 11.4 copy-start.32
  118.6 11.4 copy-start.134
  118.9 11.1 copy-start.166
  118.9 11.1 slice-start.3
  118.9 11.1 copy-start.216
  131.6 15.6 %copy-start.132 = (f32[256]{0:T(256)}, f32[256]{0:T(256)S(1)}, u32[]{:S(2)}) copy-start(f32[256]{0:T(256)S(1)} %broadcast_multiply_fusion.18) | copy-start | bytes 3076
  163.3 7.5 slice-start.12
  166.5 15.4 %slice-start.4 = ((s8[4718592]{0:T(1024)(128)(4,1)}), s8[524288]{0:T(1024)(128)(4,1)S(1)}, s32[]{:S(2)}) async-start(s8[4718592]{0:T(1024)(128)(4,1)} %bitcast.414), calls=%async_computation.25 | async-start | bytes 1048576
  168.7 13.2 %copy-start.104 = (bf16[12,64,256]{2,1,0:T(8,128)(2,1)}, bf16[12,64,256]{2,1,0:T(8,128)(2,1)S(1)}, u32[]{:S(2)}) copy-start(bf16[12,64,256]{2,1,0:T(8,128)(2,1)S(1)} %fusion.82) | copy-start | bytes 1179652
  170.5 11.4 copy-start.35
  170.5 11.4 copy-start.137
  170.8 11.1 copy-start.169
  170.8 11.1 slice-start.5
  170.8 11.1 copy-start.217
  183.5 15.5 %copy-start.162 = (f32[256]{0:T(256)}, f32[256]{0:T(256)S(1)}, u32[]{:S(2)}) copy-start(f32[256]{0:T(256)S(1)} %broadcast_multiply_fusion.20) | copy-start | bytes 3076
  215.6 7.5 slice-start.14
  218.8 15.5 %slice-start.6 = ((s8[4718592]{0:T(1024)(128)(4,1)}), s8[4194304]{0:T(1024)(128)(4,1)S(1)}, s32[]{:S(2)}) async-start(s8[4718592]{0:T(1024)(128)(4,1)} %bitcast.416), calls=%async_computation.27 | async-start | bytes 8388608
  222.8 43.1 %copy-start.61 = (f32[256,768]{1,0:T(8,128)}, f32[256,768]{1,0:T(8,128)S(1)}, u32[]{:S(2)}) copy-start(f32[256,768]{1,0:T(8,128)S(1)} %get-tuple-element.176) | copy-start | bytes 2359300
  222.8 43.1 %copy-start.160 = (f32[256]{0:T(256)}, f32[256]{0:T(256)S(1)}, u32[]{:S(2)}) copy-start(f32[256]{0:T(256)S(1)} %broadcast_multiply_fusion.23) | copy-start | bytes 3076
  223.1 42.8 %copy-start.181 = (f32[256]{0:T(256)}, f32[256]{0:T(256)S(1)}, u32[]{:S(2)}) copy-start(f32[256]{0:T(256)S(1)} %add_rsqrt_fusion.7) | copy-start | bytes 3076
  223.1 11.1 slice-start.7
  223.1 11.1 copy-start.218
  241.1 12.3 copy-start.52
  243.1 16.5 %copy-start.56 = (f32[256,768]{1,0:T(8,128)}, f32[256,768]{1,0:T(8,128)S(1)}, u32[]{:S(2)}) copy-start(f32[256,768]{1,0:T(8,128)S(1)} %get-tuple-element.139) | copy-start | bytes 2359300
  243.1 22.8 %copy-start.66 = (f32[256,768]{1,0:T(8,128)}, f32[256,768]{1,0:T(8,128)S(1)}, u32[]{:S(2)}) copy-start(f32[256,768]{1,0:T(8,128)S(1)} %get-tuple-element.137) | copy-start | bytes 2359300
  280.9 185.6 %reduce-scatter.17.cloned.1.call-start = ((), (), s32[]{:S(2)}) async-start(), calls=%async_computation.12 | async-start | bytes 1179648 | tf_op jit(solution)/shard_map/reduce_scatter | solution.py:194
  286.1 5.6 copy-start.50
  293.4 180.2 %reduce-scatter.11.cloned.1.call-start = ((), (), s32[]{:S(2)}) async-start(), calls=%async_computation.9 | async-start | bytes 1179648 | tf_op jit(solution)/shard_map/reduce_scatter | solution.py:200
  303.9 169.7 %reduce-scatter.9.cloned.1.call-start = ((), (), s32[]{:S(2)}) async-start(), calls=%async_computation.8 | async-start | bytes 1179648 | tf_op jit(solution)/shard_map/reduce_scatter | solution.py:194
  316.0 164.6 %reduce-scatter.15.cloned.1.call-start = ((), (), s32[]{:S(2)}) async-start(), calls=%async_computation.11 | async-start | bytes 1179648 | tf_op jit(solution)/shard_map/reduce_scatter | solution.py:200
  326.7 153.9 %reduce-scatter.13.cloned.1.call-start = ((), (), s32[]{:S(2)}) async-start(), calls=%async_computation.10 | async-start | bytes 1179648 | tf_op jit(solution)/shard_map/reduce_scatter | solution.py:194
  339.0 148.7 %reduce-scatter.23.cloned.1.call-start = ((), (), s32[]{:S(2)}) async-start(), calls=%async_computation.15 | async-start | bytes 1179648 | tf_op jit(solution)/shard_map/reduce_scatter | solution.py:200
  349.8 137.9 %reduce-scatter.21.cloned.1.call-start = ((), (), s32[]{:S(2)}) async-start(), calls=%async_computation.14 | async-start | bytes 1179648 | tf_op jit(solution)/shard_map/reduce_scatter | solution.py:194
  362.1 624.9 %all-reduce.11.cloned.1.call-start = ((), (), s32[]{:S(2)}) async-start(), calls=%async_computation.20 | async-start | bytes 393216 | tf_op jit(solution)/shard_map/psum | solution.py:142
  371.6 670.4 %all-gather.15.cloned.1.call-start = ((), (), s32[]{:S(2)}) async-start(), calls=%async_computation.17 | async-start | bytes 1216512 | tf_op jit(solution)/shard_map/all_gather | solution.py:247
  435.0 6.0 copy-start.67
  435.0 6.0 copy-start.78
  466.4 5.5 copy-start.46
  466.4 5.5 copy-start.80
  473.5 5.5 copy-start.42
  473.5 5.5 copy-start.84
  524.1 462.9 %copy-start.187 = (f32[32]{0:T(128)S(1)}, f32[32]{0:T(128)}, u32[]{:S(2)}) copy-start(f32[32]{0:T(128)} %get-tuple-element.146) | copy-start | bytes 388
  524.1 462.9 %copy-start.189 = (f32[32]{0:T(128)S(1)}, f32[32]{0:T(128)}, u32[]{:S(2)}) copy-start(f32[32]{0:T(128)} %get-tuple-element.147) | copy-start | bytes 388
  524.1 463.8 %copy-start.185 = (f32[32]{0:T(128)S(1)}, f32[32]{0:T(128)}, u32[]{:S(2)}) copy-start(f32[32]{0:T(128)} %get-tuple-element.145) | copy-start | bytes 388
  524.1 463.9 %copy-start.205 = (f32[32]{0:T(128)S(1)}, f32[32]{0:T(128)}, u32[]{:S(2)}) copy-start(f32[32]{0:T(128)} %get-tuple-element.144) | copy-start | bytes 388
  982.0 115.3 %all-gather.13.cloned.1.call-start = ((), (), s32[]{:S(2)}) async-start(), calls=%async_computation.16 | async-start | bytes 3649536 | tf_op jit(solution)/shard_map/all_gather | solution.py:247
  983.7 179.5 %all-gather.17.cloned.1.call-start = ((), (), s32[]{:S(2)}) async-start(), calls=%async_computation.18 | async-start | bytes 4866048 | tf_op jit(solution)/shard_map/all_gather | solution.py:247
  985.3 243.2 %all-gather.19.cloned.1.call-start = ((), (), s32[]{:S(2)}) async-start(), calls=%async_computation.19 | async-start | bytes 4866048 | tf_op jit(solution)/shard_map/all_gather | solution.py:247
  (192 other events, 643.2 us)
Sparse Core Ops, SparseCore 0:
  281.0 17.8 reduce-scatter.18
  301.2 17.4 reduce-scatter.16
  320.9 17.4 reduce-scatter.10
  340.6 17.4 reduce-scatter.8
  360.1 17.4 reduce-scatter.14
  379.8 17.4 reduce-scatter.12
  399.5 17.4 reduce-scatter.22
  419.3 17.4 reduce-scatter.20
  439.8 22.7 all-reduce.10
  982.2 52.4 all-gather.14
  1038.2 59.1 all-gather.12
  1100.7 62.4 all-gather.16
  1166.1 62.4 all-gather.18
where the time goes:
time: 1250 us
  blocking collectives  579 us (46%)
  matrix products  282 us (23%)
  waiting for transfers between devices  167 us (13%)
  local copies, waits for them, and re-layouts  143 us (11%)
  other arithmetic  55.6 us (4%)
  between operations  17.5 us (1%)
    unnamed x2, blocking collectives  496 us
    all_gather x4, waiting for transfers between devices, local(): lax.all_gather(for_sending(totals), ('dp', 'seq'), axis=0, tiled=True)  167 us
    dot_general x16, matrix products, weight_grad(): jnp.einsum('nd,nf->df', left_arg, right_arg, preferred_element_type=jnp.f...  90.6 us
    dot_general x4, matrix products, local(): jnp.dot(mid_low, up_weight, preferred_element_type=jnp.float32) + up_bias  44.2 us
    all_gather x4, blocking collectives, local(): lax.all_gather(keys_own, 'seq', axis=1, tiled=True)  43.1 us
    unnamed x526, local copies, waits for them, and re-layouts  41.8 us
    all_gather x4, blocking collectives, local(): lax.all_gather(values_own, 'seq', axis=1, tiled=True)  40.4 us
    dot_general x16, matrix products, back_product(): jnp.einsum('nf,df->nd', grad_low, weight_mat, preferred_element_type=jnp....  35.8 us
  transfers between devices with their start and end apart: 13, of which 3 were waited for; matrix products, arithmetic and copies ran while one was open for 22% of the time, Pallas kernels for 0%

commit v1 on v0

v1 whole, which is shorter than its diff:
```python
import jax
import jax.numpy as jnp
from jax import lax
from jax.sharding import PartitionSpec as P

D = 768
HEADS = 12
HEAD_DIM = 64
FF = 3072
SEGS = 32

NORM_EPS = 1e-05
MASK_FILL = -1e30
BF = jnp.bfloat16
F32 = jnp.float32


def norm_forward(total_in, gain_vec, shift_vec):
    row_mean = jnp.mean(total_in, axis=-1, keepdims=True)
    centered = total_in - row_mean
    inv_std = lax.rsqrt(jnp.mean(centered * centered, axis=-1, keepdims=True) + NORM_EPS)
    normed = centered * inv_std
    return (normed * gain_vec + shift_vec, normed, inv_std)


def norm_backward(grad_in, normed, inv_std, gain_vec):
    scaled = grad_in * gain_vec
    inner_part = (
        scaled
        - jnp.mean(scaled, axis=-1, keepdims=True)
        - normed * jnp.mean(scaled * normed, axis=-1, keepdims=True)
    )
    return (inner_part * inv_std, jnp.sum(grad_in * normed, axis=0), jnp.sum(grad_in, axis=0))


def weight_grad(left_arg, right_arg):
    return jnp.einsum("nd,nf->df", left_arg, right_arg, preferred_element_type=F32)


def back_product(grad_low, weight_mat):
    return jnp.einsum("nf,df->nd", grad_low, weight_mat, preferred_element_type=F32)


class Links:
    def __init__(self):
        self.dp = lax.axis_size("dp")
        self.seq = lax.axis_size("seq")
        dp_at = lax.axis_index("dp")
        seq_at = lax.axis_index("seq")
        core = dp_at % 2

        def flip(bit_of):
            pairs = []
            for d in range(self.dp):
                for s in range(self.seq):
                    bit = bit_of(d % 2)
                    to = (d, s ^ 1) if bit < 0 else (d ^ (1 << bit), s)
                    pairs.append((d * self.seq + s, to[0] * self.seq + to[1]))
            return pairs

        def side(bit):
            return seq_at if bit < 0 else (dp_at >> bit) % 2

        self.stages = [
            (flip(lambda c: 0), core),
            (flip(lambda c: 1 if c == 0 else -1), jnp.where(core == 0, side(1), side(-1))),
            (flip(lambda c: -1 if c == 0 else 1), jnp.where(core == 0, side(-1), side(1))),
        ]
        bits = (self.dp - 1).bit_length()
        for bit in range(2, bits):
            self.stages.append((flip(lambda c, bit=bit: bit), side(bit)))

    def scatter_sum(self, full):
        cur = full
        for pairs, at in self.stages:
            half = cur.shape[0] // 2
            send = lax.dynamic_slice_in_dim(cur, (1 - at) * half, half, 0).astype(BF)
            keep = lax.dynamic_slice_in_dim(cur, at * half, half, 0)
            recv = lax.ppermute(send, ("dp", "seq"), pairs)
            cur = keep.astype(F32) + recv.astype(F32)
        return cur.astype(BF)

    def gather(self, part):
        cur = part
        for pairs, at in reversed(self.stages):
            recv = lax.ppermute(cur, ("dp", "seq"), pairs)
            cur = jnp.where(at == 0, jnp.concatenate([cur, recv]), jnp.concatenate([recv, cur]))
        return cur


def swap_seq(value):
    return lax.ppermute(value, "seq", [(0, 1), (1, 0)])


def local(
    hidden_in,
    segment_ids,
    segment_counts,
    pooled_grad,
    qkv_weight,
    query_bias,
    value_bias,
    out_weight,
    out_bias,
    norm1_gain,
    norm1_shift,
    up_weight,
    up_bias,
    down_weight,
    down_bias,
    norm2_gain,
    norm2_shift,
):
    links = Links()
    seq_at = lax.axis_index("seq")
    micro, row_count, piece, _ = hidden_in.shape
    length = piece * 2
    own_micro = micro // 2
    rows = own_micro * row_count
    tokens = rows * length
    score_scale = HEAD_DIM ** (-0.5)

    def own_part(value):
        return lax.dynamic_slice_in_dim(value, seq_at * own_micro, own_micro, 0)

    def other_part(value):
        return lax.dynamic_slice_in_dim(value, (1 - seq_at) * own_micro, own_micro, 0)

    got = swap_seq(other_part(hidden_in))
    mine = own_part(hidden_in)
    full_rows = jnp.where(
        seq_at == 0,
        jnp.concatenate([mine, got], axis=2),
        jnp.concatenate([got, mine], axis=2),
    )
    flat_in = full_rows.reshape(tokens, D)
    counts = own_part(segment_counts).reshape(rows, SEGS)
    grads_pooled = own_part(pooled_grad).reshape(rows, SEGS, D)
    ends = jnp.sum(
        jnp.where(jnp.arange(SEGS)[None, :, None] <= jnp.arange(SEGS)[None, None, :], counts[:, :, None], 0),
        axis=1,
    )
    positions = jnp.arange(length, dtype=jnp.int32)
    ids = jnp.sum((positions[None, :, None] >= ends[:, None, :-1]).astype(jnp.int32), axis=-1)
    same_seg = ids[:, None, :, None] == ids[:, None, None, :]
    shift_qkv = jnp.concatenate([query_bias, jnp.zeros((D,), F32), value_bias])
    qkv_proj = (jnp.dot(flat_in, qkv_weight, preferred_element_type=F32) + shift_qkv).astype(BF)
    queries = qkv_proj[:, :D].reshape(rows, length, HEADS, HEAD_DIM)
    keys = qkv_proj[:, D : 2 * D].reshape(rows, length, HEADS, HEAD_DIM)
    values = qkv_proj[:, 2 * D :].reshape(rows, length, HEADS, HEAD_DIM)
    scores = jnp.where(
        same_seg,
        jnp.einsum("rqhd,rkhd->rhqk", queries, keys, preferred_element_type=F32) * score_scale,
        MASK_FILL,
    )
    row_max = jnp.max(scores, axis=-1, keepdims=True)
    exps = jnp.exp(scores - row_max)
    total_e = jnp.sum(exps, axis=-1, keepdims=True)
    log_total = row_max + jnp.log(total_e)
    probs_low = (exps / total_e).astype(BF)
    context = (
        jnp.einsum("rhqk,rkhd->rqhd", probs_low, values, preferred_element_type=F32)
        .reshape(tokens, D)
        .astype(BF)
    )
    attn_out = jnp.dot(context, out_weight, preferred_element_type=F32) + out_bias
    mid_out, normed1, inv_std1 = norm_forward(
        flat_in.astype(F32) + attn_out, norm1_gain, norm1_shift
    )
    mid_low = mid_out.astype(BF)
    up_pre = jnp.dot(mid_low, up_weight, preferred_element_type=F32) + up_bias
    cdf = 0.5 * (1.0 + lax.erf(up_pre * (0.5**0.5)))
    act_low = (up_pre * cdf).astype(BF)
    down_out = jnp.dot(act_low, down_weight, preferred_element_type=F32) + down_bias
    normed_out, normed2, inv_std2 = norm_forward(mid_out + down_out, norm2_gain, norm2_shift)
    member = (ids[..., None] == jnp.arange(SEGS, dtype=jnp.int32)).astype(F32)
    seg_size = counts.astype(F32)[..., None]
    pooled_own = (
        jnp.einsum(
            "rts,rtd->rsd",
            member,
            normed_out.reshape(rows, length, D),
            precision=lax.Precision.HIGHEST,
        )
        / seg_size
    ).reshape(own_micro, row_count, SEGS, D)
    pooled_got = swap_seq(pooled_own)
    pooled_local = jnp.where(
        seq_at == 0,
        jnp.concatenate([pooled_own, pooled_got]),
        jnp.concatenate([pooled_got, pooled_own]),
    )
    grad_out = jnp.einsum(
        "rts,rsd->rtd", member, grads_pooled / seg_size, precision=lax.Precision.HIGHEST
    ).reshape(tokens, D)
    grad_h2, grad_gain2, grad_shift2 = norm_backward(grad_out, normed2, inv_std2, norm2_gain)
    grad_down_low = grad_h2.astype(BF)
    grad_down_w = links.scatter_sum(weight_grad(act_low, grad_down_low).astype(BF))
    grad_down_b = jnp.sum(grad_down_low.astype(F32), axis=0)
    grad_act = back_product(grad_down_low, down_weight)
    slope = cdf + up_pre * (jnp.exp(-0.5 * up_pre * up_pre) * 0.3989422804014327)
    grad_up_low = (grad_act * slope).astype(BF)
    grad_up_w = links.scatter_sum(weight_grad(mid_low, grad_up_low).astype(BF))
    grad_up_b = jnp.sum(grad_up_low.astype(F32), axis=0)
    grad_mid = grad_h2 + back_product(grad_up_low, up_weight)
    grad_h1, grad_gain1, grad_shift1 = norm_backward(grad_mid, normed1, inv_std1, norm1_gain)
    grad_attn_low = grad_h1.astype(BF)
    grad_out_w = weight_grad(context, grad_attn_low).astype(BF)
    grad_out_b = jnp.sum(grad_attn_low.astype(F32), axis=0)
    grad_context = (
        back_product(grad_attn_low, out_weight).astype(BF).reshape(rows, length, HEADS, HEAD_DIM)
    )
    probs_back = jnp.exp(scores - log_total)
    probs_back_low = probs_back.astype(BF)
    grad_probs = jnp.einsum("rqhd,rkhd->rhqk", grad_context, values, preferred_element_type=F32)
    grad_scores = (
        probs_back * (grad_probs - jnp.sum(probs_back * grad_probs, axis=-1, keepdims=True))
    ).astype(BF)
    grad_queries = (
        jnp.einsum("rhqk,rkhd->rqhd", grad_scores, keys, preferred_element_type=F32) * score_scale
    )
    grad_keys = (
        jnp.einsum("rhqk,rqhd->rkhd", grad_scores, queries, preferred_element_type=F32) * score_scale
    )
    grad_values = jnp.einsum(
        "rhqk,rqhd->rkhd", probs_back_low, grad_context, preferred_element_type=F32
    )
    grad_qkv = jnp.concatenate(
        [
            grad_queries.reshape(tokens, D),
            grad_keys.reshape(tokens, D),
            grad_values.reshape(tokens, D),
        ],
        axis=1,
    ).astype(BF)
    grad_qkv_w = weight_grad(flat_in, grad_qkv).astype(BF)
    bias_sums = jnp.sum(grad_qkv.astype(F32), axis=0)
    grad_flat = (grad_h1 + back_product(grad_qkv, qkv_weight)).astype(BF)
    grad_rows = grad_flat.reshape(own_micro, row_count, length, D)
    back_own = lax.dynamic_slice_in_dim(grad_rows, seq_at * piece, piece, 2)
    back_got = swap_seq(lax.dynamic_slice_in_dim(grad_rows, (1 - seq_at) * piece, piece, 2))
    input_local = jnp.where(
        seq_at == 0, jnp.concatenate([back_own, back_got]), jnp.concatenate([back_got, back_own])
    )
    small = jnp.stack(
        [
            bias_sums[:D],
            bias_sums[2 * D :],
            grad_out_b,
            grad_gain1,
            grad_shift1,
            grad_down_b,
            grad_gain2,
            grad_shift2,
        ]
        + [grad_up_b[i * D : (i + 1) * D] for i in range(FF // D)],
        axis=1,
    )
    small = jnp.pad(small, ((0, 0), (0, 128 - small.shape[1]))).astype(BF)
    tail = links.scatter_sum(jnp.concatenate([grad_out_w, grad_qkv_w, small], axis=1))
    down_all = links.gather(grad_down_w).astype(F32)
    up_all = links.gather(grad_up_w).astype(F32)
    tail_all = links.gather(tail).astype(F32)
    small_all = tail_all[:, 4 * D :]
    return (
        pooled_local,
        input_local,
        tail_all[:, D : 4 * D],
        small_all[:, 0],
        small_all[:, 1],
        tail_all[:, :D],
        small_all[:, 2],
        small_all[:, 3],
        small_all[:, 4],
        up_all,
        small_all[:, 8 : 8 + FF // D].T.reshape(FF),
        down_all,
        small_all[:, 5],
        small_all[:, 6],
        small_all[:, 7],
    )


def solution(mesh):
    rep = P()
    in_specs = (
        P(None, "dp", "seq", None),
        P(None, "dp", "seq"),
        P(None, "dp", None),
        P(None, "dp", None, None),
    ) + (rep,) * 13
    out_specs = (P(None, "dp", None, None), P(None, "dp", "seq", None)) + (rep,) * 13
    return jax.shard_map(local, mesh=mesh, in_specs=in_specs, out_specs=out_specs, check_vma=False)
```

time: 1250 us -> 540 us (0.43)
  blocking collectives: 579 us -> 0 us
  matrix products: 282 us -> 163 us
  local copies, waits for them, and re-layouts: 143 us -> 81.7 us
  other arithmetic: 55.6 us -> 97.9 us
  starting transfers between devices: 1.16 us -> 38.5 us
  between operations: 17.5 us -> 1.75 us
  waiting for transfers between devices: 167 us -> 153 us
    unnamed x2 -> x0, blocking collectives: 496 us -> none
    all_gather x4 -> x0, waiting for transfers between devices: 167 us -> none  [local(): lax.all_gather(for_sending(totals), ('dp', 'seq'), axis=0, tiled=True)]
    ppermute x0 -> x33, waiting for transfers between devices: none -> 153 us  [the longest x15 78.8 us: scatter_sum(): recv = lax.ppermute(send, ('dp', 'seq'), pairs)]
    dot_general x72 -> x18, matrix products: 256 us -> 141 us  [the longest x4 31.1 us: back_product(): jnp.einsum('nf,df->nd', grad_low, weight_mat, preferred_element_type=F32)]
    all_gather x8 -> x0, blocking collectives: 83.5 us -> none  [the longest x4 43.1 us: local(): lax.all_gather(keys_own, 'seq', axis=1, tiled=True)]
    ppermute x0 -> x33, starting transfers between devices: none -> 38.5 us  [the longest x15 18.2 us: scatter_sum(): recv = lax.ppermute(send, ('dp', 'seq'), pairs)]
    unnamed x526 -> x91, local copies, waits for them, and re-layouts: 41.8 us -> 10.9 us
    add x4 -> x0, local copies, waits for them, and re-layouts: 30.1 us -> none  [local(): a + b]
  transfers between devices with their start and end apart: 13 -> 33, of which waited for: 3 -> 18; matrix products, arithmetic and copies ran while one was open for 22% -> 16% of each run, Pallas kernels for 0% -> 0%
where the time goes in v1:
time: 540 us; the launch traced here: 536 us
  matrix products  163 us (30%)
  waiting for transfers between devices  153 us (28%)
  other arithmetic  97.9 us (18%)
  local copies, waits for them, and re-layouts  81.7 us (15%)
  starting transfers between devices  38.5 us (7%)
    ppermute x15, waiting for transfers between devices, scatter_sum(): recv = lax.ppermute(send, ('dp', 'seq'), pairs)  78.8 us
    ppermute x15, waiting for transfers between devices, gather(): recv = lax.ppermute(cur, ('dp', 'seq'), pairs)  44.3 us
    dot_general x4, matrix products, back_product(): jnp.einsum('nf,df->nd', grad_low, weight_mat, preferred_element_type=F32)  31.1 us
    ppermute x3, waiting for transfers between devices, swap_seq(): return lax.ppermute(value, 'seq', [(0, 1), (1, 0)])  29.7 us
    dot_general x4, matrix products, weight_grad(): jnp.einsum('nd,nf->df', left_arg, right_arg, preferred_element_type=F32)  29.1 us
    convert_element_type x1, other arithmetic, local(): grad_scores = (probs_back * (grad_probs - jnp.sum(probs_back * grad_probs...  21.6 us
    select_n x12, other arithmetic, gather(): jnp.where(at == 0, jnp.concatenate([cur, recv]), jnp.concatenate([recv, c...  20.5 us
    ppermute x15, starting transfers between devices, scatter_sum(): recv = lax.ppermute(send, ('dp', 'seq'), pairs)  18.2 us
  transfers between devices with their start and end apart: 33, of which 18 were waited for; matrix products, arithmetic and copies ran while one was open for 16% of the time, Pallas kernels for 0%

profile of v1, /device:TPU:0, one launch (start us, length us, event | category | flops | bytes accessed | tf_op | source)
XLA Modules:
  0.0 535.9 jit_solution(5607585350910956672)
XLA Ops:
  0.7 2.8 constant_dynamic-slice_fusion.6
  3.5 3.0 collective-permute-start
  8.2 4.3 fusion.60
  14.9 9.4 %collective-permute-done = bf16[2,1,256,768]{3,2,1,0:T(8,128)(2,1)} collective-permute-done((bf16[2,1,256,768]{3,2,1,0:T(8,128)(2,1)}, bf16[2,1,256,768]{3,2,1,0:T(8,128)(2,1)}, u32[]{:S(2)}, u32[]{:S(2)}) %collective-permute-start) | collective-permute-done | bytes 786464 | tf_op jit(solution)/shard_map/ppermute | solution.py:92
  27.7 4.2 add_convert_fusion
  36.8 3.9 reshape.303
  43.3 3.8 reshape.305
  49.7 3.9 reshape.304
  53.5 12.4 %fusion.13 = (f32[2,12,512]{2,1,0:T(8,128)S(1)}, f32[2,12,512,512]{2,3,1,0:T(8,128)}) fusion(pred[2,512,512]{1,2,0:T(8,128)(4,1)} %broadcast_compare_fusion, bf16[2,512,12,64]{1,0,3,2:T(2,128)(2,1)} %reshape.305, bf16[2,512,12,64]{1,0,3,2:T(2,128)(2,1)} %reshape.304), kind=kOutput, calls=%fused_computation.23 | convolution fusion | flops 824168448 | bytes 28884992 | tf_op jit(solution)/shard_map/rqhd,rkhd->rhqk/dot_general | solution.py:153
  65.9 11.1 %fusion = f32[2,12,512]{2,1,0:T(8,128)S(1)} fusion(f32[2,12,512]{2,1,0:T(8,128)S(1)} %get-tuple-element.109, f32[2,12,512,512]{2,3,1,0:T(8,128)} %get-tuple-element.110, pred[2,512,512]{1,2,0:T(8,128)(4,1)S(1)} %copy-done.5), kind=kLoop, calls=%fused_computation.6 | loop fusion | flops 25153536 | bytes 25788416 | tf_op jit(solution)/shard_map/reduce_sum | solution.py:158
  77.7 12.0 %fusion.29 = bf16[2,512,12,64]{1,3,2,0:T(8,128)(2,1)S(1)} fusion(f32[2,12,512]{2,1,0:T(8,128)S(1)} %fusion, f32[2,12,512]{2,1,0:T(8,128)S(1)} %get-tuple-element.109, f32[2,12,512,512]{2,3,1,0:T(8,128)} %get-tuple-element.110, pred[2,512,512]{1,2,0:T(8,128)(4,1)S(1)} %copy-done.5, bf16[2,512,12,64]{1,0,3,2:T(2,128)(2,1)S(1)} %copy-done.8), kind=kOutput, calls=%fused_computation.78 | convolution fusion | flops 837550080 | bytes 28934144 | tf_op jit(solution)/shard_map/rhqk,rkhd->rqhd/dot_general | solution.py:162
  94.4 11.1 %multiply_convert_fusion.1 = (bf16[1024,3072]{1,0:T(8,128)(2,1)}, f32[1024,3072]{1,0:T(8,128)}) fusion(f32[3072]{0:T(1024)S(1)} %copy-done.30, bf16[768,3072]{1,0:T(8,128)(2,1)S(1)} %bitcast.114, f32[1024,768]{1,0:T(8,128)S(1)} %get-tuple-element.112, f32[768]{0:T(1024)S(1)} %copy-done.33, f32[768]{0:T(1024)S(1)} %copy-done.25, ...), kind=kOutput, calls=%fused_computation.17 | convolution fusion | flops 4854644736 | bytes 26765312 | tf_op jit(solution)/shard_map/dot_general | solution.py:171
  105.5 7.6 %fusion.65 = (f32[1024]{0:T(1024)S(1)}, f32[1024,768]{1,0:T(8,128)S(1)}) fusion(f32[768]{0:T(1024)S(1)} %copy-done.32, bf16[1024,3072]{1,0:T(8,128)(2,1)} %get-tuple-element.113, bf16[3072,768]{1,0:T(8,128)(2,1)S(1)} %bitcast.112, f32[768]{0:T(1024)S(1)} %copy-done.33, f32[768]{0:T(1024)S(1)} %copy-done.25, f32[1024]{0:T(1024)S(1)} %add_rsqrt_fusion.1, ...), kind=kOutput, calls=%fused_computation.179 | convolution fusion | flops 4837342208 | bytes 17323008 | tf_op jit(solution)/shard_map/dot_general | solution.py:174
  115.0 3.5 fusion.18
  120.5 9.9 %convolution_convert_fusion = bf16[3072,768]{1,0:T(8,128)(2,1)} fusion(bf16[1024,3072]{1,0:T(8,128)(2,1)} %get-tuple-element.113, f32[1024,768]{1,0:T(8,128)S(1)} %get-tuple-element.92), kind=kOutput, calls=%fused_computation.24 | convolution fusion | flops 4834983936 | bytes 14155776 | tf_op jit(solution)/shard_map/nd,nf->df/dot_general | solution.py:37
  130.4 13.5 %fusion.66 = (bf16[3072]{0:T(1024)(128)(2,1)S(1)}, bf16[1024,3072]{1,0:T(8,128)(2,1)}) fusion(f32[1024,3072]{1,0:T(8,128)} %get-tuple-element.114, f32[3072]{0:T(1024)S(1)} %copy-done.30, bf16[3072,768]{1,0:T(8,128)(2,1)S(1)} %bitcast.112, f32[1024,768]{1,0:T(8,128)S(1)} %get-tuple-element.92), kind=kOutput, calls=%fused_computation.180 | convolution fusion | flops 4870370304 | bytes 26757120 | tf_op jit(solution)/shard_map/nf,df->nd/dot_general | solution.py:41
  143.9 8.8 %multiply_reduce_fusion.1 = (bf16[768]{0:T(1024)(128)(2,1)}, f32[1024]{0:T(1024)S(1)}, f32[1024]{0:T(1024)S(1)}, bf16[768]{0:T(1024)(128)(2,1)}, f32[1024,768]{1,0:T(8,128)S(1)}) fusion(f32[1024,768]{1,0:T(8,128)S(1)} %get-tuple-element.112, f32[1024]{0:T(1024)S(1)} %add_rsqrt_fusion.1, f32[1024]{0:T(1024)S(1)} %broadcast_multiply_fusion.4, ...), kind=kOutput, calls=%fused_computation.40 | convolution fusion | flops 4839698432 | bytes 20469760 | tf_op jit(solution)/shard_map/nf,df->nd/dot_general | solution.py:41
  152.6 9.9 %convolution_convert_fusion.1 = bf16[768,3072]{1,0:T(8,128)(2,1)} fusion(bf16[1024,3072]{1,0:T(8,128)(2,1)} %get-tuple-element.122, f32[1024,768]{1,0:T(8,128)S(1)} %get-tuple-element.112, f32[768]{0:T(1024)S(1)} %copy-done.33, f32[768]{0:T(1024)S(1)} %copy-done.25, f32[1024]{0:T(1024)S(1)} %add_rsqrt_fusion.1, f32[1024]{0:T(1024)S(1)} %broadcast_multiply_fusion.4), kind=kOutput, calls=%fused_computation.25 | convolution fusion | flops 4838129664 | bytes 14170112 | tf_op jit(solution)/shard_map/nd,nf->df/dot_general | solution.py:37
  166.8 2.6 convolution_convert_fusion.3
  172.0 3.8 reshape.309
  175.8 12.8 %fusion.24 = bf16[2,512,12,64]{1,3,2,0:T(8,128)(2,1)} fusion(f32[2,12,512]{2,1,0:T(8,128)} %log_add_fusion, f32[2,12,512,512]{2,3,1,0:T(8,128)} %get-tuple-element.110, pred[2,512,512]{1,2,0:T(8,128)(4,1)} %broadcast_compare_fusion, bf16[2,512,12,64]{1,0,3,2:T(2,128)(2,1)} %reshape.309), kind=kOutput, calls=%fused_computation.75 | convolution fusion | flops 831258624 | bytes 28884992 | tf_op jit(solution)/shard_map/rhqk,rqhd->rkhd/dot_general | solution.py:225
  188.7 18.2 %multiply_reduce_fusion = (f32[2,12,512]{2,1,0:T(8,128)}, f32[2,12,512,512]{2,3,1,0:T(8,128)}) fusion(f32[2,12,512]{2,1,0:T(8,128)} %log_add_fusion, f32[2,12,512,512]{2,3,1,0:T(8,128)} %get-tuple-element.110, pred[2,512,512]{1,2,0:T(8,128)(4,1)} %broadcast_compare_fusion, bf16[2,512,12,64]{1,0,3,2:T(2,128)(2,1)} %reshape.303, ...), kind=kOutput, calls=%fused_computation.1 | convolution fusion | flops 836751360 | bytes 54099968 | tf_op jit(solution)/shard_map/rqhd,rkhd->rhqk/dot_general | solution.py:215
  206.8 21.6 %multiply_convert_fusion = bf16[2,12,512,512]{2,3,1,0:T(8,128)(2,1)} fusion(f32[2,12,512,512]{2,3,1,0:T(8,128)} %get-tuple-element.120, f32[2,12,512]{2,1,0:T(8,128)} %get-tuple-element.119, f32[2,12,512]{2,1,0:T(8,128)} %log_add_fusion, f32[2,12,512,512]{2,3,1,0:T(8,128)} %get-tuple-element.110, pred[2,512,512]{1,2,0:T(8,128)(4,1)} %broadcast_compare_fusion), kind=kLoop, calls=%fused_computation | loop fusion | flops 37748736 | bytes 63537152 | tf_op jit(solution)/shard_map/convert_element_type | solution.py:218
  228.4 9.7 %fusion.28 = bf16[2,512,12,64]{1,3,2,0:T(8,128)(2,1)} fusion(bf16[2,12,512,512]{2,3,1,0:T(8,128)(2,1)} %multiply_convert_fusion, bf16[2,512,12,64]{1,0,3,2:T(2,128)(2,1)S(1)} %copy-done.4), kind=kOutput, calls=%fused_computation.77 | convolution fusion | flops 806879232 | bytes 15728640 | tf_op jit(solution)/shard_map/rhqk,rqhd->rkhd/dot_general | solution.py:223
  238.2 7.9 %fusion.27 = bf16[2,512,12,64]{1,3,2,0:T(8,128)(2,1)} fusion(bf16[2,12,512,512]{2,3,1,0:T(8,128)(2,1)} %multiply_convert_fusion, bf16[2,512,12,64]{1,0,3,2:T(2,128)(2,1)S(1)} %copy-done.2), kind=kOutput, calls=%fused_computation.76 | convolution fusion | flops 806879232 | bytes 15728640 | tf_op jit(solution)/shard_map/rhqk,rkhd->rqhd/dot_general | solution.py:220
  250.2 2.6 copy.134
  253.9 3.2 copy.130
  257.5 3.2 constant_dynamic-slice_fusion.1
  270.7 3.0 reduce.2
  273.8 2.7 stack.64
  278.1 6.8 %convolution_convert_fusion.2 = bf16[768,2304]{1,0:T(8,128)(2,1)S(1)} fusion(bf16[1024,768]{1,0:T(8,128)(2,1)} %bitcast.105, bf16[1024,2304]{0,1:T(8,128)(2,1)} %constant_dynamic-update-slice_fusion), kind=kOutput, calls=%fused_computation.26 | convolution fusion | flops 3625648128 | bytes 9830400 | tf_op jit(solution)/shard_map/nd,nf->df/dot_general | solution.py:37
  289.6 3.2 convert_add_fusion.2
  294.8 2.9 convert_add_fusion.1
  302.5 6.8 %collective-permute-done.14 = bf16[192,3072]{1,0:T(8,128)(2,1)S(1)} collective-permute-done((bf16[192,3072]{1,0:T(8,128)(2,1)S(1)}, bf16[192,3072]{1,0:T(8,128)(2,1)S(1)}, u32[]{:S(2)}, u32[]{:S(2)}) %collective-permute-start.14) | collective-permute-done | bytes 1179680 | tf_op jit(solution)/shard_map/ppermute | solution.py:79
  311.5 16.8 %collective-permute-done.24 = bf16[768,768]{1,0:T(8,128)(2,1)S(1)} collective-permute-done((bf16[768,768]{1,0:T(8,128)(2,1)S(1)}, bf16[768,768]{1,0:T(8,128)(2,1)S(1)}, u32[]{:S(2)}, u32[]{:S(2)}) %collective-permute-start.24) | collective-permute-done | bytes 1179680 | tf_op jit(solution)/shard_map/ppermute | solution.py:79
  330.4 17.4 %collective-permute-done.4 = bf16[192,3200]{1,0:T(8,128)(2,1)S(1)} collective-permute-done((bf16[192,3200]{1,0:T(8,128)(2,1)S(1)}, bf16[192,3200]{1,0:T(8,128)(2,1)S(1)}, u32[]{:S(2)}, u32[]{:S(2)}) %collective-permute-start.4) | collective-permute-done | bytes 1228832 | tf_op jit(solution)/shard_map/ppermute | solution.py:79
  352.4 5.9 %collective-permute-done.5 = bf16[96,3200]{1,0:T(8,128)(2,1)S(1)} collective-permute-done((bf16[96,3200]{1,0:T(8,128)(2,1)S(1)}, bf16[96,3200]{1,0:T(8,128)(2,1)S(1)}, u32[]{:S(2)}, u32[]{:S(2)}) %collective-permute-start.5) | collective-permute-done | bytes 614432 | tf_op jit(solution)/shard_map/ppermute | solution.py:79
  360.5 2.7 collective-permute-start.17
  363.1 8.0 %collective-permute-done.26 = bf16[192,768]{1,0:T(8,128)(2,1)S(1)} collective-permute-done((bf16[192,768]{1,0:T(8,128)(2,1)S(1)}, bf16[192,768]{1,0:T(8,128)(2,1)S(1)}, u32[]{:S(2)}, u32[]{:S(2)}) %collective-permute-start.26) | collective-permute-done | bytes 294944 | tf_op jit(solution)/shard_map/ppermute | solution.py:79
  375.2 3.5 collective-permute-start.18
  378.9 11.9 %collective-permute-done.27 = bf16[96,768]{1,0:T(8,128)(2,1)S(1)} collective-permute-done((bf16[96,768]{1,0:T(8,128)(2,1)S(1)}, bf16[96,768]{1,0:T(8,128)(2,1)S(1)}, u32[]{:S(2)}, u32[]{:S(2)}) %collective-permute-start.27) | collective-permute-done | bytes 147488 | tf_op jit(solution)/shard_map/ppermute | solution.py:79
  391.0 9.7 %collective-permute-done.7 = bf16[24,3200]{1,0:T(8,128)(2,1)S(1)} collective-permute-done((bf16[24,3200]{1,0:T(8,128)(2,1)S(1)}, bf16[24,3200]{1,0:T(8,128)(2,1)S(1)}, u32[]{:S(2)}, u32[]{:S(2)}) %collective-permute-start.7) | collective-permute-done | bytes 153632 | tf_op jit(solution)/shard_map/ppermute | solution.py:79
  401.1 4.3 collective-permute-done.28
  407.6 5.4 %collective-permute-done.19 = bf16[48,3072]{1,0:T(8,128)(2,1)S(1)} collective-permute-done((bf16[48,3072]{1,0:T(8,128)(2,1)S(1)}, bf16[48,3072]{1,0:T(8,128)(2,1)S(1)}, u32[]{:S(2)}, u32[]{:S(2)}) %collective-permute-start.19) | collective-permute-done | bytes 294944 | tf_op jit(solution)/shard_map/ppermute | solution.py:86
  414.2 5.2 collective-permute-done.29
  420.6 4.1 collective-permute-done.9
  425.6 3.0 maximum_select_fusion.9
  430.7 2.9 maximum_select_fusion.10
  433.6 10.3 %collective-permute-done.10 = bf16[96,3200]{1,0:T(8,128)(2,1)} collective-permute-done((bf16[96,3200]{1,0:T(8,128)(2,1)}, bf16[96,3200]{1,0:T(8,128)(2,1)}, u32[]{:S(2)}, u32[]{:S(2)}) %collective-permute-start.10) | collective-permute-done | bytes 614432 | tf_op jit(solution)/shard_map/ppermute | solution.py:86
  443.9 2.9 maximum_select_fusion.8
  446.8 2.7 maximum_select_fusion.4
  449.5 3.2 collective-permute-start.22
  452.7 6.5 %collective-permute-done.31 = bf16[768,768]{1,0:T(8,128)(2,1)} collective-permute-done((bf16[768,768]{1,0:T(8,128)(2,1)}, bf16[768,768]{1,0:T(8,128)(2,1)}, u32[]{:S(2)}, u32[]{:S(2)}) %collective-permute-start.31) | collective-permute-done | bytes 1179680 | tf_op jit(solution)/shard_map/ppermute | solution.py:86
  459.2 2.8 maximum_select_fusion.5
  462.1 3.4 collective-permute-start.32
  465.5 6.9 %collective-permute-done.11 = bf16[192,3200]{1,0:T(8,128)(2,1)} collective-permute-done((bf16[192,3200]{1,0:T(8,128)(2,1)}, bf16[192,3200]{1,0:T(8,128)(2,1)}, u32[]{:S(2)}, u32[]{:S(2)}) %collective-permute-start.11) | collective-permute-done | bytes 1228832 | tf_op jit(solution)/shard_map/ppermute | solution.py:86
  472.4 3.1 maximum_select_fusion.3
  475.5 3.1 collective-permute-start.12
  478.6 6.3 %add_convert_fusion.1 = bf16[1024,768]{1,0:T(8,128)(2,1)S(1)} fusion(f32[1024,768]{1,0:T(8,128)S(1)} %copy-done.12, bf16[1024,2304]{0,1:T(8,128)(2,1)} %constant_dynamic-update-slice_fusion, bf16[768,2304]{1,0:T(8,128)(2,1)S(1)} %copy-done), kind=kOutput, calls=%fused_computation.41 | convolution fusion | flops 3625451520 | bytes 12976128 | tf_op jit(solution)/shard_map/nf,df->nd/dot_general | solution.py:41
  488.4 20.3 %collective-permute-done.1 = f32[2,1,32,768]{3,2,0,1:T(8,128)S(1)} collective-permute-done((f32[2,1,32,768]{3,2,0,1:T(8,128)S(1)}, f32[2,1,32,768]{3,2,0,1:T(8,128)S(1)}, u32[]{:S(2)}, u32[]{:S(2)}) %collective-permute-start.1) | collective-permute-done | bytes 196640 | tf_op jit(solution)/shard_map/ppermute | solution.py:92
  510.9 4.3 fusion.17
  515.3 4.8 fusion.16
  520.1 5.6 %fusion.15 = f32[768,3200]{1,0:T(8,128)S(1)} fusion(bf16[384,3200]{1,0:T(8,128)(2,1)S(1)} %collective-permute-done.12, bf16[384,3200]{1,0:T(8,128)(2,1)S(1)} %maximum_select_fusion.3, pred[]{:T(512)S(6)} %eq.76), kind=kLoop, calls=%fused_computation.29 | loop fusion | flops 24576000 | bytes 14745601 | tf_op jit(solution)/shard_map/convert_element_type | solution.py:263
  530.4 3.5 slice.109
  (230 shorter events, 97.6 us)
Async XLA Ops:
  0.6 27.1 %copy-start = (bf16[768,2304]{1,0:T(8,128)(2,1)S(1)}, bf16[768,2304]{1,0:T(8,128)(2,1)}, u32[]{:S(2)}) copy-start(bf16[768,2304]{1,0:T(8,128)(2,1)} %param.20) | copy-start | bytes 10616836
  0.7 5.8 %copy-start.28 = (s32[4,1,32]{2,1,0:T(1,128)S(1)}, s32[4,1,32]{2,1,0:T(1,128)}, u32[]{:S(2)}) copy-start(s32[4,1,32]{2,1,0:T(1,128)} %param.18) | copy-start | bytes 1540
  0.7 7.5 %copy-start.18 = (f32[768]{0:T(1024)S(1)}, f32[768]{0:T(1024)}, u32[]{:S(2)}) copy-start(f32[768]{0:T(1024)} %param.31) | copy-start | bytes 9220
  3.5 20.8 %collective-permute-start = (bf16[2,1,256,768]{3,2,1,0:T(8,128)(2,1)}, bf16[2,1,256,768]{3,2,1,0:T(8,128)(2,1)}, u32[]{:S(2)}, u32[]{:S(2)}) collective-permute-start(bf16[2,1,256,768]{3,2,1,0:T(8,128)(2,1)} %get-tuple-element.102), channel_id=1, source_target_pairs={{0,1},{1,0},{2,3},{3,2},{4,5},{5,4},{6,7},{7,6},{8,9},{9,8},{10,11... | collective-permute-start | bytes 2359304 | tf_op jit(solution)/shard_map/ppermute | solution.py:92
  6.5 6.5 %copy-start.20 = (f32[2,32]{1,0:T(2,128)}, f32[2,32]{1,0:T(2,128)S(1)}, u32[]{:S(2)}) copy-start(f32[2,32]{1,0:T(2,128)S(1)} %convert_element_type.201) | copy-start | bytes 772
  8.1 18.4 %copy-start.16 = (s32[2,512]{1,0:T(2,128)}, s32[2,512]{1,0:T(2,128)S(1)}, u32[]{:S(2)}) copy-start(s32[2,512]{1,0:T(2,128)S(1)} %fusion.44) | copy-start | bytes 12292
  53.5 12.4 %copy-start.5 = (pred[2,512,512]{1,2,0:T(8,128)(4,1)S(1)}, pred[2,512,512]{1,2,0:T(8,128)(4,1)}, u32[]{:S(2)}) copy-start(pred[2,512,512]{1,2,0:T(8,128)(4,1)} %broadcast_compare_fusion) | copy-start | bytes 1572868
  65.9 11.8 %copy-start.8 = (bf16[2,512,12,64]{1,0,3,2:T(2,128)(2,1)S(1)}, bf16[2,512,12,64]{1,0,3,2:T(2,128)(2,1)}, u32[]{:S(2)}) copy-start(bf16[2,512,12,64]{1,0,3,2:T(2,128)(2,1)} %reshape.303) | copy-start | bytes 4718596
  89.7 2.1 copy-start.14
  89.7 2.1 copy-start.29
  91.8 2.3 slice-start.6
  91.8 2.3 slice-start.7
  93.6 11.9 %slice-start.4 = ((s8[4718592]{0:T(1024)(128)(4,1)}), s8[4194304]{0:T(1024)(128)(4,1)S(1)}, s32[]{:S(2)}) async-start(s8[4718592]{0:T(1024)(128)(4,1)} %bitcast.111), calls=%async_computation.4 | async-start | bytes 8388608
  94.4 11.1 %slice-start.5 = ((s8[4718592]{0:T(1024)(128)(4,1)}), s8[524288]{0:T(1024)(128)(4,1)S(1)}, s32[]{:S(2)}) async-start(s8[4718592]{0:T(1024)(128)(4,1)} %bitcast.111), calls=%async_computation.5 | async-start | bytes 1048576
  94.4 11.1 %copy-start.32 = (f32[768]{0:T(1024)S(1)}, f32[768]{0:T(1024)}, u32[]{:S(2)}) copy-start(f32[768]{0:T(1024)} %param.30) | copy-start | bytes 9220
  164.3 2.5 copy-start.11
  206.8 21.6 %copy-start.4 = (bf16[2,512,12,64]{1,0,3,2:T(2,128)(2,1)S(1)}, bf16[2,512,12,64]{1,0,3,2:T(2,128)(2,1)}, u32[]{:S(2)}) copy-start(bf16[2,512,12,64]{1,0,3,2:T(2,128)(2,1)} %reshape.304) | copy-start | bytes 4718596
  228.4 9.7 %copy-start.2 = (bf16[2,512,12,64]{1,0,3,2:T(2,128)(2,1)S(1)}, bf16[2,512,12,64]{1,0,3,2:T(2,128)(2,1)}, u32[]{:S(2)}) copy-start(bf16[2,512,12,64]{1,0,3,2:T(2,128)(2,1)} %reshape.305) | copy-start | bytes 4718596
  238.1 7.9 %copy-start.22 = (bf16[768]{0:T(1024)(128)(2,1)S(1)}, bf16[768]{0:T(1024)(128)(2,1)}, u32[]{:S(2)}) copy-start(bf16[768]{0:T(1024)(128)(2,1)} %get-tuple-element.83) | copy-start | bytes 4612
  238.1 7.9 %copy-start.23 = (bf16[768]{0:T(1024)(128)(2,1)S(1)}, bf16[768]{0:T(1024)(128)(2,1)}, u32[]{:S(2)}) copy-start(bf16[768]{0:T(1024)(128)(2,1)} %get-tuple-element.91) | copy-start | bytes 4612
  238.1 10.8 %copy-start.27 = (bf16[768]{0:T(1024)(128)(2,1)S(1)}, bf16[768]{0:T(1024)(128)(2,1)}, u32[]{:S(2)}) copy-start(bf16[768]{0:T(1024)(128)(2,1)} %get-tuple-element.85) | copy-start | bytes 4612
  238.2 11.4 %copy-start.26 = (bf16[768]{0:T(1024)(128)(2,1)S(1)}, bf16[768]{0:T(1024)(128)(2,1)}, u32[]{:S(2)}) copy-start(bf16[768]{0:T(1024)(128)(2,1)} %get-tuple-element.90) | copy-start | bytes 4612
  253.9 6.8 %slice-start.2 = ((s8[4718592]{0:T(1024)(128)(4,1)}), s8[4194304]{0:T(1024)(128)(4,1)S(1)}, s32[]{:S(2)}) async-start(s8[4718592]{0:T(1024)(128)(4,1)} %bitcast.99), calls=%async_computation.2 | async-start | bytes 8388608
  257.1 3.7 slice-start.3
  260.8 28.9 %collective-permute-start.13 = (bf16[384,3072]{1,0:T(8,128)(2,1)}, bf16[384,3072]{1,0:T(8,128)(2,1)}, u32[]{:S(2)}, u32[]{:S(2)}) collective-permute-start(bf16[384,3072]{1,0:T(8,128)(2,1)} %constant_dynamic-slice_fusion.1), channel_id=1, source_target_pairs={{0,2},{1,3},{2,0},{3,1},{4,6},{5,7},{6,4},{7,5},{8,10},{9,11},{10,... | collective-permute-start | bytes 7077896 | tf_op jit(solution)/shard_map/ppermute | solution.py:79
  262.4 2.5 copy-start.9
  262.4 32.5 %collective-permute-start.23 = (bf16[1536,768]{1,0:T(8,128)(2,1)}, bf16[1536,768]{1,0:T(8,128)(2,1)}, u32[]{:S(2)}, u32[]{:S(2)}) collective-permute-start(bf16[1536,768]{1,0:T(8,128)(2,1)} %constant_dynamic-slice_fusion), channel_id=1, source_target_pairs={{0,2},{1,3},{2,0},{3,1},{4,6},{5,7},{6,4},{7,5},{8,10},{9,11},{10,... | collective-permute-start | bytes 7077896 | tf_op jit(solution)/shard_map/ppermute | solution.py:79
  270.7 3.1 copy-start.19
  278.1 6.8 %copy-start.10 = (bf16[768,768]{1,0:T(8,128)(2,1)S(1)}, bf16[768,768]{1,0:T(8,128)(2,1)}, u32[]{:S(2)}) copy-start(bf16[768,768]{1,0:T(8,128)(2,1)} %copy.134) | copy-start | bytes 3538948
  278.1 6.8 %copy-start.15 = (bf16[768,12]{1,0:T(8,128)(2,1)S(1)}, bf16[768,12]{1,0:T(8,128)(2,1)}, u32[]{:S(2)}) copy-start(bf16[768,12]{1,0:T(8,128)(2,1)} %copy.133) | copy-start | bytes 55300
  285.7 2.3 copy-start.3
  289.6 8.9 %collective-permute-start.3 = (bf16[384,3200]{1,0:T(8,128)(2,1)}, bf16[384,3200]{1,0:T(8,128)(2,1)}, u32[]{:S(2)}, u32[]{:S(2)}) collective-permute-start(bf16[384,3200]{1,0:T(8,128)(2,1)} %constant_dynamic-slice_fusion.2), channel_id=1, source_target_pairs={{0,2},{1,3},{2,0},{3,1},{4,6},{5,7},{6,4},{7,5},{8,10},{9,11},{10,... | collective-permute-start | bytes 7372808 | tf_op jit(solution)/shard_map/ppermute | solution.py:79
  292.9 5.7 %slice-start = ((s8[4915200]{0:T(1024)(128)(4,1)}), s8[4194304]{0:T(1024)(128)(4,1)S(1)}, s32[]{:S(2)}) async-start(s8[4915200]{0:T(1024)(128)(4,1)} %bitcast.89), calls=%async_computation | async-start | bytes 8388608
  293.0 5.5 %slice-start.1 = ((s8[4915200]{0:T(1024)(128)(4,1)}), s8[720896]{0:T(1024)(128)(4,1)S(1)}, s32[]{:S(2)}) async-start(s8[4915200]{0:T(1024)(128)(4,1)} %bitcast.89), calls=%async_computation.1 | async-start | bytes 1441792
  293.1 16.3 %collective-permute-start.14 = (bf16[192,3072]{1,0:T(8,128)(2,1)S(1)}, bf16[192,3072]{1,0:T(8,128)(2,1)S(1)}, u32[]{:S(2)}, u32[]{:S(2)}) collective-permute-start(bf16[192,3072]{1,0:T(8,128)(2,1)S(1)} %dynamic-slice_convert_fusion.2), channel_id=1, source_target_pairs={{0,4},{1,5},{2,3},{3,2},{4,0},{5,1},{6,7},{7,6},{8,12},{9,13},{10,... | collective-permute-start | bytes 3538952 | tf_op jit(solution)/shard_map/ppermute | solution.py:79
  297.9 30.4 %collective-permute-start.24 = (bf16[768,768]{1,0:T(8,128)(2,1)S(1)}, bf16[768,768]{1,0:T(8,128)(2,1)S(1)}, u32[]{:S(2)}, u32[]{:S(2)}) collective-permute-start(bf16[768,768]{1,0:T(8,128)(2,1)S(1)} %dynamic-slice_convert_fusion.1), channel_id=1, source_target_pairs={{0,4},{1,5},{2,3},{3,2},{4,0},{5,1},{6,7},{7,6},{8,12},{9,13},{10,... | collective-permute-start | bytes 3538952 | tf_op jit(solution)/shard_map/ppermute | solution.py:79
  301.0 46.7 %collective-permute-start.4 = (bf16[192,3200]{1,0:T(8,128)(2,1)S(1)}, bf16[192,3200]{1,0:T(8,128)(2,1)S(1)}, u32[]{:S(2)}, u32[]{:S(2)}) collective-permute-start(bf16[192,3200]{1,0:T(8,128)(2,1)S(1)} %dynamic-slice_convert_fusion), channel_id=1, source_target_pairs={{0,4},{1,5},{2,3},{3,2},{4,0},{5,1},{6,7},{7,6},{8,12},{9,13},{10,... | collective-permute-start | bytes 3686408 | tf_op jit(solution)/shard_map/ppermute | solution.py:79
  309.7 40.3 %collective-permute-start.15 = (bf16[96,3072]{1,0:T(8,128)(2,1)S(1)}, bf16[96,3072]{1,0:T(8,128)(2,1)S(1)}, u32[]{:S(2)}, u32[]{:S(2)}) collective-permute-start(bf16[96,3072]{1,0:T(8,128)(2,1)S(1)} %dynamic-slice_convert_fusion.5), channel_id=1, source_target_pairs={{0,1},{1,0},{2,6},{3,7},{4,5},{5,4},{6,2},{7,3},{8,9},{9,8},{10,14... | collective-permute-start | bytes 1769480 | tf_op jit(solution)/shard_map/ppermute | solution.py:79
  328.6 23.2 %collective-permute-start.25 = (bf16[384,768]{1,0:T(8,128)(2,1)S(1)}, bf16[384,768]{1,0:T(8,128)(2,1)S(1)}, u32[]{:S(2)}, u32[]{:S(2)}) collective-permute-start(bf16[384,768]{1,0:T(8,128)(2,1)S(1)} %dynamic-slice_convert_fusion.4), channel_id=1, source_target_pairs={{0,1},{1,0},{2,6},{3,7},{4,5},{5,4},{6,2},{7,3},{8,9},{9,8},{10,14... | collective-permute-start | bytes 1769480 | tf_op jit(solution)/shard_map/ppermute | solution.py:79
  348.1 10.2 %collective-permute-start.5 = (bf16[96,3200]{1,0:T(8,128)(2,1)S(1)}, bf16[96,3200]{1,0:T(8,128)(2,1)S(1)}, u32[]{:S(2)}, u32[]{:S(2)}) collective-permute-start(bf16[96,3200]{1,0:T(8,128)(2,1)S(1)} %dynamic-slice_convert_fusion.3), channel_id=1, source_target_pairs={{0,1},{1,0},{2,6},{3,7},{4,5},{5,4},{6,2},{7,3},{8,9},{9,8},{10,14... | collective-permute-start | bytes 1843208 | tf_op jit(solution)/shard_map/ppermute | solution.py:79
  350.1 10.3 %collective-permute-start.16 = (bf16[48,3072]{1,0:T(8,128)(2,1)S(1)}, bf16[48,3072]{1,0:T(8,128)(2,1)S(1)}, u32[]{:S(2)}, u32[]{:S(2)}) collective-permute-start(bf16[48,3072]{1,0:T(8,128)(2,1)S(1)} %dynamic-slice_convert_fusion.8), channel_id=1, source_target_pairs={{0,8},{1,9},{2,10},{3,11},{4,12},{5,13},{6,14},{7,15},{8,0},{9,1},... | collective-permute-start | bytes 884744 | tf_op jit(solution)/shard_map/ppermute | solution.py:79
  351.9 19.3 %collective-permute-start.26 = (bf16[192,768]{1,0:T(8,128)(2,1)S(1)}, bf16[192,768]{1,0:T(8,128)(2,1)S(1)}, u32[]{:S(2)}, u32[]{:S(2)}) collective-permute-start(bf16[192,768]{1,0:T(8,128)(2,1)S(1)} %dynamic-slice_convert_fusion.7), channel_id=1, source_target_pairs={{0,8},{1,9},{2,10},{3,11},{4,12},{5,13},{6,14},{7,15},{8,0},{9,1},... | collective-permute-start | bytes 884744 | tf_op jit(solution)/shard_map/ppermute | solution.py:79
  358.5 20.2 %collective-permute-start.6 = (bf16[48,3200]{1,0:T(8,128)(2,1)S(1)}, bf16[48,3200]{1,0:T(8,128)(2,1)S(1)}, u32[]{:S(2)}, u32[]{:S(2)}) collective-permute-start(bf16[48,3200]{1,0:T(8,128)(2,1)S(1)} %dynamic-slice_convert_fusion.6), channel_id=1, source_target_pairs={{0,8},{1,9},{2,10},{3,11},{4,12},{5,13},{6,14},{7,15},{8,0},{9,1},... | collective-permute-start | bytes 921608 | tf_op jit(solution)/shard_map/ppermute | solution.py:79
  360.5 14.7 %collective-permute-start.17 = (bf16[24,3072]{1,0:T(8,128)(2,1)S(1)}, bf16[24,3072]{1,0:T(8,128)(2,1)S(1)}, u32[]{:S(2)}, u32[]{:S(2)}) collective-permute-start(bf16[24,3072]{1,0:T(8,128)(2,1)S(1)} %dynamic-slice_convert_fusion.11), channel_id=1, source_target_pairs={{0,16},{1,17},{2,18},{3,19},{4,20},{5,21},{6,22},{7,23},{8,24},{9,... | collective-permute-start | bytes 442376 | tf_op jit(solution)/shard_map/ppermute | solution.py:79
  371.3 19.6 %collective-permute-start.27 = (bf16[96,768]{1,0:T(8,128)(2,1)S(1)}, bf16[96,768]{1,0:T(8,128)(2,1)S(1)}, u32[]{:S(2)}, u32[]{:S(2)}) collective-permute-start(bf16[96,768]{1,0:T(8,128)(2,1)S(1)} %dynamic-slice_convert_fusion.10), channel_id=1, source_target_pairs={{0,16},{1,17},{2,18},{3,19},{4,20},{5,21},{6,22},{7,23},{8,24},{9,... | collective-permute-start | bytes 442376 | tf_op jit(solution)/shard_map/ppermute | solution.py:79
  375.2 25.5 %collective-permute-start.18 = (bf16[24,3072]{1,0:T(8,128)(2,1)S(1)}, bf16[24,3072]{1,0:T(8,128)(2,1)S(1)}, u32[]{:S(2)}, u32[]{:S(2)}) collective-permute-start(bf16[24,3072]{1,0:T(8,128)(2,1)S(1)} %add_convert_fusion.4), channel_id=1, source_target_pairs={{0,16},{1,17},{2,18},{3,19},{4,20},{5,21},{6,22},{7,23},{8,24},{9,... | collective-permute-start | bytes 442376 | tf_op jit(solution)/shard_map/ppermute | solution.py:86
  378.8 21.8 %collective-permute-start.7 = (bf16[24,3200]{1,0:T(8,128)(2,1)S(1)}, bf16[24,3200]{1,0:T(8,128)(2,1)S(1)}, u32[]{:S(2)}, u32[]{:S(2)}) collective-permute-start(bf16[24,3200]{1,0:T(8,128)(2,1)S(1)} %dynamic-slice_convert_fusion.9), channel_id=1, source_target_pairs={{0,16},{1,17},{2,18},{3,19},{4,20},{5,21},{6,22},{7,23},{8,24},{9,... | collective-permute-start | bytes 460808 | tf_op jit(solution)/shard_map/ppermute | solution.py:79
  390.9 14.5 %collective-permute-start.28 = (bf16[96,768]{1,0:T(8,128)(2,1)S(1)}, bf16[96,768]{1,0:T(8,128)(2,1)S(1)}, u32[]{:S(2)}, u32[]{:S(2)}) collective-permute-start(bf16[96,768]{1,0:T(8,128)(2,1)S(1)} %add_convert_fusion.3), channel_id=1, source_target_pairs={{0,16},{1,17},{2,18},{3,19},{4,20},{5,21},{6,22},{7,23},{8,24},{9,... | collective-permute-start | bytes 442376 | tf_op jit(solution)/shard_map/ppermute | solution.py:86
  400.6 6.5 %collective-permute-start.8 = (bf16[24,3200]{1,0:T(8,128)(2,1)S(1)}, bf16[24,3200]{1,0:T(8,128)(2,1)S(1)}, u32[]{:S(2)}, u32[]{:S(2)}) collective-permute-start(bf16[24,3200]{1,0:T(8,128)(2,1)S(1)} %add_convert_fusion.2), channel_id=1, source_target_pairs={{0,16},{1,17},{2,18},{3,19},{4,20},{5,21},{6,22},{7,23},{8,24},{9,... | collective-permute-start | bytes 460808 | tf_op jit(solution)/shard_map/ppermute | solution.py:86
  400.8 12.2 %collective-permute-start.19 = (bf16[48,3072]{1,0:T(8,128)(2,1)S(1)}, bf16[48,3072]{1,0:T(8,128)(2,1)S(1)}, u32[]{:S(2)}, u32[]{:S(2)}) collective-permute-start(bf16[48,3072]{1,0:T(8,128)(2,1)S(1)} %maximum_select_fusion.16), channel_id=1, source_target_pairs={{0,8},{1,9},{2,10},{3,11},{4,12},{5,13},{6,14},{7,15},{8,0},{9,1},... | collective-permute-start | bytes 884744 | tf_op jit(solution)/shard_map/ppermute | solution.py:86
  405.4 13.9 %collective-permute-start.29 = (bf16[192,768]{1,0:T(8,128)(2,1)S(1)}, bf16[192,768]{1,0:T(8,128)(2,1)S(1)}, u32[]{:S(2)}, u32[]{:S(2)}) collective-permute-start(bf16[192,768]{1,0:T(8,128)(2,1)S(1)} %maximum_select_fusion.17), channel_id=1, source_target_pairs={{0,8},{1,9},{2,10},{3,11},{4,12},{5,13},{6,14},{7,15},{8,0},{9,1},... | collective-permute-start | bytes 884744 | tf_op jit(solution)/shard_map/ppermute | solution.py:86
  407.2 17.4 %collective-permute-start.9 = (bf16[48,3200]{1,0:T(8,128)(2,1)S(1)}, bf16[48,3200]{1,0:T(8,128)(2,1)S(1)}, u32[]{:S(2)}, u32[]{:S(2)}) collective-permute-start(bf16[48,3200]{1,0:T(8,128)(2,1)S(1)} %maximum_select_fusion.15), channel_id=1, source_target_pairs={{0,8},{1,9},{2,10},{3,11},{4,12},{5,13},{6,14},{7,15},{8,0},{9,1},... | collective-permute-start | bytes 921608 | tf_op jit(solution)/shard_map/ppermute | solution.py:86
  414.0 11.6 %collective-permute-start.20 = (bf16[96,3072]{1,0:T(8,128)(2,1)}, bf16[96,3072]{1,0:T(8,128)(2,1)}, u32[]{:S(2)}, u32[]{:S(2)}) collective-permute-start(bf16[96,3072]{1,0:T(8,128)(2,1)} %maximum_select_fusion.12), channel_id=1, source_target_pairs={{0,1},{1,0},{2,6},{3,7},{4,5},{5,4},{6,2},{7,3},{8,9},{9,8},{10,14... | collective-permute-start | bytes 1769480 | tf_op jit(solution)/shard_map/ppermute | solution.py:86
  420.4 10.3 %collective-permute-start.30 = (bf16[384,768]{1,0:T(8,128)(2,1)}, bf16[384,768]{1,0:T(8,128)(2,1)}, u32[]{:S(2)}, u32[]{:S(2)}) collective-permute-start(bf16[384,768]{1,0:T(8,128)(2,1)} %maximum_select_fusion.13), channel_id=1, source_target_pairs={{0,1},{1,0},{2,6},{3,7},{4,5},{5,4},{6,2},{7,3},{8,9},{9,8},{10,14... | collective-permute-start | bytes 1769480 | tf_op jit(solution)/shard_map/ppermute | solution.py:86
  425.6 18.3 %collective-permute-start.10 = (bf16[96,3200]{1,0:T(8,128)(2,1)}, bf16[96,3200]{1,0:T(8,128)(2,1)}, u32[]{:S(2)}, u32[]{:S(2)}) collective-permute-start(bf16[96,3200]{1,0:T(8,128)(2,1)} %maximum_select_fusion.11), channel_id=1, source_target_pairs={{0,1},{1,0},{2,6},{3,7},{4,5},{5,4},{6,2},{7,3},{8,9},{9,8},{10,14... | collective-permute-start | bytes 1843208 | tf_op jit(solution)/shard_map/ppermute | solution.py:86
  428.6 18.2 %collective-permute-start.21 = (bf16[192,3072]{1,0:T(8,128)(2,1)}, bf16[192,3072]{1,0:T(8,128)(2,1)}, u32[]{:S(2)}, u32[]{:S(2)}) collective-permute-start(bf16[192,3072]{1,0:T(8,128)(2,1)} %maximum_select_fusion.9), channel_id=1, source_target_pairs={{0,4},{1,5},{2,3},{3,2},{4,0},{5,1},{6,7},{7,6},{8,12},{9,13},{10,... | collective-permute-start | bytes 3538952 | tf_op jit(solution)/shard_map/ppermute | solution.py:86
  433.6 25.6 %collective-permute-start.31 = (bf16[768,768]{1,0:T(8,128)(2,1)}, bf16[768,768]{1,0:T(8,128)(2,1)}, u32[]{:S(2)}, u32[]{:S(2)}) collective-permute-start(bf16[768,768]{1,0:T(8,128)(2,1)} %maximum_select_fusion.10), channel_id=1, source_target_pairs={{0,4},{1,5},{2,3},{3,2},{4,0},{5,1},{6,7},{7,6},{8,12},{9,13},{10,... | collective-permute-start | bytes 3538952 | tf_op jit(solution)/shard_map/ppermute | solution.py:86
  446.8 25.6 %collective-permute-start.11 = (bf16[192,3200]{1,0:T(8,128)(2,1)}, bf16[192,3200]{1,0:T(8,128)(2,1)}, u32[]{:S(2)}, u32[]{:S(2)}) collective-permute-start(bf16[192,3200]{1,0:T(8,128)(2,1)} %maximum_select_fusion.8), channel_id=1, source_target_pairs={{0,4},{1,5},{2,3},{3,2},{4,0},{5,1},{6,7},{7,6},{8,12},{9,13},{10,... | collective-permute-start | bytes 3686408 | tf_op jit(solution)/shard_map/ppermute | solution.py:86
  449.5 65.8 %collective-permute-start.22 = (bf16[384,3072]{1,0:T(8,128)(2,1)S(1)}, bf16[384,3072]{1,0:T(8,128)(2,1)S(1)}, u32[]{:S(2)}, u32[]{:S(2)}) collective-permute-start(bf16[384,3072]{1,0:T(8,128)(2,1)S(1)} %maximum_select_fusion.4), channel_id=1, source_target_pairs={{0,2},{1,3},{2,0},{3,1},{4,6},{5,7},{6,4},{7,5},{8,10},{9,11},{10,... | collective-permute-start | bytes 7077896 | tf_op jit(solution)/shard_map/ppermute | solution.py:86
  462.1 16.5 %copy-start.12 = (f32[1024,768]{1,0:T(8,128)S(1)}, f32[1024,768]{1,0:T(8,128)}, u32[]{:S(2)}) copy-start(f32[1024,768]{1,0:T(8,128)} %copy-done.11) | copy-start | bytes 9437188
  462.1 48.9 %collective-permute-start.32 = (bf16[1536,768]{1,0:T(8,128)(2,1)S(1)}, bf16[1536,768]{1,0:T(8,128)(2,1)S(1)}, u32[]{:S(2)}, u32[]{:S(2)}) collective-permute-start(bf16[1536,768]{1,0:T(8,128)(2,1)S(1)} %maximum_select_fusion.5), channel_id=1, source_target_pairs={{0,2},{1,3},{2,0},{3,1},{4,6},{5,7},{6,4},{7,5},{8,10},{9,11},{10,... | collective-permute-start | bytes 7077896 | tf_op jit(solution)/shard_map/ppermute | solution.py:86
  475.5 44.6 %collective-permute-start.12 = (bf16[384,3200]{1,0:T(8,128)(2,1)S(1)}, bf16[384,3200]{1,0:T(8,128)(2,1)S(1)}, u32[]{:S(2)}, u32[]{:S(2)}) collective-permute-start(bf16[384,3200]{1,0:T(8,128)(2,1)S(1)} %maximum_select_fusion.3), channel_id=1, source_target_pairs={{0,2},{1,3},{2,0},{3,1},{4,6},{5,7},{6,4},{7,5},{8,10},{9,11},{10,... | collective-permute-start | bytes 7372808 | tf_op jit(solution)/shard_map/ppermute | solution.py:86
  485.0 24.5 %collective-permute-start.2 = (bf16[2,1,256,768]{3,2,1,0:T(8,128)(2,1)S(1)}, bf16[2,1,256,768]{3,2,1,0:T(8,128)(2,1)S(1)}, u32[]{:S(2)}, u32[]{:S(2)}) collective-permute-start(bf16[2,1,256,768]{3,2,1,0:T(8,128)(2,1)S(1)} %get-tuple-element.100), channel_id=1, source_target_pairs={{0,1},{1,0},{2,3},{3,2},{4,5},{5,4},{6,7},{7,6},{8,9},{9,8},{10,11... | collective-permute-start | bytes 2359304 | tf_op jit(solution)/shard_map/ppermute | solution.py:92
  488.0 20.7 %collective-permute-start.1 = (f32[2,1,32,768]{3,2,0,1:T(8,128)S(1)}, f32[2,1,32,768]{3,2,0,1:T(8,128)S(1)}, u32[]{:S(2)}, u32[]{:S(2)}) collective-permute-start(f32[2,1,32,768]{3,2,0,1:T(8,128)S(1)} %fusion.40), channel_id=1, source_target_pairs={{0,1},{1,0},{2,3},{3,2},{4,5},{5,4},{6,7},{7,6},{8,9},{9,8},{10,11... | collective-permute-start | bytes 589832 | tf_op jit(solution)/shard_map/ppermute | solution.py:92
  (11 other events, 17.3 us)

commit v2 on v1

v2 whole, which is shorter than its diff:
```python
import functools

import jax
import jax.numpy as jnp
from jax import lax
from jax.experimental import pallas as pl
from jax.experimental.pallas import tpu as pltpu
from jax.sharding import PartitionSpec as P

D = 768
HEADS = 12
HEAD_DIM = 64
FF = 3072
SEGS = 32
NORM_EPS = 1e-05
MASK_FILL = -1e30
BF = jnp.bfloat16
F32 = jnp.float32
VMEM_LIMIT = 60 * 1024 * 1024
PAIR = 2 * HEAD_DIM
STRIP = 128
CHUNK = 512
STAT_ROWS = 4 * HEADS

NN = (((1,), (0,)), ((), ()))
NT = (((1,), (1,)), ((), ()))
TN = (((0,), (0,)), ((), ()))


def mm(left, right, dims=NN):
    return lax.dot_general(left, right, dims, preferred_element_type=F32)


def whole(shape):
    zeros = (0,) * len(shape)
    return pl.BlockSpec(shape, lambda *_: zeros, pipeline_mode=pl.Buffered(1))


def params():
    return pltpu.CompilerParams(vmem_limit_bytes=VMEM_LIMIT)


def row_mean(value):
    return jnp.sum(value, axis=-1, keepdims=True) * (1.0 / D)


def attend_forward(at_ref, own_ref, got_ref, idc_ref, idr_ref, wqkv_ref, bqkv_ref, wo_ref, bo_ref, qkv_ref, xt_ref, ctxt_ref, lse_ref, xhat_ref, inv_ref, x_ref, ctx_ref, mask_ref, stat_ref):
    length = x_ref.shape[0]
    half = length // 2
    x_ref[pl.ds(pl.multiple_of(at_ref[0] * half, half), half), :] = own_ref[...]
    x_ref[pl.ds(pl.multiple_of((1 - at_ref[0]) * half, half), half), :] = got_ref[...]
    xt_ref[...] = jnp.transpose(x_ref[...])
    for c in range(3):
        cols = pl.ds(c * D, D)
        part = mm(x_ref[...], wqkv_ref[:, cols]) + bqkv_ref[:, cols]
        part = part.astype(BF)
        if c == 0:
            part = part * BF(HEAD_DIM**-0.5)
        qkv_ref[:, cols] = part
    mask_ref[...] = jnp.where(idc_ref[...] == idr_ref[...], 0.0, MASK_FILL)
    low = lax.broadcasted_iota(jnp.int32, (length, PAIR), 1) < HEAD_DIM
    low_strip = lax.broadcasted_iota(jnp.int32, (STRIP, PAIR), 1) < HEAD_DIM
    lane = lax.broadcasted_iota(jnp.int32, (STRIP, 128), 1)
    stat_ref[...] = jnp.zeros_like(stat_ref)

    def pair_step(p, carry):
        at = pl.multiple_of(p * PAIR, PAIR)
        keys = qkv_ref[:, pl.ds(D + at, PAIR)]
        values = qkv_ref[:, pl.ds(2 * D + at, PAIR)]
        value_of = [jnp.where(low, values, BF(0)), jnp.where(low, BF(0), values)]
        for s in range(length // STRIP):
            rows = pl.ds(s * STRIP, STRIP)
            queries = qkv_ref[rows, pl.ds(at, PAIR)]
            outs = []
            stats = stat_ref[rows, :]
            for h in range(2):
                query = jnp.where(low_strip, queries, BF(0)) if h == 0 else jnp.where(low_strip, BF(0), queries)
                scores = mm(query, keys, NT) + mask_ref[rows, :]
                top = jnp.max(scores, axis=-1, keepdims=True)
                exps = jnp.exp(scores - top)
                total = jnp.sum(exps, axis=-1, keepdims=True)
                outs.append(mm(exps.astype(BF), value_of[h]) * (1.0 / total))
                stats = jnp.where(lane == 8 * p + h, top + jnp.log(total), stats)
            ctx_ref[rows, pl.ds(at, PAIR)] = (outs[0] + outs[1]).astype(BF)
            stat_ref[rows, :] = stats
        return carry

    lax.fori_loop(0, HEADS // 2, pair_step, 0)
    lse_ref[...] = jnp.transpose(stat_ref[...])[: lse_ref.shape[0], :]
    ctxt_ref[...] = jnp.transpose(ctx_ref[...])
    total_in = mm(ctx_ref[...], wo_ref[...]) + bo_ref[...] + x_ref[...].astype(F32)
    centered = total_in - row_mean(total_in)
    inv = lax.rsqrt(row_mean(centered * centered) + NORM_EPS)
    xhat_ref[...] = centered * inv
    inv_ref[...] = jnp.broadcast_to(inv, inv_ref.shape)


def run_attend_forward(at, hidden, got, ids, wqkv, bqkv, wo, bo):
    rows, half, _ = got.shape
    length = 2 * half
    row_spec = lambda *tail: pl.BlockSpec((None,) + tail, lambda r, at: (r,) + (0,) * len(tail))
    turned = pl.BlockSpec((D, length), lambda r, at: (0, r))
    return pl.pallas_call(
        attend_forward,
        grid_spec=pltpu.PrefetchScalarGridSpec(
            num_scalar_prefetch=1,
            grid=(rows,),
            in_specs=[
                pl.BlockSpec((None, half, D), lambda r, at: (at[0] * rows + r, 0, 0)),
                row_spec(half, D), row_spec(length, 1), row_spec(1, length), whole((D, 3 * D)), whole((1, 3 * D)), whole((D, D)), whole((1, D))],
            out_specs=[row_spec(length, 3 * D), turned, turned, row_spec(STAT_ROWS, length), row_spec(length, D), row_spec(length, 128)],
            scratch_shapes=[pltpu.VMEM((length, D), BF), pltpu.VMEM((length, D), BF), pltpu.VMEM((length, length), F32), pltpu.VMEM((length, 128), F32)],
        ),
        out_shape=[
            jax.ShapeDtypeStruct((rows, length, 3 * D), BF),
            jax.ShapeDtypeStruct((D, rows * length), BF),
            jax.ShapeDtypeStruct((D, rows * length), BF),
            jax.ShapeDtypeStruct((rows, STAT_ROWS, length), F32),
            jax.ShapeDtypeStruct((rows, length, D), F32),
            jax.ShapeDtypeStruct((rows, length, 128), F32),
        ],
        compiler_params=params(),
        name="attend_forward",
    )(at, hidden, got, ids[:, :, None], ids[:, None, :], wqkv, bqkv[None], wo, bo[None])


def gelu_parts(value):
    cdf = 0.5 * (1.0 + lax.erf(value * (0.5**0.5)))
    density = jnp.exp(-0.5 * value * value) * 0.3989422804014327
    return cdf, cdf + value * density


def split_terms(value, count):
    parts = []
    for _ in range(count):
        part = value.astype(BF)
        parts.append(part)
        value = value - part.astype(F32)
    return parts


def feed_forward(xhat_ref, idc_ref, idr_ref, cnt_ref, pg_ref, g1_ref, s1_ref, up_ref, upb_ref, down_ref, downb_ref, g2_ref, s2_ref,
                 midt_ref, actt_ref, slope_ref, gh2_ref, gdl_ref, pooled_ref, sums_ref, mid_ref, acc_ref):
    length = xhat_ref.shape[0]
    mid = xhat_ref[...] * g1_ref[...] + s1_ref[...]
    mid_ref[...] = mid.astype(BF)
    midt_ref[...] = jnp.transpose(mid_ref[...])
    acc_ref[...] = mid + downb_ref[...]

    def chunk_step(c, carry):
        cols = pl.ds(pl.multiple_of(c * CHUNK, CHUNK), CHUNK)
        pre = mm(mid_ref[...], up_ref[:, cols]) + upb_ref[:, cols]
        cdf, slope = gelu_parts(pre)
        act = (pre * cdf).astype(BF)
        actt_ref[cols, :] = jnp.transpose(act)
        slope_ref[:, cols] = slope.astype(BF)
        acc_ref[...] += mm(act, down_ref[cols, :])
        return carry

    lax.fori_loop(0, FF // CHUNK, chunk_step, 0)
    total_in = acc_ref[...]
    centered = total_in - row_mean(total_in)
    inv = lax.rsqrt(row_mean(centered * centered) + NORM_EPS)
    normed = centered * inv
    final = normed * g2_ref[...] + s2_ref[...]
    member = (lax.broadcasted_iota(jnp.int32, (SEGS, length), 0) == idr_ref[...]).astype(BF)
    sums = sum(mm(member, part) for part in split_terms(final, 3))
    pooled_ref[...] = sums / cnt_ref[...]
    spread = (lax.broadcasted_iota(jnp.int32, (length, SEGS), 1) == idc_ref[...]).astype(BF)
    grad_final = sum(mm(spread, part) for part in split_terms(pg_ref[...] / cnt_ref[...], 3))
    scaled = grad_final * g2_ref[...]
    grad_h2 = inv * (scaled - row_mean(scaled) - normed * row_mean(scaled * normed))
    gh2_ref[...] = grad_h2
    low = grad_h2.astype(BF)
    gdl_ref[...] = low
    sums_ref[0:1, :] = jnp.sum(grad_final * normed, axis=0, keepdims=True)
    sums_ref[1:2, :] = jnp.sum(grad_final, axis=0, keepdims=True)
    sums_ref[2:3, :] = jnp.sum(low.astype(F32), axis=0, keepdims=True)
    sums_ref[3:8, :] = jnp.zeros((5, D), F32)


def run_feed_forward(xhat, ids, counts, pooled_grad, g1, s1, up, upb, down, downb, g2, s2):
    rows, length, _ = xhat.shape
    row_spec = lambda *tail: pl.BlockSpec((None,) + tail, lambda r: (r,) + (0,) * len(tail))
    return pl.pallas_call(
        feed_forward,
        grid=(rows,),
        in_specs=[row_spec(length, D), row_spec(length, 1), row_spec(1, length), row_spec(SEGS, 1), row_spec(SEGS, D), whole((1, D)), whole((1, D)),
                  whole((D, FF)), whole((1, FF)), whole((FF, D)), whole((1, D)), whole((1, D)), whole((1, D))],
        out_specs=[pl.BlockSpec((D, length), lambda r: (0, r)), pl.BlockSpec((FF, length), lambda r: (0, r)), row_spec(length, FF), row_spec(length, D), row_spec(length, D), row_spec(SEGS, D), row_spec(8, D)],
        out_shape=[
            jax.ShapeDtypeStruct((D, rows * length), BF),
            jax.ShapeDtypeStruct((FF, rows * length), BF),
            jax.ShapeDtypeStruct((rows, length, FF), BF),
            jax.ShapeDtypeStruct((rows, length, D), F32),
            jax.ShapeDtypeStruct((rows, length, D), BF),
            jax.ShapeDtypeStruct((rows, SEGS, D), F32),
            jax.ShapeDtypeStruct((rows, 8, D), F32),
        ],
        scratch_shapes=[pltpu.VMEM((length, D), BF), pltpu.VMEM((length, D), F32)],
        compiler_params=params(),
        name="feed_forward",
    )(xhat, ids[:, :, None], ids[:, None, :], counts.astype(F32)[:, :, None], pooled_grad, g1[None], s1[None], up, upb[None], down, downb[None], g2[None], s2[None])


def feed_backward(gdl_ref, slope_ref, gh2_ref, xhat_ref, inv_ref, g1_ref, up_ref, down_ref, gul_ref, gh1_ref, gal_ref, sums_ref, upsum_ref, acc_ref):
    acc_ref[...] = gh2_ref[...]

    def chunk_step(c, carry):
        cols = pl.ds(pl.multiple_of(c * CHUNK, CHUNK), CHUNK)
        grad_act = mm(gdl_ref[...], down_ref[cols, :], NT)
        low = (grad_act * slope_ref[:, cols].astype(F32)).astype(BF)
        gul_ref[:, cols] = low
        upsum_ref[0:1, cols] = jnp.sum(low.astype(F32), axis=0, keepdims=True)
        acc_ref[...] += mm(low, up_ref[:, cols], NT)
        return carry

    lax.fori_loop(0, FF // CHUNK, chunk_step, 0)
    grad_mid = acc_ref[...]
    normed = xhat_ref[...]
    scaled = grad_mid * g1_ref[...]
    inv = inv_ref[:, 0:1]
    grad_h1 = inv * (scaled - row_mean(scaled) - normed * row_mean(scaled * normed))
    gh1_ref[...] = grad_h1
    low = grad_h1.astype(BF)
    gal_ref[...] = low
    sums_ref[0:1, :] = jnp.sum(grad_mid * normed, axis=0, keepdims=True)
    sums_ref[1:2, :] = jnp.sum(grad_mid, axis=0, keepdims=True)
    sums_ref[2:3, :] = jnp.sum(low.astype(F32), axis=0, keepdims=True)
    sums_ref[3:8, :] = jnp.zeros((5, D), F32)


def run_feed_backward(gdl, slope, gh2, xhat, inv, g1, up, down):
    rows, length, _ = gdl.shape
    row_spec = lambda *tail: pl.BlockSpec((None,) + tail, lambda r: (r,) + (0,) * len(tail))
    return pl.pallas_call(
        feed_backward,
        grid=(rows,),
        in_specs=[row_spec(length, D), row_spec(length, FF), row_spec(length, D), row_spec(length, D), row_spec(length, 128), whole((1, D)), whole((D, FF)), whole((FF, D))],
        out_specs=[row_spec(length, FF), row_spec(length, D), row_spec(length, D), row_spec(8, D), row_spec(1, FF)],
        out_shape=[
            jax.ShapeDtypeStruct((rows, length, FF), BF),
            jax.ShapeDtypeStruct((rows, length, D), F32),
            jax.ShapeDtypeStruct((rows, length, D), BF),
            jax.ShapeDtypeStruct((rows, 8, D), F32),
            jax.ShapeDtypeStruct((rows, 1, FF), F32),
        ],
        scratch_shapes=[pltpu.VMEM((length, D), F32)],
        compiler_params=params(),
        name="feed_backward",
    )(gdl, slope, gh2, xhat, inv, g1[None], up, down)


def attend_backward(at_ref, gal_ref, gh1_ref, qkv_ref, lse_ref, idc_ref, idr_ref, wo_ref, wqkv_ref, gqkv_ref, own_ref, send_ref, sums_ref, mask_ref, gctx_ref):
    length = gal_ref.shape[0]
    gctx_ref[...] = mm(gal_ref[...], wo_ref[...], NT).astype(BF)
    mask_ref[...] = jnp.where(idc_ref[...] == idr_ref[...], 0.0, MASK_FILL)
    low_strip = lax.broadcasted_iota(jnp.int32, (STRIP, PAIR), 1) < HEAD_DIM
    low = lax.broadcasted_iota(jnp.int32, (length, PAIR), 1) < HEAD_DIM

    def pair_step(p, carry):
        at = pl.multiple_of(p * PAIR, PAIR)
        keys = qkv_ref[:, pl.ds(D + at, PAIR)]
        values = qkv_ref[:, pl.ds(2 * D + at, PAIR)]
        key_of = [jnp.where(low, keys, BF(0)), jnp.where(low, BF(0), keys)]
        grad_k = jnp.zeros((length, PAIR), F32)
        grad_v = jnp.zeros((length, PAIR), F32)
        for s in range(length // STRIP):
            rows = pl.ds(s * STRIP, STRIP)
            lses = lse_ref[pl.ds(pl.multiple_of(8 * p, 8), 8), rows]
            queries = qkv_ref[rows, pl.ds(at, PAIR)]
            grads = gctx_ref[rows, pl.ds(at, PAIR)]
            grad_q = jnp.zeros((STRIP, PAIR), F32)
            for h in range(2):
                pick = (lambda v: jnp.where(low_strip, v, BF(0))) if h == 0 else (lambda v: jnp.where(low_strip, BF(0), v))
                query, grad = pick(queries), pick(grads)
                scores = mm(keys, query, NT) + mask_ref[:, rows]
                probs = jnp.exp(scores - lses[h : h + 1, :])
                grad_p = mm(values, grad, NT)
                inner = jnp.sum(probs * grad_p, axis=0, keepdims=True)
                grad_s = (probs * (grad_p - inner)).astype(BF)
                grad_v += mm(probs.astype(BF), grad)
                grad_k += mm(grad_s, query)
                grad_q += mm(grad_s, key_of[h], TN)
            low_q = (grad_q * HEAD_DIM**-0.5).astype(BF)
            gqkv_ref[rows, pl.ds(at, PAIR)] = low_q
        gqkv_ref[:, pl.ds(D + at, PAIR)] = grad_k.astype(BF)
        gqkv_ref[:, pl.ds(2 * D + at, PAIR)] = grad_v.astype(BF)
        return carry

    lax.fori_loop(0, HEADS // 2, pair_step, 0)
    half = length // 2
    for out, first in ((own_ref, at_ref[0]), (send_ref, 1 - at_ref[0])):
        rows = pl.ds(pl.multiple_of(first * half, half), half)
        out[...] = (gh1_ref[rows, :] + mm(gqkv_ref[rows, :], wqkv_ref[...], NT)).astype(BF)
    sums_ref[...] = jnp.sum(gqkv_ref[...].astype(F32), axis=0, keepdims=True)


def run_attend_backward(at, gal, gh1, qkv, lse, ids, wo, wqkv):
    rows, length, _ = gal.shape
    half = length // 2
    row_spec = lambda *tail: pl.BlockSpec((None,) + tail, lambda r, at: (r,) + (0,) * len(tail))
    return pl.pallas_call(
        attend_backward,
        grid_spec=pltpu.PrefetchScalarGridSpec(
            num_scalar_prefetch=1,
            grid=(rows,),
            in_specs=[row_spec(length, D), row_spec(length, D), row_spec(length, 3 * D), row_spec(STAT_ROWS, length), row_spec(length, 1), row_spec(1, length), whole((D, D)), whole((D, 3 * D))],
            out_specs=[row_spec(length, 3 * D), row_spec(half, D), row_spec(half, D), row_spec(1, 3 * D)],
            scratch_shapes=[pltpu.VMEM((length, length), F32), pltpu.VMEM((length, D), BF)],
        ),
        out_shape=[
            jax.ShapeDtypeStruct((rows, length, 3 * D), BF),
            jax.ShapeDtypeStruct((rows, half, D), BF),
            jax.ShapeDtypeStruct((rows, half, D), BF),
            jax.ShapeDtypeStruct((rows, 1, 3 * D), F32),
        ],
        compiler_params=params(),
        name="attend_backward",
    )(at, gal, gh1, qkv, lse, ids[:, :, None], ids[:, None, :], wo, wqkv)


def grad_send(sides_ref, left_ref, right_ref, out_ref):
    out_ref[...] = mm(left_ref[...], right_ref[...]).astype(BF)


def grad_keep(sides_ref, left_send_ref, left_keep_ref, right_ref, got_send_ref, got_keep_ref, send_ref, keep_ref):
    right = right_ref[...]
    send_ref[...] = (mm(left_send_ref[...], right) + got_send_ref[...].astype(F32)).astype(BF)
    keep_ref[...] = mm(left_keep_ref[...], right) + got_keep_ref[...].astype(F32)


BLOCK = 384


def down_send(sides, left, right):
    total, width = left.shape[0], right.shape[1]
    steps = total // 2 // BLOCK
    return pl.pallas_call(
        grad_send,
        grid_spec=pltpu.PrefetchScalarGridSpec(
            num_scalar_prefetch=1,
            grid=(steps,),
            in_specs=[pl.BlockSpec((BLOCK, left.shape[1]), lambda i, sd: ((1 - sd[0]) * steps + i, 0)), whole(right.shape)],
            out_specs=pl.BlockSpec((BLOCK, width), lambda i, sd: (i, 0)),
        ),
        out_shape=jax.ShapeDtypeStruct((total // 2, width), BF),
        compiler_params=params(),
        name="down_send",
    )(sides, left, right)


def down_keep(sides, left, right, got):
    total, width = left.shape[0], right.shape[1]
    steps = total // 4 // BLOCK
    left_at = lambda part: pl.BlockSpec((BLOCK, left.shape[1]), lambda i, sd: ((2 * sd[0] + part(sd[1])) * steps + i, 0))
    got_at = lambda part: pl.BlockSpec((BLOCK, width), lambda i, sd: (part(sd[1]) * steps + i, 0))
    away, here = (lambda side: 1 - side), (lambda side: side)
    return pl.pallas_call(
        grad_keep,
        grid_spec=pltpu.PrefetchScalarGridSpec(
            num_scalar_prefetch=1,
            grid=(steps,),
            in_specs=[left_at(away), left_at(here), whole(right.shape), got_at(away), got_at(here)],
            out_specs=[pl.BlockSpec((BLOCK, width), lambda i, sd: (i, 0))] * 2,
        ),
        out_shape=[jax.ShapeDtypeStruct((total // 4, width), BF), jax.ShapeDtypeStruct((total // 4, width), F32)],
        compiler_params=params(),
        name="down_keep",
    )(sides, left, left, right, got, got)


def up_send_body(steps, sides_ref, mid_ref, gul_ref, ctx_ref, gal_ref, out_ref):
    @pl.when(pl.program_id(0) < steps)
    def _():
        out_ref[...] = mm(mid_ref[...], gul_ref[...]).astype(BF)

    @pl.when(pl.program_id(0) == steps)
    def _():
        out_ref[...] = mm(ctx_ref[...], gal_ref[...]).astype(BF)


def up_send(sides, mid, gul, ctx, gal):
    steps, half, tokens = FF // D, D // 2, mid.shape[1]
    return pl.pallas_call(
        functools.partial(up_send_body, steps),
        grid_spec=pltpu.PrefetchScalarGridSpec(
            num_scalar_prefetch=1,
            grid=(steps + 1,),
            in_specs=[
                pl.BlockSpec((half, tokens), lambda j, sd: (1 - sd[0], 0)),
                pl.BlockSpec((tokens, D), lambda j, sd: (0, jnp.minimum(j, steps - 1))),
                pl.BlockSpec((half, tokens), lambda j, sd: (1 - sd[0], 0)),
                whole(gal.shape),
            ],
            out_specs=pl.BlockSpec((half, D), lambda j, sd: (0, j)),
        ),
        out_shape=jax.ShapeDtypeStruct((half, FF + D), BF),
        compiler_params=params(),
        name="up_send",
    )(sides, mid, gul, ctx, gal)


def up_keep_body(steps, sides_ref, mid_send_ref, mid_keep_ref, gul_ref, ctx_send_ref, ctx_keep_ref, gal_ref, got_send_ref, got_keep_ref, send_ref, keep_ref):
    @pl.when(pl.program_id(0) < steps)
    def _():
        send_ref[...] = (mm(mid_send_ref[...], gul_ref[...]) + got_send_ref[...].astype(F32)).astype(BF)
        keep_ref[...] = mm(mid_keep_ref[...], gul_ref[...]) + got_keep_ref[...].astype(F32)

    @pl.when(pl.program_id(0) == steps)
    def _():
        send_ref[...] = (mm(ctx_send_ref[...], gal_ref[...]) + got_send_ref[...].astype(F32)).astype(BF)
        keep_ref[...] = mm(ctx_keep_ref[...], gal_ref[...]) + got_keep_ref[...].astype(F32)


def up_keep(sides, mid, gul, ctx, gal, got):
    steps, quarter, tokens = FF // D, D // 4, mid.shape[1]
    away, here = (lambda side: 1 - side), (lambda side: side)
    left_at = lambda part: pl.BlockSpec((quarter, tokens), lambda j, sd: (2 * sd[0] + part(sd[1]), 0))
    got_at = lambda part: pl.BlockSpec((quarter, D), lambda j, sd: (part(sd[1]), j))
    return pl.pallas_call(
        functools.partial(up_keep_body, steps),
        grid_spec=pltpu.PrefetchScalarGridSpec(
            num_scalar_prefetch=1,
            grid=(steps + 1,),
            in_specs=[
                left_at(away), left_at(here), pl.BlockSpec((tokens, D), lambda j, sd: (0, jnp.minimum(j, steps - 1))),
                left_at(away), left_at(here), whole(gal.shape), got_at(away), got_at(here),
            ],
            out_specs=[pl.BlockSpec((quarter, D), lambda j, sd: (0, j))] * 2,
        ),
        out_shape=[jax.ShapeDtypeStruct((quarter, FF + D), BF), jax.ShapeDtypeStruct((quarter, FF + D), F32)],
        compiler_params=params(),
        name="up_keep",
    )(sides, mid, mid, gul, ctx, ctx, gal, got, got)


SMALLS = 128


def gather_small(sums1_ref, sums2_ref, ups_ref, sq_ref, small_ref, pack_ref):
    pack_ref[...] = jnp.zeros_like(pack_ref)
    total = lambda ref: jnp.sum(ref[...], axis=0)
    first, second, ups, sq = total(sums1_ref), total(sums2_ref), total(ups_ref), total(sq_ref)
    lines = [sq[:, :D], sq[:, 2 * D :], first[2:3], first[0:1], first[1:2], second[2:3], second[0:1], second[1:2]]
    lines += [ups[:, i * D : (i + 1) * D] for i in range(FF // D)]
    for i, line in enumerate(lines):
        pack_ref[i : i + 1, :] = line
    small_ref[...] = jnp.transpose(pack_ref[...])


def tail_send_body(sides_ref, x_ref, gqkv_ref, sums1_ref, sums2_ref, ups_ref, sq_ref, out_ref, small_ref, pack_ref):
    half = x_ref.shape[0]
    gather_small(sums1_ref, sums2_ref, ups_ref, sq_ref, small_ref, pack_ref)
    out_ref[:, : 3 * D] = mm(x_ref[...], gqkv_ref[...]).astype(BF)
    rows = pl.ds(pl.multiple_of((1 - sides_ref[0]) * half, half), half)
    out_ref[:, 3 * D :] = small_ref[rows, :].astype(BF)


def tail_send(sides, x, gqkv, smalls):
    half, tokens = D // 2, x.shape[1]
    return pl.pallas_call(
        tail_send_body,
        grid_spec=pltpu.PrefetchScalarGridSpec(
            num_scalar_prefetch=1,
            grid=(1,),
            in_specs=[pl.BlockSpec((half, tokens), lambda j, sd: (1 - sd[0], 0)), whole(gqkv.shape)] + [whole(v.shape) for v in smalls],
            out_specs=pl.BlockSpec((half, 3 * D + SMALLS), lambda j, sd: (0, 0)),
            scratch_shapes=[pltpu.VMEM((D, SMALLS), F32), pltpu.VMEM((SMALLS, D), F32)],
        ),
        out_shape=jax.ShapeDtypeStruct((half, 3 * D + SMALLS), BF),
        compiler_params=params(),
        name="tail_send",
    )(sides, x, gqkv, *smalls)


def tail_keep_body(sides_ref, x_send_ref, x_keep_ref, gqkv_ref, sums1_ref, sums2_ref, ups_ref, sq_ref, got_send_ref, got_keep_ref, send_ref, keep_ref, small_ref, pack_ref):
    quarter = x_send_ref.shape[0]
    gather_small(sums1_ref, sums2_ref, ups_ref, sq_ref, small_ref, pack_ref)
    for left, got, out, side in ((x_send_ref, got_send_ref, send_ref, 1 - sides_ref[1]), (x_keep_ref, got_keep_ref, keep_ref, sides_ref[1])):
        rows = pl.ds(pl.multiple_of((2 * sides_ref[0] + side) * quarter, quarter), quarter)
        out[:, : 3 * D] = (mm(left[...], gqkv_ref[...]) + got[:, : 3 * D].astype(F32)).astype(out.dtype)
        out[:, 3 * D :] = (small_ref[rows, :] + got[:, 3 * D :].astype(F32)).astype(out.dtype)


def tail_keep(sides, x, gqkv, smalls, got):
    quarter, tokens, width = D // 4, x.shape[1], 3 * D + SMALLS
    away, here = (lambda side: 1 - side), (lambda side: side)
    left_at = lambda part: pl.BlockSpec((quarter, tokens), lambda j, sd: (2 * sd[0] + part(sd[1]), 0))
    got_at = lambda part: pl.BlockSpec((quarter, width), lambda j, sd: (part(sd[1]), 0))
    return pl.pallas_call(
        tail_keep_body,
        grid_spec=pltpu.PrefetchScalarGridSpec(
            num_scalar_prefetch=1,
            grid=(1,),
            in_specs=[left_at(away), left_at(here), whole(gqkv.shape)] + [whole(v.shape) for v in smalls] + [got_at(away), got_at(here)],
            out_specs=[pl.BlockSpec((quarter, width), lambda j, sd: (0, 0))] * 2,
            scratch_shapes=[pltpu.VMEM((D, SMALLS), F32), pltpu.VMEM((SMALLS, D), F32)],
        ),
        out_shape=[jax.ShapeDtypeStruct((quarter, width), BF), jax.ShapeDtypeStruct((quarter, width), F32)],
        compiler_params=params(),
        name="tail_keep",
    )(sides, x, x, gqkv, *smalls, got, got)


def add_split_body(at_ref, keep_away_ref, keep_here_ref, got_away_ref, got_here_ref, send_ref, next_ref):
    send_ref[...] = (keep_away_ref[...] + got_away_ref[...].astype(F32)).astype(BF)
    next_ref[...] = keep_here_ref[...] + got_here_ref[...].astype(F32)


def add_split(at, keep, got):
    half, width = keep.shape[0] // 2, keep.shape[1]
    cols = width // 2 if width % 256 == 0 else width
    away = pl.BlockSpec((half, cols), lambda j, at: (1 - at[0], j))
    here = pl.BlockSpec((half, cols), lambda j, at: (at[0], j))
    return pl.pallas_call(
        add_split_body,
        grid_spec=pltpu.PrefetchScalarGridSpec(
            num_scalar_prefetch=1,
            grid=(width // cols,),
            in_specs=[away, here, away, here],
            out_specs=[pl.BlockSpec((half, cols), lambda j, at: (0, j))] * 2,
        ),
        out_shape=[jax.ShapeDtypeStruct((half, width), BF), jax.ShapeDtypeStruct((half, width), F32)],
        compiler_params=params(),
        name="add_split",
    )(at, keep, keep, got, got)


def assemble_body(steps, widths, place_ref, *refs):
    pieces, outs = refs[:4], refs[4:]
    at = pl.program_id(0) // steps
    for p in range(4):

        @pl.when(at == p)
        def _(p=p):
            start = 0
            for out, width in zip(outs, widths):
                out[...] = pieces[p][:, start : start + width].astype(F32)
                start += width


def assemble(places, pieces, widths):
    quarter, width = pieces[0].shape
    block = min(quarter, 96)
    steps = quarter // block
    return pl.pallas_call(
        functools.partial(assemble_body, steps, widths),
        grid_spec=pltpu.PrefetchScalarGridSpec(
            num_scalar_prefetch=1,
            grid=(4 * steps,),
            in_specs=[pl.BlockSpec((block, width), lambda i, pos, p=p: (jnp.clip(i - p * steps, 0, steps - 1), 0)) for p in range(4)],
            out_specs=[pl.BlockSpec((block, w), lambda i, pos: (pos[i // steps] * steps + i % steps, 0)) for w in widths],
        ),
        out_shape=[jax.ShapeDtypeStruct((4 * quarter, w), F32) for w in widths],
        compiler_params=params(),
        name="assemble",
    )(places, *pieces)


class Links:
    def __init__(self):
        dp, seq = lax.axis_size("dp"), lax.axis_size("seq")
        dp_at, seq_at = lax.axis_index("dp"), lax.axis_index("seq")
        self.core = dp_at % 2

        def flip(bit_of):
            pairs = []
            for d in range(dp):
                for s in range(seq):
                    bit = bit_of(d % 2)
                    to = (d, s ^ 1) if bit < 0 else (d ^ (1 << bit), s)
                    pairs.append((d * seq + s, to[0] * seq + to[1]))
            return pairs

        second = (dp_at >> 1) % 2
        self.side_a = jnp.where(self.core == 0, second, seq_at)
        self.side_b = jnp.where(self.core == 0, seq_at, second)
        self.pairs_core = flip(lambda c: 0)
        self.pairs_a = flip(lambda c: 1 if c == 0 else -1)
        self.pairs_b = flip(lambda c: -1 if c == 0 else 1)
        self.rest = [(flip(lambda c, bit=bit: bit), (dp_at >> bit) % 2) for bit in range(2, (dp - 1).bit_length())]
        self.sides = jnp.stack([self.core, self.side_a]).astype(jnp.int32)
        self.side_b_array = self.side_b.astype(jnp.int32).reshape(1)
        other = 2 * (1 - self.core)
        mine = 2 * self.core
        self.places = jnp.stack([mine + self.side_a, mine + 1 - self.side_a, other + self.side_b, other + 1 - self.side_b]).astype(jnp.int32)

    def send(self, value, pairs):
        return lax.ppermute(value, ("dp", "seq"), pairs)

    def reduce_rest(self, keep, got):
        cur = keep + got.astype(F32)
        for pairs, at in self.rest:
            half = cur.shape[0] // 2
            away = lax.dynamic_slice_in_dim(cur, (1 - at) * half, half, 0).astype(BF)
            cur = lax.dynamic_slice_in_dim(cur, at * half, half, 0) + self.send(away, pairs).astype(F32)
        return cur.astype(BF)

    def spread_rest(self, part):
        cur = part
        for pairs, at in reversed(self.rest):
            got = self.send(cur, pairs)
            cur = jnp.where(at == 0, jnp.concatenate([cur, got]), jnp.concatenate([got, cur]))
        return cur

    def finish(self, away, keep, widths):
        got = self.send(away, self.pairs_a)
        away, keep = add_split(self.side_b_array, keep, got)
        got = self.send(away, self.pairs_b)
        part = self.reduce_rest(keep, got)
        cur = self.spread_rest(part)
        got = self.send(cur, self.pairs_b)
        quarter = jnp.where(self.side_b == 0, jnp.concatenate([cur, got]), jnp.concatenate([got, cur]))
        got = self.send(quarter, self.pairs_a)
        pieces = [quarter, got, self.send(quarter, self.pairs_core), self.send(got, self.pairs_core)]
        return assemble(self.places, pieces, widths)


def swap_seq(value):
    return lax.ppermute(value, "seq", [(0, 1), (1, 0)])


def local(
    hidden_in,
    segment_ids,
    segment_counts,
    pooled_grad,
    qkv_weight,
    query_bias,
    value_bias,
    out_weight,
    out_bias,
    norm1_gain,
    norm1_shift,
    up_weight,
    up_bias,
    down_weight,
    down_bias,
    norm2_gain,
    norm2_shift,
):
    links = Links()
    seq_at = lax.axis_index("seq")
    seq_array = seq_at.astype(jnp.int32).reshape(1)
    micro, row_count, piece, _ = hidden_in.shape
    length = piece * 2
    own_micro = micro // 2
    rows = own_micro * row_count
    tokens = rows * length

    def own_part(value):
        return lax.dynamic_slice_in_dim(value, seq_at * own_micro, own_micro, 0)

    got = swap_seq(lax.dynamic_slice_in_dim(hidden_in, (1 - seq_at) * own_micro, own_micro, 0))
    counts = own_part(segment_counts).reshape(rows, SEGS)
    pooled_cot = own_part(pooled_grad).reshape(rows, SEGS, D)
    seg = jnp.arange(SEGS, dtype=jnp.int32)
    ends = jnp.sum(jnp.where(seg[None, :, None] <= seg[None, None, :], counts[:, :, None], 0), axis=1)
    positions = jnp.arange(length, dtype=jnp.int32)
    ids = jnp.sum((positions[None, :, None] >= ends[:, None, :-1]).astype(jnp.int32), axis=-1)
    shift_qkv = jnp.concatenate([query_bias, jnp.zeros((D,), F32), value_bias])

    qkv, x_turned, ctx_turned, lse, xhat, inv = run_attend_forward(
        seq_array,
        hidden_in.reshape(micro * row_count, piece, D),
        got.reshape(rows, piece, D),
        ids,
        qkv_weight,
        shift_qkv,
        out_weight,
        out_bias,
    )
    mid_turned, act_turned, slope, grad_h2, grad_down_low, pooled, sums2 = run_feed_forward(
        xhat, ids, counts, pooled_cot, norm1_gain, norm1_shift, up_weight, up_bias, down_weight, down_bias, norm2_gain, norm2_shift
    )
    flat_down = grad_down_low.reshape(tokens, D)
    got_down = links.send(down_send(links.sides, act_turned, flat_down), links.pairs_core)
    pooled_own = pooled.reshape(own_micro, row_count, SEGS, D)
    pooled_got = swap_seq(pooled_own)
    pooled_local = jnp.where(
        seq_at == 0, jnp.concatenate([pooled_own, pooled_got]), jnp.concatenate([pooled_got, pooled_own])
    )
    grad_up_low, grad_h1, grad_attn_low, sums1, ups = run_feed_backward(
        grad_down_low, slope, grad_h2, xhat, inv, norm1_gain, up_weight, down_weight
    )
    away_down, keep_down = down_keep(links.sides, act_turned, flat_down, got_down)
    flat_up, flat_attn = grad_up_low.reshape(tokens, FF), grad_attn_low.reshape(tokens, D)
    got_up = links.send(up_send(links.sides, mid_turned, flat_up, ctx_turned, flat_attn), links.pairs_core)
    away_up, keep_up = up_keep(links.sides, mid_turned, flat_up, ctx_turned, flat_attn, got_up)
    grad_qkv, back_own, back_send, sums_qkv = run_attend_backward(
        seq_array, grad_attn_low, grad_h1, qkv, lse, ids, out_weight, qkv_weight
    )
    back_own = back_own.reshape(own_micro, row_count, piece, D)
    back_got = swap_seq(back_send.reshape(own_micro, row_count, piece, D))
    input_local = jnp.where(
        seq_at == 0, jnp.concatenate([back_own, back_got]), jnp.concatenate([back_got, back_own])
    )
    smalls = (sums1, sums2, ups, sums_qkv)
    flat_qkv = grad_qkv.reshape(tokens, 3 * D)
    got_tail = links.send(tail_send(links.sides, x_turned, flat_qkv, smalls), links.pairs_core)
    away_tail, keep_tail = tail_keep(links.sides, x_turned, flat_qkv, smalls, got_tail)
    (down_all,) = links.finish(away_down, keep_down, (D,))
    up_all, out_all = links.finish(away_up, keep_up, (FF, D))
    qkv_all, small_all = links.finish(away_tail, keep_tail, (3 * D, SMALLS))
    lines = small_all[:, : 8 + FF // D].T
    return (
        pooled_local,
        input_local,
        qkv_all,
        lines[0],
        lines[1],
        out_all,
        lines[2],
        lines[3],
        lines[4],
        up_all,
        lines[8 : 8 + FF // D].reshape(FF),
        down_all,
        lines[5],
        lines[6],
        lines[7],
    )


def solution(mesh):
    rep = P()
    in_specs = (
        P(None, "dp", "seq", None),
        P(None, "dp", "seq"),
        P(None, "dp", None),
        P(None, "dp", None, None),
    ) + (rep,) * 13
    out_specs = (P(None, "dp", None, None), P(None, "dp", "seq", None)) + (rep,) * 13
    return jax.shard_map(local, mesh=mesh, in_specs=in_specs, out_specs=out_specs, check_vma=False)
```

time: 540 us -> 450 us (0.83)
  Pallas kernels: 0 us -> 228 us
  matrix products: 163 us -> 0 us
  other arithmetic: 97.9 us -> 8.86 us
  local copies, waits for them, and re-layouts: 81.7 us -> 19.9 us
  waiting for transfers between devices: 153 us -> 110 us
  starting transfers between devices: 38.5 us -> 80.5 us
    pallas_call x0 -> x16, Pallas kernels: none -> 228 us  [the longest x1 43 us: run_attend_backward(): pl.pallas_call(attend_backward, grid_spec=pltpu.PrefetchScalarGridSpec(nu...]
    dot_general x20 -> x0, matrix products: 163 us -> none  [the longest x4 31.1 us: back_product(): jnp.einsum('nf,df->nd', grad_low, weight_mat, preferred_element_type=F32)]
    ppermute x30 -> x33, starting transfers between devices: 34.8 us -> 74.1 us  [send(): return lax.ppermute(value, ('dp', 'seq'), pairs)]
    convert_element_type x8 -> x4, other arithmetic: 36.5 us -> 0.1 us  [the longest x3 0.09 us: reduce_rest(): return cur.astype(BF)]
    ppermute x30 -> x33, waiting for transfers between devices: 123 us -> 99 us  [send(): return lax.ppermute(value, ('dp', 'seq'), pairs)]
    select_n x14 -> x9, other arithmetic: 24.2 us -> 1.43 us  [the longest x3 0.86 us: finish(): jnp.where(self.side_b == 0, jnp.concatenate([cur, got]), jnp.concatenate(...]
    reduce_sum x8 -> x1, other arithmetic: 22.5 us -> 0.09 us  [local(): jnp.sum(jnp.where(seg[None, :, None] <= seg[None, None, :], counts[:, :,...]
    ppermute x3, waiting for transfers between devices: 29.7 us -> 10.9 us  [swap_seq(): return lax.ppermute(value, 'seq', [(0, 1), (1, 0)])]
  transfers between devices with their start and end apart: 33 -> 36, of which waited for: 18 -> 15; matrix products, arithmetic and copies ran while one was open for 16% -> 5% of each run, Pallas kernels for 0% -> 26%
where the time goes in v2:
time: 450 us; the launch traced here: 449 us
  Pallas kernels  228 us (51%)
  waiting for transfers between devices  110 us (24%)
  starting transfers between devices  80.5 us (18%)
  local copies, waits for them, and re-layouts  19.9 us (4%)
  other arithmetic  8.86 us (2%)
    ppermute x33, waiting for transfers between devices, send(): return lax.ppermute(value, ('dp', 'seq'), pairs)  99 us
    ppermute x33, starting transfers between devices, send(): return lax.ppermute(value, ('dp', 'seq'), pairs)  74.1 us
    pallas_call x1, Pallas kernels, run_attend_backward(): pl.pallas_call(attend_backward, grid_spec=pltpu.PrefetchScalarGridSpec(nu...  43 us
    pallas_call x3, Pallas kernels, assemble(): pl.pallas_call(functools.partial(assemble_body, steps, widths), grid_spec...  38.3 us
    pallas_call x1, Pallas kernels, run_attend_forward(): pl.pallas_call(attend_forward, grid_spec=pltpu.PrefetchScalarGridSpec(num...  38.2 us
    pallas_call x1, Pallas kernels, run_feed_forward(): pl.pallas_call(feed_forward, grid=(rows,), in_specs=[row_spec(length, D),...  27.9 us
    pallas_call x1, Pallas kernels, run_feed_backward(): pl.pallas_call(feed_backward, grid=(rows,), in_specs=[row_spec(length, D)...  24.8 us
    ppermute x3, waiting for transfers between devices, swap_seq(): return lax.ppermute(value, 'seq', [(0, 1), (1, 0)])  10.9 us
  transfers between devices with their start and end apart: 36, of which 15 were waited for; matrix products, arithmetic and copies ran while one was open for 5% of the time, Pallas kernels for 26%

profile of v2, /device:TPU:0, one launch (start us, length us, event | category | flops | bytes accessed | tf_op | source)
XLA Modules:
  0.0 448.7 jit_solution(14144358745804076316)
XLA Ops:
  0.8 1.3 constant_dynamic-slice_fusion.1
  2.0 3.0 collective-permute-start
  6.0 1.0 copy.54.idc_ref
  8.3 0.7 copy.56.cnt_ref
  12.5 0.7 dynamic-slice_bitcast_fusion.pg_ref
  13.2 9.5 %collective-permute-done = bf16[2,1,256,768]{3,2,0,1:T(8,128)(2,1)S(1)} collective-permute-done((bf16[2,1,256,768]{3,2,0,1:T(8,128)(2,1)S(1)}, bf16[2,1,256,768]{3,2,0,1:T(8,128)(2,1)S(1)}, u32[]{:S(2)}, u32[]{:S(2)}) %collective-permute-start) | collective-permute-done | bytes 786464 | tf_op jit(solution)/shard_map/ppermute | solution.py:621
  22.6 0.9 copy-done.12
  23.5 38.2 %attend_forward.1 = (bf16[2,512,2304]{2,1,0:T(8,128)(2,1)}, bf16[768,1024]{1,0:T(8,128)(2,1)}, bf16[768,1024]{1,0:T(8,128)(2,1)}, f32[2,48,512]{2,1,0:T(8,128)},...) custom-call(s32[1]{0:T(128)} %bitcast.at_ref, bf16[4,256,768]{2,1,0:T(8,128)(2,1)} %bitcast.40, ...), custom_call_target="tpu_custom_call" | custom-call | tf_op jit(solution)/shard_map/attend_forward/pallas_call | solution.py:103
  61.7 27.9 %feed_forward.1 = (bf16[768,1024]{1,0:T(8,128)(2,1)}, bf16[3072,1024]{1,0:T(8,128)(2,1)}, bf16[2,512,3072]{2,1,0:T(8,128)(2,1)}, f32[2,512,768]{2,1,0:T(8,128)},...) custom-call(f32[2,512,768]{2,1,0:T(8,128)} %get-tuple-element.53.xhat_ref, ...), custom_call_target="tpu_custom_call" | custom-call | tf_op jit(solution)/shard_map/feed_forward/pallas_call | solution.py:185
  89.6 24.8 %feed_backward.1 = (bf16[2,512,3072]{2,1,0:T(8,128)(2,1)}, f32[2,512,768]{2,1,0:T(8,128)}, bf16[2,512,768]{2,1,0:T(8,128)(2,1)}, f32[2,8,768]{2,1,0:T(8,128)}, f32[2,1,3072]{2,1,0:T(1,128)}) custom-call(bf16[2,512,768]{2,1,0:T(8,128)(2,1)} %get-tuple-element.55.gdl_ref, bf16[2,512,3072]{2,1,0:T(8,128)(2,1)} %get-tuple-element.56.slope_ref, ...), custom_call_target="tpu_custom_call" | custom-call | tf_op jit(solution)/shard_map/feed_backward/pallas_call | solution.py:236
  114.4 8.9 %up_send.1 = bf16[384,3840]{1,0:T(8,128)(2,1)} custom-call(s32[2]{0:T(128)} %pad_add_fusion.1.sides_ref, bf16[768,1024]{1,0:T(8,128)(2,1)} %get-tuple-element.77.mid_ref.mid_send_ref.mid_keep_ref, bf16[1024,3072]{1,0:T(8,128)(2,1)} %bitcast.31, bf16[768,1024]{1,0:T(8,128)(2,1)} %get-tuple-element.79.ctx_ref.ctx_send_ref.ctx_keep_ref, bf16[1024,768]{1,0:T(8,128)(2,1)} %bitcast.35), custom_call_target="tpu_custom_call" | custom-call | tf_op jit(solution)/shard_map/up_send/pallas_call | solution.py:385
  123.3 43.0 %attend_backward.1 = (bf16[2,512,2304]{2,1,0:T(8,128)(2,1)}, bf16[2,256,768]{2,1,0:T(8,128)(2,1)}, bf16[2,256,768]{2,1,0:T(8,128)(2,1)}, f32[2,1,2304]{2,1,0:T(1,128)}) custom-call(s32[1]{0:T(128)} %bitcast.at_ref, bf16[2,512,768]{2,1,0:T(8,128)(2,1)} %get-tuple-element.59.gal_ref, f32[2,512,768]{2,1,0:T(8,128)} %get-tuple-element.60.gh1_ref, ...), custom_call_target="tpu_custom_call" | custom-call | tf_op jit(solution)/shard_map/attend_backward/pallas_call | solution.py:303
  166.4 6.5 %tail_send.1 = bf16[384,2432]{1,0:T(8,128)(2,1)} custom-call(s32[2]{0:T(128)} %pad_add_fusion.1.sides_ref, bf16[768,1024]{1,0:T(8,128)(2,1)} %get-tuple-element.65.x_ref.x_send_ref.x_keep_ref, bf16[1024,2304]{1,0:T(8,128)(2,1)} %bitcast.33, f32[2,8,768]{2,1,0:T(8,128)} %get-tuple-element.67.sums1_ref, f32[2,8,768]{2,1,0:T(8,128)} %get-tuple-element.68.sums2_ref, ...), custom_call_target="tpu_custom_call" | custom-call | tf_op jit(solution)/shard_map/tail_send/pallas_call | solution.py:462
  173.4 6.9 %down_send.1 = bf16[1536,768]{1,0:T(8,128)(2,1)} custom-call(s32[2]{0:T(128)} %pad_add_fusion.1.sides_ref, bf16[3072,1024]{1,0:T(8,128)(2,1)} %get-tuple-element.86.left_ref.left_send_ref.left_keep_ref, bf16[1024,768]{1,0:T(8,128)(2,1)} %bitcast.37), custom_call_target="tpu_custom_call" | custom-call | tf_op jit(solution)/shard_map/down_send/pallas_call | solution.py:339
  180.4 1.6 copy-done.2
  182.0 10.2 %up_keep.1 = (bf16[192,3840]{1,0:T(8,128)(2,1)}, f32[192,3840]{1,0:T(8,128)}) custom-call(s32[2]{0:T(128)} %pad_add_fusion.1.sides_ref, bf16[768,1024]{1,0:T(8,128)(2,1)} %get-tuple-element.77.mid_ref.mid_send_ref.mid_keep_ref, bf16[768,1024]{1,0:T(8,128)(2,1)} %get-tuple-element.77.mid_ref.mid_send_ref.mid_keep_ref, bf16[1024,3072]{1,0:T(8,128)(2,1)} %bitcast.32, ...), custom_call_target="tpu_custom_call" | custom-call | tf_op jit(solution)/shard_map/up_keep/pallas_call | solution.py:421
  192.2 1.7 collective-permute-start.15
  193.9 7.3 %tail_keep.1 = (bf16[192,2432]{1,0:T(8,128)(2,1)}, f32[192,2432]{1,0:T(8,128)}) custom-call(s32[2]{0:T(128)} %pad_add_fusion.1.sides_ref, bf16[768,1024]{1,0:T(8,128)(2,1)} %get-tuple-element.65.x_ref.x_send_ref.x_keep_ref, bf16[768,1024]{1,0:T(8,128)(2,1)} %get-tuple-element.65.x_ref.x_send_ref.x_keep_ref, bf16[1024,2304]{1,0:T(8,128)(2,1)} %bitcast.34, ...), custom_call_target="tpu_custom_call" | custom-call | tf_op jit(solution)/shard_map/tail_keep/pallas_call | solution.py:491
  201.5 20.3 %collective-permute-done.4.got_away_ref.got_here_ref = bf16[192,2432]{1,0:T(8,128)(2,1)S(1)} collective-permute-done((bf16[192,2432]{1,0:T(8,128)(2,1)}, bf16[192,2432]{1,0:T(8,128)(2,1)S(1)}, u32[]{:S(2)}, u32[]{:S(2)}) %collective-permute-start.4) | collective-permute-done | bytes 933920 | tf_op jit(solution)/shard_map/ppermute | solution.py:590
  221.7 0.9 copy-done.8
  222.7 2.9 add_split.3
  225.6 1.7 collective-permute-start.5
  227.3 7.0 %down_keep.1 = (bf16[768,768]{1,0:T(8,128)(2,1)}, f32[768,768]{1,0:T(8,128)}) custom-call(s32[2]{0:T(128)} %pad_add_fusion.1.sides_ref, bf16[3072,1024]{1,0:T(8,128)(2,1)} %get-tuple-element.86.left_ref.left_send_ref.left_keep_ref, bf16[3072,1024]{1,0:T(8,128)(2,1)} %get-tuple-element.86.left_ref.left_send_ref.left_keep_ref, bf16[1024,768]{1,0:T(8,128)(2,1)} %bitcast.38, ...), custom_call_target="tpu_custom_call" | custom-call | tf_op jit(solution)/shard_map/down_keep/pallas_call | solution.py:359
  234.3 1.5 collective-permute-start.26
  235.8 1.1 copy-done.3
  236.9 3.3 add_split.4
  240.8 1.3 convert_add_fusion.2
  242.1 1.6 collective-permute-start.6
  243.7 13.4 %collective-permute-done.16 = bf16[96,3840]{1,0:T(8,128)(2,1)S(1)} collective-permute-done((bf16[96,3840]{1,0:T(8,128)(2,1)}, bf16[96,3840]{1,0:T(8,128)(2,1)S(1)}, u32[]{:S(2)}, u32[]{:S(2)}) %collective-permute-start.16) | collective-permute-done | bytes 737312 | tf_op jit(solution)/shard_map/ppermute | solution.py:590
  257.3 1.6 collective-permute-start.17
  259.6 2.6 collective-permute-start.7
  262.2 1.0 copy-done.5
  263.2 2.9 add_split.5
  266.2 1.5 collective-permute-start.27
  267.6 3.6 collective-permute-done.17
  271.3 1.8 collective-permute-start.18
  273.1 3.2 collective-permute-done.27
  276.9 6.1 %collective-permute-done.18 = bf16[24,3840]{1,0:T(8,128)(2,1)S(1)} collective-permute-done((bf16[24,3840]{1,0:T(8,128)(2,1)S(1)}, bf16[24,3840]{1,0:T(8,128)(2,1)S(1)}, u32[]{:S(2)}, u32[]{:S(2)}) %collective-permute-start.18) | collective-permute-done | bytes 184352 | tf_op jit(solution)/shard_map/ppermute | solution.py:590
  283.2 5.5 %collective-permute-done.28 = bf16[192,768]{1,0:T(8,128)(2,1)S(1)} collective-permute-done((bf16[192,768]{1,0:T(8,128)(2,1)S(1)}, bf16[192,768]{1,0:T(8,128)(2,1)S(1)}, u32[]{:S(2)}, u32[]{:S(2)}) %collective-permute-start.28) | collective-permute-done | bytes 294944 | tf_op jit(solution)/shard_map/ppermute | solution.py:590
  288.9 9.0 %collective-permute-done.19 = bf16[24,3840]{1,0:T(8,128)(2,1)S(1)} collective-permute-done((bf16[24,3840]{1,0:T(8,128)(2,1)S(1)}, bf16[24,3840]{1,0:T(8,128)(2,1)S(1)}, u32[]{:S(2)}, u32[]{:S(2)}) %collective-permute-start.19) | collective-permute-done | bytes 184352 | tf_op jit(solution)/shard_map/ppermute | solution.py:590
  298.1 1.9 collective-permute-start.8
  300.3 0.8 collective-permute-start.30
  301.2 12.6 %collective-permute-done.20 = bf16[48,3840]{1,0:T(8,128)(2,1)S(1)} collective-permute-done((bf16[48,3840]{1,0:T(8,128)(2,1)S(1)}, bf16[48,3840]{1,0:T(8,128)(2,1)S(1)}, u32[]{:S(2)}, u32[]{:S(2)}) %collective-permute-start.20) | collective-permute-done | bytes 368672 | tf_op jit(solution)/shard_map/ppermute | solution.py:590
  314.2 2.1 collective-permute-start.31
  316.3 6.4 %collective-permute-done.9 = bf16[48,2432]{1,0:T(8,128)(2,1)S(1)} collective-permute-done((bf16[48,2432]{1,0:T(8,128)(2,1)S(1)}, bf16[48,2432]{1,0:T(8,128)(2,1)S(1)}, u32[]{:S(2)}, u32[]{:S(2)}) %collective-permute-start.9) | collective-permute-done | bytes 233504 | tf_op jit(solution)/shard_map/ppermute | solution.py:590
  322.7 1.1 collective-permute-start.10
  323.8 4.4 collective-permute-done.31
  328.8 1.4 collective-permute-start.22
  330.2 2.0 collective-permute-start.1
  332.2 12.2 %collective-permute-done.32 = bf16[384,768]{1,0:T(8,128)(2,1)S(1)} collective-permute-done((bf16[384,768]{1,0:T(8,128)(2,1)S(1)}, bf16[384,768]{1,0:T(8,128)(2,1)S(1)}, u32[]{:S(2)}, u32[]{:S(2)}) %collective-permute-start.32) | collective-permute-done | bytes 589856 | tf_op jit(solution)/shard_map/ppermute | solution.py:590
  344.8 1.7 collective-permute-start.33
  347.2 1.4 collective-permute-start.2
  348.6 17.6 %collective-permute-start.12 = (bf16[192,2432]{1,0:T(8,128)(2,1)S(1)}, bf16[192,2432]{1,0:T(8,128)(2,1)S(1)}, u32[]{:S(2)}, u32[]{:S(2)}) collective-permute-start(bf16[192,2432]{1,0:T(8,128)(2,1)S(1)} %maximum_select_fusion.3.refs_0_), channel_id=1, source_target_pairs={{0,2},{1,3},{2,0},{3,1},{4,6},{5,7},{6,4},{7,5},{8,10},{9,11},{10,... | collective-permute-start | bytes 2801672 | tf_op jit(solution)/shard_map/ppermute | solution.py:590
  366.2 1.4 collective-permute-done.2
  367.6 30.1 %collective-permute-start.23 = (bf16[192,3840]{1,0:T(8,128)(2,1)S(1)}, bf16[192,3840]{1,0:T(8,128)(2,1)}, u32[]{:S(2)}, u32[]{:S(2)}) collective-permute-start(bf16[192,3840]{1,0:T(8,128)(2,1)S(1)} %maximum_select_fusion.1.refs_0_), channel_id=1, source_target_pairs={{0,2},{1,3},{2,0},{3,1},{4,6},{5,7},{6,4},{7,5},{8,10},{9,11},{10,... | collective-permute-start | bytes 4423688 | tf_op jit(solution)/shard_map/ppermute | solution.py:590
  398.3 0.8 copy-done.11
  399.8 0.8 fusion.1
  400.6 3.5 fusion
  404.1 2.0 collective-permute-done.13.refs_3_
  406.1 8.3 %assemble.3 = (f32[768,2304]{1,0:T(8,128)}, f32[768,128]{1,0:T(8,128)}) custom-call(s32[4]{0:T(128)} %pad_add_fusion.place_ref, bf16[192,2432]{1,0:T(8,128)(2,1)} %copy-done.7, bf16[192,2432]{1,0:T(8,128)(2,1)} %collective-permute-done.11.refs_1_, bf16[192,2432]{1,0:T(8,128)(2,1)} %copy-done.11, bf16[192,2432]{1,0:T(8,128)(2,1)} %collective-permute-done.13.refs_3_), custom_call_target="tpu_custom_call" | custom-call | tf_op jit(solution)/shard_map/assemble/pallas_call | solution.py:547
  414.4 1.0 slice_bitcast_fusion
  416.4 2.2 slice_reduce_fusion
  418.6 20.0 %assemble.5 = f32[3072,768]{1,0:T(8,128)} custom-call(s32[4]{0:T(128)} %pad_add_fusion.place_ref, bf16[768,768]{1,0:T(8,128)(2,1)} %copy-done.6, bf16[768,768]{1,0:T(8,128)(2,1)} %collective-permute-done.33.refs_1_, bf16[768,768]{1,0:T(8,128)(2,1)} %collective-permute-done.34.refs_2_, bf16[768,768]{1,0:T(8,128)(2,1)} %collective-permute-done.35.refs_3_), custom_call_target="tpu_custom_call" | custom-call | tf_op jit(solution)/shard_map/assemble/pallas_call | solution.py:547
  438.6 10.0 %assemble.4 = (f32[768,3072]{1,0:T(8,128)}, f32[768,768]{1,0:T(8,128)}) custom-call(s32[4]{0:T(128)} %pad_add_fusion.place_ref, bf16[192,3840]{1,0:T(8,128)(2,1)} %copy-done.4, bf16[192,3840]{1,0:T(8,128)(2,1)} %collective-permute-done.22.refs_1_, bf16[192,3840]{1,0:T(8,128)(2,1)} %collective-permute-done.23.refs_2_, ...), custom_call_target="tpu_custom_call" | custom-call | tf_op jit(solution)/shard_map/assemble/pallas_call | solution.py:547
  (126 shorter events, 13.8 us)
Async XLA Ops:
  0.6 11.8 %copy-start = (f32[4,1,32,768]{3,2,1,0:T(8,128)S(1)}, f32[4,1,32,768]{3,2,1,0:T(8,128)}, u32[]{:S(2)}) copy-start(f32[4,1,32,768]{3,2,1,0:T(8,128)} %param.19) | copy-start | bytes 1179652
  0.7 4.4 copy-start.23
  0.7 6.4 %copy-start.21 = (f32[768]{0:T(1024)S(1)}, f32[768]{0:T(1024)}, u32[]{:S(2)}) copy-start(f32[768]{0:T(1024)} %param.22) | copy-start | bytes 9220
  0.7 6.4 %copy-start.22 = (f32[768]{0:T(1024)S(1)}, f32[768]{0:T(1024)}, u32[]{:S(2)}) copy-start(f32[768]{0:T(1024)} %param.21) | copy-start | bytes 9220
  0.7 7.0 %copy-start.15 = (f32[768]{0:T(1024)S(1)}, f32[768]{0:T(1024)}, u32[]{:S(2)}) copy-start(f32[768]{0:T(1024)} %param.24) | copy-start | bytes 9220
  0.7 8.2 %copy-start.16 = (f32[768]{0:T(1024)S(1)}, f32[768]{0:T(1024)}, u32[]{:S(2)}) copy-start(f32[768]{0:T(1024)} %param.25) | copy-start | bytes 9220
  0.7 8.8 %copy-start.17 = (f32[768]{0:T(1024)S(1)}, f32[768]{0:T(1024)}, u32[]{:S(2)}) copy-start(f32[768]{0:T(1024)} %param.26) | copy-start | bytes 9220
  0.7 9.4 %copy-start.18 = (f32[768]{0:T(1024)S(1)}, f32[768]{0:T(1024)}, u32[]{:S(2)}) copy-start(f32[768]{0:T(1024)} %param.30) | copy-start | bytes 9220
  0.7 10.0 %copy-start.19 = (f32[768]{0:T(1024)S(1)}, f32[768]{0:T(1024)}, u32[]{:S(2)}) copy-start(f32[768]{0:T(1024)} %param.31) | copy-start | bytes 9220
  0.7 10.5 %copy-start.20 = (f32[768]{0:T(1024)S(1)}, f32[768]{0:T(1024)}, u32[]{:S(2)}) copy-start(f32[768]{0:T(1024)} %param.32) | copy-start | bytes 9220
  2.0 20.6 %collective-permute-start = (bf16[2,1,256,768]{3,2,0,1:T(8,128)(2,1)S(1)}, bf16[2,1,256,768]{3,2,0,1:T(8,128)(2,1)S(1)}, u32[]{:S(2)}, u32[]{:S(2)}) collective-permute-start(bf16[2,1,256,768]{3,2,0,1:T(8,128)(2,1)S(1)} %constant_dynamic-slice_fusion.1), channel_id=1, source_target_pairs={{0,1},{1,0},{2,3},{3,2},{4,5},{5,4},{6,7},{7,6},{8,9},{9,8},{10,11... | collective-permute-start | bytes 2359304 | tf_op jit(solution)/shard_map/ppermute | solution.py:621
  22.6 0.9 copy-start.12
  123.3 57.0 %collective-permute-start.14 = (bf16[384,3840]{1,0:T(8,128)(2,1)}, bf16[384,3840]{1,0:T(8,128)(2,1)S(1)}, u32[]{:S(2)}, u32[]{:S(2)}) collective-permute-start(bf16[384,3840]{1,0:T(8,128)(2,1)} %up_send.1), channel_id=1, source_target_pairs={{0,2},{1,3},{2,0},{3,1},{4,6},{5,7},{6,4},{7,5},{8,10},{9,11},{10,... | collective-permute-start | bytes 8847368 | tf_op jit(solution)/shard_map/ppermute | solution.py:590
  172.9 21.0 %collective-permute-start.3 = (bf16[384,2432]{1,0:T(8,128)(2,1)}, bf16[384,2432]{1,0:T(8,128)(2,1)}, u32[]{:S(2)}, u32[]{:S(2)}) collective-permute-start(bf16[384,2432]{1,0:T(8,128)(2,1)} %tail_send.1), channel_id=1, source_target_pairs={{0,2},{1,3},{2,0},{3,1},{4,6},{5,7},{6,4},{7,5},{8,10},{9,11},{10,... | collective-permute-start | bytes 5603336 | tf_op jit(solution)/shard_map/ppermute | solution.py:590
  180.3 47.0 %collective-permute-start.25 = (bf16[1536,768]{1,0:T(8,128)(2,1)}, bf16[1536,768]{1,0:T(8,128)(2,1)}, u32[]{:S(2)}, u32[]{:S(2)}) collective-permute-start(bf16[1536,768]{1,0:T(8,128)(2,1)} %down_send.1), channel_id=1, source_target_pairs={{0,2},{1,3},{2,0},{3,1},{4,6},{5,7},{6,4},{7,5},{8,10},{9,11},{10,... | collective-permute-start | bytes 7077896 | tf_op jit(solution)/shard_map/ppermute | solution.py:590
  180.4 1.6 copy-start.2
  192.2 43.7 %collective-permute-start.15 = (bf16[192,3840]{1,0:T(8,128)(2,1)}, bf16[192,3840]{1,0:T(8,128)(2,1)S(1)}, u32[]{:S(2)}, u32[]{:S(2)}) collective-permute-start(bf16[192,3840]{1,0:T(8,128)(2,1)} %get-tuple-element.81), channel_id=1, source_target_pairs={{0,4},{1,5},{2,3},{3,2},{4,0},{5,1},{6,7},{7,6},{8,12},{9,13},{10,... | collective-permute-start | bytes 4423688 | tf_op jit(solution)/shard_map/ppermute | solution.py:590
  201.1 20.6 %collective-permute-start.4 = (bf16[192,2432]{1,0:T(8,128)(2,1)}, bf16[192,2432]{1,0:T(8,128)(2,1)S(1)}, u32[]{:S(2)}, u32[]{:S(2)}) collective-permute-start(bf16[192,2432]{1,0:T(8,128)(2,1)} %get-tuple-element.72), channel_id=1, source_target_pairs={{0,4},{1,5},{2,3},{3,2},{4,0},{5,1},{6,7},{7,6},{8,12},{9,13},{10,... | collective-permute-start | bytes 2801672 | tf_op jit(solution)/shard_map/ppermute | solution.py:590
  221.7 0.9 copy-start.8
  225.6 15.2 %collective-permute-start.5 = (bf16[96,2432]{1,0:T(8,128)(2,1)}, bf16[96,2432]{1,0:T(8,128)(2,1)S(1)}, u32[]{:S(2)}, u32[]{:S(2)}) collective-permute-start(bf16[96,2432]{1,0:T(8,128)(2,1)} %get-tuple-element.74), channel_id=1, source_target_pairs={{0,1},{1,0},{2,6},{3,7},{4,5},{5,4},{6,2},{7,3},{8,9},{9,8},{10,14... | collective-permute-start | bytes 1400840 | tf_op jit(solution)/shard_map/ppermute | solution.py:590
  234.3 27.9 %collective-permute-start.26 = (bf16[768,768]{1,0:T(8,128)(2,1)}, bf16[768,768]{1,0:T(8,128)(2,1)S(1)}, u32[]{:S(2)}, u32[]{:S(2)}) collective-permute-start(bf16[768,768]{1,0:T(8,128)(2,1)} %get-tuple-element.88), channel_id=1, source_target_pairs={{0,4},{1,5},{2,3},{3,2},{4,0},{5,1},{6,7},{7,6},{8,12},{9,13},{10,... | collective-permute-start | bytes 3538952 | tf_op jit(solution)/shard_map/ppermute | solution.py:590
  235.8 1.1 copy-start.3
  240.2 16.8 %copy-start.9 = (f32[96,3840]{1,0:T(8,128)S(1)}, f32[96,3840]{1,0:T(8,128)}, u32[]{:S(2)}) copy-start(f32[96,3840]{1,0:T(8,128)} %get-tuple-element.82) | copy-start | bytes 4423684
  240.2 16.8 %collective-permute-start.16 = (bf16[96,3840]{1,0:T(8,128)(2,1)}, bf16[96,3840]{1,0:T(8,128)(2,1)S(1)}, u32[]{:S(2)}, u32[]{:S(2)}) collective-permute-start(bf16[96,3840]{1,0:T(8,128)(2,1)} %get-tuple-element.83), channel_id=1, source_target_pairs={{0,1},{1,0},{2,6},{3,7},{4,5},{5,4},{6,2},{7,3},{8,9},{9,8},{10,14... | collective-permute-start | bytes 2211848 | tf_op jit(solution)/shard_map/ppermute | solution.py:590
  242.1 16.8 %collective-permute-start.6 = (bf16[48,2432]{1,0:T(8,128)(2,1)S(1)}, bf16[48,2432]{1,0:T(8,128)(2,1)S(1)}, u32[]{:S(2)}, u32[]{:S(2)}) collective-permute-start(bf16[48,2432]{1,0:T(8,128)(2,1)S(1)} %dynamic-slice_convert_fusion.2), channel_id=1, source_target_pairs={{0,8},{1,9},{2,10},{3,11},{4,12},{5,13},{6,14},{7,15},{8,0},{9,1},... | collective-permute-start | bytes 700424 | tf_op jit(solution)/shard_map/ppermute | solution.py:590
  257.3 13.9 %collective-permute-start.17 = (bf16[48,3840]{1,0:T(8,128)(2,1)S(1)}, bf16[48,3840]{1,0:T(8,128)(2,1)S(1)}, u32[]{:S(2)}, u32[]{:S(2)}) collective-permute-start(bf16[48,3840]{1,0:T(8,128)(2,1)S(1)} %dynamic-slice_convert_fusion), channel_id=1, source_target_pairs={{0,8},{1,9},{2,10},{3,11},{4,12},{5,13},{6,14},{7,15},{8,0},{9,1},... | collective-permute-start | bytes 1105928 | tf_op jit(solution)/shard_map/ppermute | solution.py:590
  259.6 38.4 %collective-permute-start.7 = (bf16[24,2432]{1,0:T(8,128)(2,1)}, bf16[24,2432]{1,0:T(8,128)(2,1)S(1)}, u32[]{:S(2)}, u32[]{:S(2)}) collective-permute-start(bf16[24,2432]{1,0:T(8,128)(2,1)} %dynamic-slice_convert_fusion.5), channel_id=1, source_target_pairs={{0,16},{1,17},{2,18},{3,19},{4,20},{5,21},{6,22},{7,23},{8,24},{9,... | collective-permute-start | bytes 350216 | tf_op jit(solution)/shard_map/ppermute | solution.py:590
  262.2 1.0 copy-start.5
  266.2 10.1 %copy-start.10 = (f32[384,768]{1,0:T(8,128)S(1)}, f32[384,768]{1,0:T(8,128)}, u32[]{:S(2)}) copy-start(f32[384,768]{1,0:T(8,128)} %get-tuple-element.89) | copy-start | bytes 3538948
  266.2 10.1 %collective-permute-start.27 = (bf16[384,768]{1,0:T(8,128)(2,1)}, bf16[384,768]{1,0:T(8,128)(2,1)S(1)}, u32[]{:S(2)}, u32[]{:S(2)}) collective-permute-start(bf16[384,768]{1,0:T(8,128)(2,1)} %get-tuple-element.90), channel_id=1, source_target_pairs={{0,1},{1,0},{2,6},{3,7},{4,5},{5,4},{6,2},{7,3},{8,9},{9,8},{10,14... | collective-permute-start | bytes 1769480 | tf_op jit(solution)/shard_map/ppermute | solution.py:590
  271.3 11.8 %collective-permute-start.18 = (bf16[24,3840]{1,0:T(8,128)(2,1)S(1)}, bf16[24,3840]{1,0:T(8,128)(2,1)S(1)}, u32[]{:S(2)}, u32[]{:S(2)}) collective-permute-start(bf16[24,3840]{1,0:T(8,128)(2,1)S(1)} %dynamic-slice_convert_fusion.3), channel_id=1, source_target_pairs={{0,16},{1,17},{2,18},{3,19},{4,20},{5,21},{6,22},{7,23},{8,24},{9,... | collective-permute-start | bytes 552968 | tf_op jit(solution)/shard_map/ppermute | solution.py:590
  276.4 12.3 %collective-permute-start.28 = (bf16[192,768]{1,0:T(8,128)(2,1)S(1)}, bf16[192,768]{1,0:T(8,128)(2,1)S(1)}, u32[]{:S(2)}, u32[]{:S(2)}) collective-permute-start(bf16[192,768]{1,0:T(8,128)(2,1)S(1)} %dynamic-slice_convert_fusion.1), channel_id=1, source_target_pairs={{0,8},{1,9},{2,10},{3,11},{4,12},{5,13},{6,14},{7,15},{8,0},{9,1},... | collective-permute-start | bytes 884744 | tf_op jit(solution)/shard_map/ppermute | solution.py:590
  283.1 14.8 %collective-permute-start.19 = (bf16[24,3840]{1,0:T(8,128)(2,1)S(1)}, bf16[24,3840]{1,0:T(8,128)(2,1)S(1)}, u32[]{:S(2)}, u32[]{:S(2)}) collective-permute-start(bf16[24,3840]{1,0:T(8,128)(2,1)S(1)} %add_convert_fusion), channel_id=1, source_target_pairs={{0,16},{1,17},{2,18},{3,19},{4,20},{5,21},{6,22},{7,23},{8,24},{9,... | collective-permute-start | bytes 552968 | tf_op jit(solution)/shard_map/ppermute | solution.py:590
  288.8 11.5 %collective-permute-start.29 = (bf16[96,768]{1,0:T(8,128)(2,1)S(1)}, bf16[96,768]{1,0:T(8,128)(2,1)S(1)}, u32[]{:S(2)}, u32[]{:S(2)}) collective-permute-start(bf16[96,768]{1,0:T(8,128)(2,1)S(1)} %dynamic-slice_convert_fusion.4), channel_id=1, source_target_pairs={{0,16},{1,17},{2,18},{3,19},{4,20},{5,21},{6,22},{7,23},{8,24},{9,... | collective-permute-start | bytes 442376 | tf_op jit(solution)/shard_map/ppermute | solution.py:590
  298.0 15.8 %collective-permute-start.20 = (bf16[48,3840]{1,0:T(8,128)(2,1)S(1)}, bf16[48,3840]{1,0:T(8,128)(2,1)S(1)}, u32[]{:S(2)}, u32[]{:S(2)}) collective-permute-start(bf16[48,3840]{1,0:T(8,128)(2,1)S(1)} %maximum_select_fusion.8), channel_id=1, source_target_pairs={{0,8},{1,9},{2,10},{3,11},{4,12},{5,13},{6,14},{7,15},{8,0},{9,1},... | collective-permute-start | bytes 1105928 | tf_op jit(solution)/shard_map/ppermute | solution.py:590
  298.1 15.9 %collective-permute-start.8 = (bf16[24,2432]{1,0:T(8,128)(2,1)S(1)}, bf16[24,2432]{1,0:T(8,128)(2,1)S(1)}, u32[]{:S(2)}, u32[]{:S(2)}) collective-permute-start(bf16[24,2432]{1,0:T(8,128)(2,1)S(1)} %add_convert_fusion.2), channel_id=1, source_target_pairs={{0,16},{1,17},{2,18},{3,19},{4,20},{5,21},{6,22},{7,23},{8,24},{9,... | collective-permute-start | bytes 350216 | tf_op jit(solution)/shard_map/ppermute | solution.py:590
  300.3 13.8 %collective-permute-start.30 = (bf16[96,768]{1,0:T(8,128)(2,1)S(1)}, bf16[96,768]{1,0:T(8,128)(2,1)S(1)}, u32[]{:S(2)}, u32[]{:S(2)}) collective-permute-start(bf16[96,768]{1,0:T(8,128)(2,1)S(1)} %add_convert_fusion.1), channel_id=1, source_target_pairs={{0,16},{1,17},{2,18},{3,19},{4,20},{5,21},{6,22},{7,23},{8,24},{9,... | collective-permute-start | bytes 442376 | tf_op jit(solution)/shard_map/ppermute | solution.py:590
  313.9 14.6 %collective-permute-start.21 = (bf16[96,3840]{1,0:T(8,128)(2,1)S(1)}, bf16[96,3840]{1,0:T(8,128)(2,1)S(1)}, u32[]{:S(2)}, u32[]{:S(2)}) collective-permute-start(bf16[96,3840]{1,0:T(8,128)(2,1)S(1)} %maximum_select_fusion.4), channel_id=1, source_target_pairs={{0,1},{1,0},{2,6},{3,7},{4,5},{5,4},{6,2},{7,3},{8,9},{9,8},{10,14... | collective-permute-start | bytes 2211848 | tf_op jit(solution)/shard_map/ppermute | solution.py:590
  314.0 8.6 %collective-permute-start.9 = (bf16[48,2432]{1,0:T(8,128)(2,1)S(1)}, bf16[48,2432]{1,0:T(8,128)(2,1)S(1)}, u32[]{:S(2)}, u32[]{:S(2)}) collective-permute-start(bf16[48,2432]{1,0:T(8,128)(2,1)S(1)} %maximum_select_fusion.10), channel_id=1, source_target_pairs={{0,8},{1,9},{2,10},{3,11},{4,12},{5,13},{6,14},{7,15},{8,0},{9,1},... | collective-permute-start | bytes 700424 | tf_op jit(solution)/shard_map/ppermute | solution.py:590
  314.2 14.0 %collective-permute-start.31 = (bf16[192,768]{1,0:T(8,128)(2,1)S(1)}, bf16[192,768]{1,0:T(8,128)(2,1)S(1)}, u32[]{:S(2)}, u32[]{:S(2)}) collective-permute-start(bf16[192,768]{1,0:T(8,128)(2,1)S(1)} %maximum_select_fusion.9), channel_id=1, source_target_pairs={{0,8},{1,9},{2,10},{3,11},{4,12},{5,13},{6,14},{7,15},{8,0},{9,1},... | collective-permute-start | bytes 884744 | tf_op jit(solution)/shard_map/ppermute | solution.py:590
  322.7 23.8 %collective-permute-start.10 = (bf16[96,2432]{1,0:T(8,128)(2,1)S(1)}, bf16[96,2432]{1,0:T(8,128)(2,1)S(1)}, u32[]{:S(2)}, u32[]{:S(2)}) collective-permute-start(bf16[96,2432]{1,0:T(8,128)(2,1)S(1)} %maximum_select_fusion.6), channel_id=1, source_target_pairs={{0,1},{1,0},{2,6},{3,7},{4,5},{5,4},{6,2},{7,3},{8,9},{9,8},{10,14... | collective-permute-start | bytes 1400840 | tf_op jit(solution)/shard_map/ppermute | solution.py:590
  328.4 1.8 copy-start.14
  328.4 15.9 %collective-permute-start.32 = (bf16[384,768]{1,0:T(8,128)(2,1)S(1)}, bf16[384,768]{1,0:T(8,128)(2,1)S(1)}, u32[]{:S(2)}, u32[]{:S(2)}) collective-permute-start(bf16[384,768]{1,0:T(8,128)(2,1)S(1)} %maximum_select_fusion.5), channel_id=1, source_target_pairs={{0,1},{1,0},{2,6},{3,7},{4,5},{5,4},{6,2},{7,3},{8,9},{9,8},{10,14... | collective-permute-start | bytes 1769480 | tf_op jit(solution)/shard_map/ppermute | solution.py:590
  328.8 38.9 %copy-start.4 = (bf16[192,3840]{1,0:T(8,128)(2,1)}, bf16[192,3840]{1,0:T(8,128)(2,1)S(1)}, u32[]{:S(2)}) copy-start(bf16[192,3840]{1,0:T(8,128)(2,1)S(1)} %maximum_select_fusion.1.refs_0_) | copy-start | bytes 4423684
  328.8 68.9 %collective-permute-start.22 = (bf16[192,3840]{1,0:T(8,128)(2,1)S(1)}, bf16[192,3840]{1,0:T(8,128)(2,1)}, u32[]{:S(2)}, u32[]{:S(2)}) collective-permute-start(bf16[192,3840]{1,0:T(8,128)(2,1)S(1)} %maximum_select_fusion.1.refs_0_), channel_id=1, source_target_pairs={{0,4},{1,5},{2,3},{3,2},{4,0},{5,1},{6,7},{7,6},{8,12},{9,13},{10,... | collective-permute-start | bytes 4423688 | tf_op jit(solution)/shard_map/ppermute | solution.py:590
  330.2 17.0 %copy-start.24 = (bf16[2,256,768]{2,1,0:T(8,128)(2,1)S(1)}, bf16[2,256,768]{2,1,0:T(8,128)(2,1)}, u32[]{:S(2)}) copy-start(bf16[2,256,768]{2,1,0:T(8,128)(2,1)} %get-tuple-element.64) | copy-start | bytes 2359300
  330.2 18.4 %collective-permute-start.1 = (f32[2,1,32,768]{3,2,0,1:T(8,128)S(1)}, f32[2,1,32,768]{3,2,0,1:T(8,128)S(1)}, u32[]{:S(2)}, u32[]{:S(2)}) collective-permute-start(f32[2,1,32,768]{3,2,0,1:T(8,128)S(1)} %bitcast.43), channel_id=1, source_target_pairs={{0,1},{1,0},{2,3},{3,2},{4,5},{5,4},{6,7},{7,6},{8,9},{9,8},{10,11... | collective-permute-start | bytes 589832 | tf_op jit(solution)/shard_map/ppermute | solution.py:621
  344.8 59.3 %copy-start.6 = (bf16[768,768]{1,0:T(8,128)(2,1)}, bf16[768,768]{1,0:T(8,128)(2,1)S(1)}, u32[]{:S(2)}) copy-start(bf16[768,768]{1,0:T(8,128)(2,1)S(1)} %maximum_select_fusion.2.refs_0_) | copy-start | bytes 3538948
  344.8 53.5 %collective-permute-start.33 = (bf16[768,768]{1,0:T(8,128)(2,1)S(1)}, bf16[768,768]{1,0:T(8,128)(2,1)}, u32[]{:S(2)}, u32[]{:S(2)}) collective-permute-start(bf16[768,768]{1,0:T(8,128)(2,1)S(1)} %maximum_select_fusion.2.refs_0_), channel_id=1, source_target_pairs={{0,4},{1,5},{2,3},{3,2},{4,0},{5,1},{6,7},{7,6},{8,12},{9,13},{10,... | collective-permute-start | bytes 3538952 | tf_op jit(solution)/shard_map/ppermute | solution.py:590
  346.7 51.6 %copy-start.7 = (bf16[192,2432]{1,0:T(8,128)(2,1)}, bf16[192,2432]{1,0:T(8,128)(2,1)S(1)}, u32[]{:S(2)}) copy-start(bf16[192,2432]{1,0:T(8,128)(2,1)S(1)} %maximum_select_fusion.3.refs_0_) | copy-start | bytes 2801668
  346.7 51.1 %collective-permute-start.11 = (bf16[192,2432]{1,0:T(8,128)(2,1)S(1)}, bf16[192,2432]{1,0:T(8,128)(2,1)}, u32[]{:S(2)}, u32[]{:S(2)}) collective-permute-start(bf16[192,2432]{1,0:T(8,128)(2,1)S(1)} %maximum_select_fusion.3.refs_0_), channel_id=1, source_target_pairs={{0,4},{1,5},{2,3},{3,2},{4,0},{5,1},{6,7},{7,6},{8,12},{9,13},{10,... | collective-permute-start | bytes 2801672 | tf_op jit(solution)/shard_map/ppermute | solution.py:590
  347.2 20.5 %collective-permute-start.2 = (bf16[2,1,256,768]{3,2,0,1:T(8,128)(2,1)S(1)}, bf16[2,1,256,768]{3,2,0,1:T(8,128)(2,1)S(1)}, u32[]{:S(2)}, u32[]{:S(2)}) collective-permute-start(bf16[2,1,256,768]{3,2,0,1:T(8,128)(2,1)S(1)} %bitcast.50), channel_id=1, source_target_pairs={{0,1},{1,0},{2,3},{3,2},{4,5},{5,4},{6,7},{7,6},{8,9},{9,8},{10,11... | collective-permute-start | bytes 2359304 | tf_op jit(solution)/shard_map/ppermute | solution.py:621
  348.6 49.7 %collective-permute-start.12 = (bf16[192,2432]{1,0:T(8,128)(2,1)S(1)}, bf16[192,2432]{1,0:T(8,128)(2,1)S(1)}, u32[]{:S(2)}, u32[]{:S(2)}) collective-permute-start(bf16[192,2432]{1,0:T(8,128)(2,1)S(1)} %maximum_select_fusion.3.refs_0_), channel_id=1, source_target_pairs={{0,2},{1,3},{2,0},{3,1},{4,6},{5,7},{6,4},{7,5},{8,10},{9,11},{10,... | collective-permute-start | bytes 2801672 | tf_op jit(solution)/shard_map/ppermute | solution.py:590
  367.6 30.7 %copy-start.13 = (bf16[2,1,256,768]{3,2,0,1:T(8,128)(2,1)}, bf16[2,1,256,768]{3,2,0,1:T(8,128)(2,1)S(1)}, u32[]{:S(2)}) copy-start(bf16[2,1,256,768]{3,2,0,1:T(8,128)(2,1)S(1)} %collective-permute-done.2) | copy-start | bytes 2359300
  367.6 71.0 %collective-permute-start.23 = (bf16[192,3840]{1,0:T(8,128)(2,1)S(1)}, bf16[192,3840]{1,0:T(8,128)(2,1)}, u32[]{:S(2)}, u32[]{:S(2)}) collective-permute-start(bf16[192,3840]{1,0:T(8,128)(2,1)S(1)} %maximum_select_fusion.1.refs_0_), channel_id=1, source_target_pairs={{0,2},{1,3},{2,0},{3,1},{4,6},{5,7},{6,4},{7,5},{8,10},{9,11},{10,... | collective-permute-start | bytes 4423688 | tf_op jit(solution)/shard_map/ppermute | solution.py:590
  397.7 40.9 %collective-permute-start.24 = (bf16[192,3840]{1,0:T(8,128)(2,1)}, bf16[192,3840]{1,0:T(8,128)(2,1)}, u32[]{:S(2)}, u32[]{:S(2)}) collective-permute-start(bf16[192,3840]{1,0:T(8,128)(2,1)} %collective-permute-done.22.refs_1_), channel_id=1, source_target_pairs={{0,2},{1,3},{2,0},{3,1},{4,6},{5,7},{6,4},{7,5},{8,10},{9,11},{10,... | collective-permute-start | bytes 4423688 | tf_op jit(solution)/shard_map/ppermute | solution.py:590
  397.8 8.3 %collective-permute-start.13 = (bf16[192,2432]{1,0:T(8,128)(2,1)}, bf16[192,2432]{1,0:T(8,128)(2,1)}, u32[]{:S(2)}, u32[]{:S(2)}) collective-permute-start(bf16[192,2432]{1,0:T(8,128)(2,1)} %collective-permute-done.11.refs_1_), channel_id=1, source_target_pairs={{0,2},{1,3},{2,0},{3,1},{4,6},{5,7},{6,4},{7,5},{8,10},{9,11},{10,... | collective-permute-start | bytes 2801672 | tf_op jit(solution)/shard_map/ppermute | solution.py:590
  398.2 0.9 copy-start.11
  398.2 20.3 %collective-permute-start.34 = (bf16[768,768]{1,0:T(8,128)(2,1)S(1)}, bf16[768,768]{1,0:T(8,128)(2,1)}, u32[]{:S(2)}, u32[]{:S(2)}) collective-permute-start(bf16[768,768]{1,0:T(8,128)(2,1)S(1)} %maximum_select_fusion.2.refs_0_), channel_id=1, source_target_pairs={{0,2},{1,3},{2,0},{3,1},{4,6},{5,7},{6,4},{7,5},{8,10},{9,11},{10,... | collective-permute-start | bytes 3538952 | tf_op jit(solution)/shard_map/ppermute | solution.py:590
  399.2 19.4 %collective-permute-start.35 = (bf16[768,768]{1,0:T(8,128)(2,1)}, bf16[768,768]{1,0:T(8,128)(2,1)}, u32[]{:S(2)}, u32[]{:S(2)}) collective-permute-start(bf16[768,768]{1,0:T(8,128)(2,1)} %collective-permute-done.33.refs_1_), channel_id=1, source_target_pairs={{0,2},{1,3},{2,0},{3,1},{4,6},{5,7},{6,4},{7,5},{8,10},{9,11},{10,... | collective-permute-start | bytes 3538952 | tf_op jit(solution)/shard_map/ppermute | solution.py:590
  418.6 30.1 %copy-start.1 = (f32[4,1,32,768]{3,2,1,0:T(8,128)S(1)}, f32[4,1,32,768]{3,2,1,0:T(8,128)}, u32[]{:S(2)}) copy-start(f32[4,1,32,768]{3,2,1,0:T(8,128)} %param.19) | copy-start | bytes 1179652

commit v3 on v2

v3 whole, which is shorter than its diff:
```python
import functools

import jax
import jax.numpy as jnp
from jax import lax
from jax.experimental import pallas as pl
from jax.experimental.pallas import tpu as pltpu
from jax.sharding import PartitionSpec as P

D = 768
HEADS = 12
HEAD_DIM = 64
FF = 3072
SEGS = 32
NORM_EPS = 1e-05
MASK_FILL = -1e30
BF = jnp.bfloat16
F32 = jnp.float32
PAIR = 2 * HEAD_DIM
STRIP = 512
CHUNK = 1024
STAT_ROWS = 4 * HEADS

NN = (((1,), (0,)), ((), ()))
NT = (((1,), (1,)), ((), ()))
TN = (((0,), (0,)), ((), ()))


def mm(left, right, dims=NN):
    return lax.dot_general(left, right, dims, preferred_element_type=F32)


def whole(shape):
    zeros = (0,) * len(shape)
    return pl.BlockSpec(shape, lambda *_: zeros, pipeline_mode=pl.Buffered(1))


def params(mib=60):
    return pltpu.CompilerParams(vmem_limit_bytes=mib * 1024 * 1024)


def far(shape, dtype):
    return pltpu.HBM(shape, dtype)


def from_far(value):
    return pltpu.with_memory_space_constraint(value, pltpu.HBM)


def busy(micros):
    return pl.CostEstimate(flops=int(micros * 1e6), bytes_accessed=0, transcendentals=0)


def row_mean(value):
    return jnp.sum(value, axis=-1, keepdims=True) * (1.0 / D)


def attend_forward(at_ref, own_ref, got_ref, idc_ref, idr_ref, wqkv_ref, bqkv_ref, wo_ref, bo_ref, qkv_ref, xt_ref, ctxt_ref, lse_ref, xhat_ref, inv_ref, x_ref, ctx_ref, mask_ref, stat_ref):
    length = x_ref.shape[0]
    half = length // 2
    x_ref[pl.ds(pl.multiple_of(at_ref[0] * half, half), half), :] = own_ref[...]
    x_ref[pl.ds(pl.multiple_of((1 - at_ref[0]) * half, half), half), :] = got_ref[...]
    xt_ref[...] = jnp.transpose(x_ref[...])
    for c in range(3):
        cols = pl.ds(c * D, D)
        part = mm(x_ref[...], wqkv_ref[:, cols]) + bqkv_ref[:, cols]
        part = part.astype(BF)
        if c == 0:
            part = part * BF(HEAD_DIM**-0.5)
        qkv_ref[:, cols] = part
    mask_ref[...] = jnp.where(idc_ref[...] == idr_ref[...], 0.0, MASK_FILL)
    low = lax.broadcasted_iota(jnp.int32, (length, PAIR), 1) < HEAD_DIM
    low_strip = lax.broadcasted_iota(jnp.int32, (STRIP, PAIR), 1) < HEAD_DIM
    lane = lax.broadcasted_iota(jnp.int32, (STRIP, 128), 1)
    stat_ref[...] = jnp.zeros_like(stat_ref)

    def pair_step(p, carry):
        at = pl.multiple_of(p * PAIR, PAIR)
        keys = qkv_ref[:, pl.ds(D + at, PAIR)]
        values = qkv_ref[:, pl.ds(2 * D + at, PAIR)]
        value_of = [jnp.where(low, values, BF(0)), jnp.where(low, BF(0), values)]
        for s in range(length // STRIP):
            rows = pl.ds(s * STRIP, STRIP)
            queries = qkv_ref[rows, pl.ds(at, PAIR)]
            outs = []
            stats = stat_ref[rows, :]
            for h in range(2):
                query = jnp.where(low_strip, queries, BF(0)) if h == 0 else jnp.where(low_strip, BF(0), queries)
                scores = mm(query, keys, NT) + mask_ref[rows, :]
                top = jnp.max(scores, axis=-1, keepdims=True)
                exps = jnp.exp(scores - top)
                total = jnp.sum(exps, axis=-1, keepdims=True)
                outs.append(mm(exps.astype(BF), value_of[h]) * (1.0 / total))
                stats = jnp.where(lane == 8 * p + h, top + jnp.log(total), stats)
            ctx_ref[rows, pl.ds(at, PAIR)] = (outs[0] + outs[1]).astype(BF)
            stat_ref[rows, :] = stats
        return carry

    lax.fori_loop(0, HEADS // 2, pair_step, 0)
    lse_ref[...] = jnp.transpose(stat_ref[...])[: lse_ref.shape[0], :]
    ctxt_ref[...] = jnp.transpose(ctx_ref[...])
    total_in = mm(ctx_ref[...], wo_ref[...]) + bo_ref[...] + x_ref[...].astype(F32)
    centered = total_in - row_mean(total_in)
    inv = lax.rsqrt(row_mean(centered * centered) + NORM_EPS)
    xhat_ref[...] = centered * inv
    inv_ref[...] = jnp.broadcast_to(inv, inv_ref.shape)


def run_attend_forward(at, hidden, got, ids, wqkv, bqkv, wo, bo):
    rows, half, _ = got.shape
    length = 2 * half
    row_spec = lambda *tail: pl.BlockSpec((None,) + tail, lambda r, at: (r,) + (0,) * len(tail))
    turned = pl.BlockSpec((D, length), lambda r, at: (0, r))
    return pl.pallas_call(
        attend_forward,
        grid_spec=pltpu.PrefetchScalarGridSpec(
            num_scalar_prefetch=1,
            grid=(rows,),
            in_specs=[
                pl.BlockSpec((None, half, D), lambda r, at: (at[0] * rows + r, 0, 0)),
                row_spec(half, D), row_spec(length, 1), row_spec(1, length), whole((D, 3 * D)), whole((1, 3 * D)), whole((D, D)), whole((1, D))],
            out_specs=[row_spec(length, 3 * D), turned, turned, row_spec(STAT_ROWS, length), row_spec(length, D), row_spec(length, 128)],
            scratch_shapes=[pltpu.VMEM((length, D), BF), pltpu.VMEM((length, D), BF), pltpu.VMEM((length, length), F32), pltpu.VMEM((length, 128), F32)],
        ),
        out_shape=[
            far((rows, length, 3 * D), BF),
            far((D, rows * length), BF),
            far((D, rows * length), BF),
            far((rows, STAT_ROWS, length), F32),
            jax.ShapeDtypeStruct((rows, length, D), F32),
            jax.ShapeDtypeStruct((rows, length, 128), F32),
        ],
        compiler_params=params(26),
        cost_estimate=busy(38),
        name="attend_forward",
    )(at, hidden, got, ids[:, :, None], ids[:, None, :], wqkv, bqkv[None], wo, bo[None])


def gelu_parts(value):
    cdf = 0.5 * (1.0 + lax.erf(value * (0.5**0.5)))
    density = jnp.exp(-0.5 * value * value) * 0.3989422804014327
    return cdf, cdf + value * density


def split_terms(value, count):
    parts = []
    for _ in range(count):
        part = value.astype(BF)
        parts.append(part)
        value = value - part.astype(F32)
    return parts


def feed_both(sides_ref, xhat_ref, inv_ref, idc_ref, idr_ref, cnt_ref, pg_ref, ctxt_ref, g1_ref, s1_ref, upb_ref, downb_ref, g2_ref, s2_ref, up_ref, down_ref,
              send_down_ref, keep_down_ref, send_up_ref, keep_up_ref, gh1_ref, gal_ref, pooled_ref, sums1_ref, sums2_ref, ups_ref,
              mid_ref, act_ref, slope_ref, gdl_ref, acc_ref):
    rows, length, _ = xhat_ref.shape
    chunks = FF // D
    half = D // 2
    step = pl.program_id(0)
    core = sides_ref[0]

    @pl.when(step == 0)
    def _():
        for r in range(rows):
            at = pl.ds(r * length, length)
            mid = xhat_ref[r] * g1_ref[...] + s1_ref[...]
            mid_ref[at, :] = mid.astype(BF)
            acc_ref[at, :] = mid + downb_ref[...]

    @pl.when(step < chunks)
    def _():
        cols = pl.ds(pl.multiple_of(step * D, D), D)
        for r in range(rows):
            at = pl.ds(r * length, length)
            pre = mm(mid_ref[at, :], up_ref[...]) + upb_ref[:, cols]
            cdf, slope = gelu_parts(pre)
            act = (pre * cdf).astype(BF)
            act_ref[at, cols] = act
            slope_ref[at, cols] = slope.astype(BF)
            acc_ref[at, :] += mm(act, down_ref[...])

    @pl.when(step == chunks - 1)
    def _():
        def one_row(r, carry):
            at = pl.ds(pl.multiple_of(r * length, length), length)
            total_in = acc_ref[at, :]
            centered = total_in - row_mean(total_in)
            inv = lax.rsqrt(row_mean(centered * centered) + NORM_EPS)
            normed = centered * inv
            final = normed * g2_ref[...] + s2_ref[...]
            member = (lax.broadcasted_iota(jnp.int32, (SEGS, length), 0) == idr_ref[r]).astype(BF)
            pooled_ref[r] = sum(mm(member, part) for part in split_terms(final, 3)) / cnt_ref[r]
            spread = (lax.broadcasted_iota(jnp.int32, (length, SEGS), 1) == idc_ref[r]).astype(BF)
            grad_final = sum(mm(spread, part) for part in split_terms(pg_ref[r] / cnt_ref[r], 3))
            scaled = grad_final * g2_ref[...]
            grad_h2 = inv * (scaled - row_mean(scaled) - normed * row_mean(scaled * normed))
            acc_ref[at, :] = grad_h2
            low = grad_h2.astype(BF)
            gdl_ref[at, :] = low
            sums2_ref[r, 0:1, :] = jnp.sum(grad_final * normed, axis=0, keepdims=True)
            sums2_ref[r, 1:2, :] = jnp.sum(grad_final, axis=0, keepdims=True)
            sums2_ref[r, 2:3, :] = jnp.sum(low.astype(F32), axis=0, keepdims=True)
            return carry

        lax.fori_loop(0, rows, one_row, 0)

    away = pl.ds(pl.multiple_of((1 - core) * half, half), half)
    here = pl.ds(pl.multiple_of(core * half, half), half)

    @pl.when((step >= chunks) & (step < 2 * chunks))
    def _():
        chunk = chunk_of(step, core, chunks)
        cols = pl.ds(pl.multiple_of(chunk * D, D), D)
        total = jnp.zeros((1, D), F32)
        for r in range(rows):
            at = pl.ds(r * length, length)
            grad_act = mm(gdl_ref[at, :], down_ref[...], NT)
            low = (grad_act * slope_ref[at, cols].astype(F32)).astype(BF)
            slope_ref[at, cols] = low
            total += jnp.sum(low.astype(F32), axis=0, keepdims=True)
            acc_ref[at, :] += mm(low, up_ref[...], NT)
        ups_ref[:, cols] = total
        low = slope_ref[:, cols]
        send_up_ref[...] = mm(mid_ref[:, away], low, TN).astype(BF)
        keep_up_ref[...] = mm(mid_ref[:, here], low, TN).astype(BF)

    for first, out in ((chunks, send_down_ref), (chunks + chunks // 2, keep_down_ref)):

        @pl.when((step >= first) & (step < first + chunks // 2))
        def _(out=out):
            cols = pl.ds(pl.multiple_of(chunk_of(step, core, chunks) * D, D), D)
            out[...] = mm(act_ref[:, cols], gdl_ref[...], TN).astype(BF)

    @pl.when(step == 2 * chunks)
    def _():
        def one_row(r, carry):
            at = pl.ds(pl.multiple_of(r * length, length), length)
            grad_mid = acc_ref[at, :]
            normed = xhat_ref[r]
            scaled = grad_mid * g1_ref[...]
            grad_h1 = inv_ref[r, :, 0:1] * (scaled - row_mean(scaled) - normed * row_mean(scaled * normed))
            gh1_ref[r] = grad_h1
            low = grad_h1.astype(BF)
            gal_ref[r] = low
            gdl_ref[at, :] = low
            sums1_ref[r, 0:1, :] = jnp.sum(grad_mid * normed, axis=0, keepdims=True)
            sums1_ref[r, 1:2, :] = jnp.sum(grad_mid, axis=0, keepdims=True)
            sums1_ref[r, 2:3, :] = jnp.sum(low.astype(F32), axis=0, keepdims=True)
            return carry

        lax.fori_loop(0, rows, one_row, 0)
        send_up_ref[...] = mm(ctxt_ref[away, :], gdl_ref[...]).astype(BF)
        keep_up_ref[...] = mm(ctxt_ref[here, :], gdl_ref[...]).astype(BF)


def chunk_of(step, core, chunks):
    back = step - chunks
    half = chunks // 2
    later = back - half
    return jnp.where(step < chunks, step, jnp.where(back < half, (1 - core) * half + back, core * half + jnp.minimum(later, half - 1)))


def run_feed_both(sides, xhat, inv, ids, counts, pooled_grad, ctxt, g1, s1, up, upb, down, downb, g2, s2):
    rows, length, _ = xhat.shape
    tokens, chunks, half = rows * length, FF // D, D // 2
    halves = chunks // 2
    vectors = [g1[None], s1[None], upb[None], downb[None], g2[None], s2[None]]
    counts = counts.astype(F32)[:, :, None]
    ready = [xhat, inv, ids[:, :, None], ids[:, None, :], counts, pooled_grad, from_far(ctxt), *vectors]
    fixed = lambda shape: pl.BlockSpec(shape, lambda t, sd: (0,) * len(shape), pipeline_mode=pl.Buffered(1))
    backward = lambda t, sd: chunk_of(jnp.maximum(t, chunks), sd[0], chunks)
    up_at = lambda t, sd: (0, jnp.where(t < 2 * chunks, backward(t, sd), chunks))
    return pl.pallas_call(
        feed_both,
        grid_spec=pltpu.PrefetchScalarGridSpec(
            num_scalar_prefetch=1,
            grid=(2 * chunks + 1,),
            in_specs=[fixed(v.shape) for v in ready]
            + [pl.BlockSpec((D, D), lambda t, sd: (0, chunk_of(t, sd[0], chunks))), pl.BlockSpec((D, D), lambda t, sd: (chunk_of(t, sd[0], chunks), 0))],
            out_specs=[
                pl.BlockSpec((D, D), lambda t, sd: (jnp.clip(t - chunks, 0, halves - 1), 0)),
                pl.BlockSpec((D, D), lambda t, sd: (jnp.clip(t - chunks - halves, 0, halves - 1), 0)),
                pl.BlockSpec((half, D), up_at),
                pl.BlockSpec((half, D), up_at),
                fixed((rows, length, D)),
                fixed((rows, length, D)),
                fixed((rows, SEGS, D)),
                fixed((rows, 8, D)),
                fixed((rows, 8, D)),
                fixed((1, FF)),
            ],
            scratch_shapes=[
                pltpu.VMEM((tokens, D), BF),
                pltpu.VMEM((tokens, FF), BF),
                pltpu.VMEM((tokens, FF), BF),
                pltpu.VMEM((tokens, D), BF),
                pltpu.VMEM((tokens, D), F32),
            ],
        ),
        out_shape=[
            far((FF // 2, D), BF),
            far((FF // 2, D), BF),
            far((half, FF + D), BF),
            far((half, FF + D), BF),
            far((rows, length, D), F32),
            far((rows, length, D), BF),
            jax.ShapeDtypeStruct((rows, SEGS, D), F32),
            jax.ShapeDtypeStruct((rows, 8, D), F32),
            jax.ShapeDtypeStruct((rows, 8, D), F32),
            jax.ShapeDtypeStruct((1, FF), F32),
        ],
        compiler_params=params(52),
        cost_estimate=busy(50),
        name="feed_both",
    )(sides, *ready, from_far(up), from_far(down))


GROUP = 2
GROUP_WIDTH = GROUP * PAIR


def attend_backward(gal_ref, q_ref, k_ref, v_ref, lse_ref, idc_ref, idr_ref, wo_ref, gqkv_ref, sums_ref, mask_ref, gctx_ref):
    length = gal_ref.shape[0]
    gctx_ref[...] = mm(gal_ref[...], wo_ref[...], NT).astype(BF)
    mask_ref[...] = jnp.where(idc_ref[...] == idr_ref[...], 0.0, MASK_FILL)
    low_strip = lax.broadcasted_iota(jnp.int32, (STRIP, PAIR), 1) < HEAD_DIM
    low = lax.broadcasted_iota(jnp.int32, (length, PAIR), 1) < HEAD_DIM

    def pair_step(p, carry):
        at = pl.multiple_of(p * PAIR, PAIR)
        keys = k_ref[:, pl.ds(at, PAIR)]
        values = v_ref[:, pl.ds(at, PAIR)]
        key_of = [jnp.where(low, keys, BF(0)), jnp.where(low, BF(0), keys)]
        grad_k = jnp.zeros((length, PAIR), F32)
        grad_v = jnp.zeros((length, PAIR), F32)
        for s in range(length // STRIP):
            rows = pl.ds(s * STRIP, STRIP)
            lses = lse_ref[pl.ds(pl.multiple_of(8 * p, 8), 8), rows]
            queries = q_ref[rows, pl.ds(at, PAIR)]
            grads = gctx_ref[rows, pl.ds(at, PAIR)]
            grad_q = jnp.zeros((STRIP, PAIR), F32)
            for h in range(2):
                pick = (lambda v: jnp.where(low_strip, v, BF(0))) if h == 0 else (lambda v: jnp.where(low_strip, BF(0), v))
                query, grad = pick(queries), pick(grads)
                scores = mm(keys, query, NT) + mask_ref[:, rows]
                probs = jnp.exp(scores - lses[h : h + 1, :])
                grad_p = mm(values, grad, NT)
                inner = jnp.sum(probs * grad_p, axis=0, keepdims=True)
                grad_s = (probs * (grad_p - inner)).astype(BF)
                grad_v += mm(probs.astype(BF), grad)
                grad_k += mm(grad_s, query)
                grad_q += mm(grad_s, key_of[h], TN)
            gqkv_ref[rows, pl.ds(at, PAIR)] = (grad_q * HEAD_DIM**-0.5).astype(BF)
        gqkv_ref[:, pl.ds(GROUP_WIDTH + at, PAIR)] = grad_k.astype(BF)
        gqkv_ref[:, pl.ds(2 * GROUP_WIDTH + at, PAIR)] = grad_v.astype(BF)
        return carry

    lax.fori_loop(0, GROUP, pair_step, 0)
    sums_ref[...] = jnp.sum(gqkv_ref[...].astype(F32), axis=0, keepdims=True)


def run_attend_backward(group, gal, qkv, lse, ids, wo):
    rows, length, _ = gal.shape
    groups = D // GROUP_WIDTH
    row_spec = lambda *tail: pl.BlockSpec((None,) + tail, lambda r: (r,) + (0,) * len(tail))
    part = lambda c: pl.BlockSpec((None, length, GROUP_WIDTH), lambda r: (r, 0, c * groups + group))
    return pl.pallas_call(
        attend_backward,
        grid=(rows,),
        in_specs=[
            row_spec(length, D), part(0), part(1), part(2),
            pl.BlockSpec((None, 8 * GROUP, length), lambda r: (r, group, 0)),
            row_spec(length, 1), row_spec(1, length),
            pl.BlockSpec((GROUP_WIDTH, D), lambda r: (group, 0)),
        ],
        out_specs=[row_spec(length, 3 * GROUP_WIDTH), row_spec(1, 3 * GROUP_WIDTH)],
        scratch_shapes=[pltpu.VMEM((length, length), F32), pltpu.VMEM((length, GROUP_WIDTH), BF)],
        out_shape=[far((rows, length, 3 * GROUP_WIDTH), BF), jax.ShapeDtypeStruct((rows, 1, 3 * GROUP_WIDTH), F32)],
        compiler_params=params(20),
        cost_estimate=busy(14),
        name="attend_backward",
    )(from_far(gal), *[from_far(qkv)] * 3, from_far(lse), ids[:, :, None], ids[:, None, :], from_far(wo))


def input_grad(at_ref, gh1_ref, *refs):
    parts, (wqkv_ref, own_ref, send_ref) = refs[:-3], refs[-3:]
    half = gh1_ref.shape[0] // 2
    for out, first in ((own_ref, at_ref[0]), (send_ref, 1 - at_ref[0])):
        rows = pl.ds(pl.multiple_of(first * half, half), half)
        total = gh1_ref[rows, :]
        for g, part in enumerate(parts):
            for c in range(3):
                total += mm(part[rows, c * GROUP_WIDTH : (c + 1) * GROUP_WIDTH], wqkv_ref[:, c * D + g * GROUP_WIDTH : c * D + (g + 1) * GROUP_WIDTH], NT)
        out[...] = total.astype(BF)


def run_input_grad(at, gh1, parts, wqkv):
    rows, length, _ = gh1.shape
    half = length // 2
    row_spec = lambda *tail: pl.BlockSpec((None,) + tail, lambda r, at: (r,) + (0,) * len(tail))
    return pl.pallas_call(
        input_grad,
        grid_spec=pltpu.PrefetchScalarGridSpec(
            num_scalar_prefetch=1,
            grid=(rows,),
            in_specs=[row_spec(length, D)] + [row_spec(length, 3 * GROUP_WIDTH)] * len(parts) + [whole((D, 3 * D))],
            out_specs=[row_spec(half, D), row_spec(half, D)],
        ),
        out_shape=[jax.ShapeDtypeStruct((rows, half, D), BF)] * 2,
        compiler_params=params(18),
        cost_estimate=busy(6),
        name="input_grad",
    )(at, from_far(gh1), *map(from_far, parts), from_far(wqkv))


SMALLS = 128


def gather_small(sums1_ref, sums2_ref, ups_ref, sq_refs, small_ref, pack_ref):
    pack_ref[...] = jnp.zeros_like(pack_ref)
    total = lambda ref: jnp.sum(ref[...], axis=0)
    first, second, ups = total(sums1_ref), total(sums2_ref), ups_ref[...]
    for g, ref in enumerate(sq_refs):
        cols = slice(g * GROUP_WIDTH, (g + 1) * GROUP_WIDTH)
        pack_ref[0:1, cols] = total(ref)[:, :GROUP_WIDTH]
        pack_ref[1:2, cols] = total(ref)[:, 2 * GROUP_WIDTH :]
    lines = [first[2:3], first[0:1], first[1:2], second[2:3], second[0:1], second[1:2]]
    lines += [ups[:, i * D : (i + 1) * D] for i in range(FF // D)]
    for i, line in enumerate(lines):
        pack_ref[i + 2 : i + 3, :] = line
    small_ref[...] = jnp.transpose(pack_ref[...])


def qkv_grads_body(parts, sides_ref, x_away_ref, x_here_ref, *refs):
    grads, refs = refs[:parts], refs[parts:]
    small_in, (away_ref, here_ref, small_ref, pack_ref) = refs[:-4], refs[-4:]
    half, wide = x_away_ref.shape[0], 3 * GROUP_WIDTH
    gather_small(*small_in[:3], small_in[3:], small_ref, pack_ref)
    for left, out, first in ((x_away_ref, away_ref, 1 - sides_ref[0]), (x_here_ref, here_ref, sides_ref[0])):
        for g, grad in enumerate(grads):
            out[:, g * wide : (g + 1) * wide] = mm(left[...], grad[...]).astype(BF)
        rows = pl.ds(pl.multiple_of(first * half, half), half)
        out[:, parts * wide :] = small_ref[rows, :].astype(BF)


def qkv_grads(sides, x, grads, smalls):
    half, tokens = D // 2, x.shape[1]
    width = 3 * GROUP_WIDTH * len(grads) + SMALLS
    return pl.pallas_call(
        functools.partial(qkv_grads_body, len(grads)),
        grid_spec=pltpu.PrefetchScalarGridSpec(
            num_scalar_prefetch=1,
            grid=(1,),
            in_specs=[pl.BlockSpec((half, tokens), lambda j, sd: (1 - sd[0], 0)), pl.BlockSpec((half, tokens), lambda j, sd: (sd[0], 0))]
            + [whole(v.shape) for v in (*grads, *smalls)],
            out_specs=[pl.BlockSpec((half, width), lambda j, sd: (0, 0))] * 2,
            scratch_shapes=[pltpu.VMEM((D, SMALLS), F32), pltpu.VMEM((SMALLS, D), F32)],
        ),
        out_shape=[far((half, width), BF)] * 2,
        compiler_params=params(24),
        cost_estimate=busy(7),
        name="qkv_grads",
    )(sides, *[from_far(x)] * 2, *map(from_far, grads), *smalls)


def add_split_body(at_ref, keep_away_ref, keep_here_ref, got_away_ref, got_here_ref, send_ref, next_ref):
    send_ref[...] = (keep_away_ref[...].astype(F32) + got_away_ref[...].astype(F32)).astype(BF)
    next_ref[...] = keep_here_ref[...].astype(F32) + got_here_ref[...].astype(F32)


def add_split(at, keep, got):
    half, width = keep.shape[0] // 2, keep.shape[1]
    cols = width // 2 if width % 256 == 0 else width
    away = pl.BlockSpec((half, cols), lambda j, at: (1 - at[0], j))
    here = pl.BlockSpec((half, cols), lambda j, at: (at[0], j))
    return pl.pallas_call(
        add_split_body,
        grid_spec=pltpu.PrefetchScalarGridSpec(
            num_scalar_prefetch=1,
            grid=(width // cols,),
            in_specs=[away, here, away, here],
            out_specs=[pl.BlockSpec((half, cols), lambda j, at: (0, j))] * 2,
        ),
        out_shape=[far((half, width), BF), far((half, width), F32)],
        compiler_params=params(16),
        cost_estimate=busy(3),
        name="add_split",
    )(at, *[from_far(keep)] * 2, got, got)


def assemble_body(steps, moves, place_ref, *refs):
    outs = refs[len(refs) - len(moves) :]
    pieces = refs[: len(refs) - len(moves)]
    at = pl.program_id(0) // steps
    for p in range(4):

        @pl.when(at == p)
        def _(p=p):
            for out, parts in zip(outs, moves):
                for source, first, width, to in parts:
                    out[:, to : to + width] = pieces[4 * source + p][:, first : first + width].astype(F32)


def assemble(places, sources, moves):
    quarter = sources[0][0].shape[0]
    block = min(quarter, 384)
    steps = quarter // block
    widths = [sum(part[2] for part in parts) for parts in moves]
    piece_at = lambda p, width: pl.BlockSpec((block, width), lambda i, pos: (jnp.clip(i - p * steps, 0, steps - 1), 0))
    return pl.pallas_call(
        functools.partial(assemble_body, steps, moves),
        grid_spec=pltpu.PrefetchScalarGridSpec(
            num_scalar_prefetch=1,
            grid=(4 * steps,),
            in_specs=[piece_at(p, pieces[p].shape[1]) for pieces in sources for p in range(4)],
            out_specs=[pl.BlockSpec((block, w), lambda i, pos: (pos[i // steps] * steps + i % steps, 0)) for w in widths],
        ),
        out_shape=[jax.ShapeDtypeStruct((4 * quarter, w), F32) for w in widths],
        compiler_params=params(36),
        cost_estimate=busy(8),
        name="assemble",
    )(places, *[piece for pieces in sources for piece in pieces])


class Links:
    def __init__(self):
        dp, seq = lax.axis_size("dp"), lax.axis_size("seq")
        dp_at, seq_at = lax.axis_index("dp"), lax.axis_index("seq")
        self.core = dp_at % 2

        def flip(bit_of):
            pairs = []
            for d in range(dp):
                for s in range(seq):
                    bit = bit_of(d % 2)
                    to = (d, s ^ 1) if bit < 0 else (d ^ (1 << bit), s)
                    pairs.append((d * seq + s, to[0] * seq + to[1]))
            return pairs

        second = (dp_at >> 1) % 2
        self.side_a = jnp.where(self.core == 0, second, seq_at)
        self.side_b = jnp.where(self.core == 0, seq_at, second)
        self.pairs_core = flip(lambda c: 0)
        self.pairs_a = flip(lambda c: 1 if c == 0 else -1)
        self.pairs_b = flip(lambda c: -1 if c == 0 else 1)
        bits = list(range(2, (dp - 1).bit_length()))
        self.rest = []
        for first in range(0, len(bits), 2):
            part = bits[first : first + 2]
            size = 1 << len(part)
            routes = [[(d * seq + s, (d ^ (hop << part[0])) * seq + s) for d in range(dp) for s in range(seq)] for hop in range(1, size)]
            self.rest.append((routes, (dp_at >> part[0]) % size))
        self.sides = jnp.stack([self.core, self.side_a]).astype(jnp.int32)
        self.side_a_array = self.side_a.astype(jnp.int32).reshape(1)
        self.side_b_array = self.side_b.astype(jnp.int32).reshape(1)
        other = 2 * (1 - self.core)
        mine = 2 * self.core
        self.places = jnp.stack([mine + self.side_a, mine + 1 - self.side_a, other + self.side_b, other + 1 - self.side_b]).astype(jnp.int32)

    def send(self, value, pairs):
        return lax.ppermute(value, ("dp", "seq"), pairs)


class Order:
    def __init__(self):
        self.last = None

    def run(self, step, first, *others):
        if self.last is not None:
            first, self.last = lax.optimization_barrier((first, self.last))
        out = step(first, *others)
        self.last = jax.tree.leaves(out)[0]
        return out

    def arrive(self, value):
        value, self.last = lax.optimization_barrier((value, self.last))
        return value


def collect(at, pieces):
    swap = 1
    while swap < len(pieces):
        bit = (at // swap) % 2
        pieces = [jnp.where(bit == 0, pieces[i], pieces[i ^ swap]) for i in range(len(pieces))]
        swap *= 2
    return jnp.concatenate(pieces)


def exchange(order, links, away, keep, done, finish):
    got = links.send(away, links.pairs_core)
    yield
    away, keep = order.run(lambda g: add_split(links.side_a_array, keep, g), got)
    got = links.send(away, links.pairs_a)
    yield
    away, keep = order.run(lambda g: add_split(links.side_b_array, keep, g), got)
    got = links.send(away, links.pairs_b)
    yield
    for routes, at in links.rest:
        piece = keep.shape[0] // (len(routes) + 1)

        def deal(got, keep=keep, at=at, piece=piece, routes=routes):
            part = lambda v, to: lax.dynamic_slice_in_dim(v, to * piece, piece, 0).astype(F32)
            both = lambda to: part(keep, to) + part(got, to)
            return [both(at ^ hop).astype(BF) for hop in range(1, len(routes) + 1)], both(at)

        parts, keep = order.run(deal, got)
        got = [links.send(p, pairs) for p, pairs in zip(parts, routes)]
        yield
        got = order.run(lambda g, *rest: sum(v.astype(F32) for v in (g, *rest)), *got)
    cur = (keep + got.astype(F32)).astype(BF)
    for routes, at in links.rest[::-1]:
        got = [links.send(cur, pairs) for pairs in routes]
        yield
        cur = order.run(lambda g, *rest: collect(at, [cur, g, *rest]), *got)
    got = links.send(cur, links.pairs_b)
    yield
    cur = order.run(lambda g: collect(links.side_b, [cur, g]), got)
    got = links.send(cur, links.pairs_a)
    across = links.send(cur, links.pairs_core)
    yield
    got = order.arrive(got)
    done.append([cur, got, across, links.send(got, links.pairs_core)])
    yield
    if finish is not None:
        done.append(order.run(lambda g: finish([cur, got, across, g]), done[0][3]))
        yield


SCHEDULE = "mduqmmqqdmudqumdqudmqumdquqddqududduquudu"


def swap_seq(value):
    return lax.ppermute(value, "seq", [(0, 1), (1, 0)])


def local(
    hidden_in,
    segment_ids,
    segment_counts,
    pooled_grad,
    qkv_weight,
    query_bias,
    value_bias,
    out_weight,
    out_bias,
    norm1_gain,
    norm1_shift,
    up_weight,
    up_bias,
    down_weight,
    down_bias,
    norm2_gain,
    norm2_shift,
):
    links = Links()
    seq_at = lax.axis_index("seq")
    seq_array = seq_at.astype(jnp.int32).reshape(1)
    micro, row_count, piece, _ = hidden_in.shape
    length = piece * 2
    own_micro = micro // 2
    rows = own_micro * row_count
    tokens = rows * length

    def own_part(value):
        return lax.dynamic_slice_in_dim(value, seq_at * own_micro, own_micro, 0)

    got = swap_seq(lax.dynamic_slice_in_dim(hidden_in, (1 - seq_at) * own_micro, own_micro, 0))
    counts = own_part(segment_counts).reshape(rows, SEGS)
    pooled_cot = own_part(pooled_grad).reshape(rows, SEGS, D)
    seg = jnp.arange(SEGS, dtype=jnp.int32)
    ends = jnp.sum(jnp.where(seg[None, :, None] <= seg[None, None, :], counts[:, :, None], 0), axis=1)
    positions = jnp.arange(length, dtype=jnp.int32)
    ids = jnp.sum((positions[None, :, None] >= ends[:, None, :-1]).astype(jnp.int32), axis=-1)
    shift_qkv = jnp.concatenate([query_bias, jnp.zeros((D,), F32), value_bias])

    order = Order()
    qkv, x_turned, ctx_turned, lse, xhat, inv = run_attend_forward(
        seq_array,
        hidden_in.reshape(micro * row_count, piece, D),
        got.reshape(rows, piece, D),
        ids,
        qkv_weight,
        shift_qkv,
        out_weight,
        out_bias,
    )
    order.last = xhat
    away_down, keep_down, away_up, keep_up, grad_h1, grad_attn_low, pooled, sums1, sums2, ups = run_feed_both(
        links.sides, xhat, inv, ids, counts, pooled_cot, ctx_turned, norm1_gain, norm1_shift,
        up_weight, up_bias, down_weight, down_bias, norm2_gain, norm2_shift,
    )
    order.last = away_down
    streams, sums, state = {}, {name: [] for name in ("down", "up", "qkv")}, {}
    finishes = {
        "down": lambda pieces: assemble(links.places, [pieces], [[(0, 0, D, 0)]]),
        "up": lambda pieces: assemble(links.places, [pieces], [[(0, 0, FF, 0)], [(0, FF, D, 0)]]),
    }

    def start(name, away, keep):
        streams[name] = exchange(order, links, away, keep, sums[name], finishes.get(name))
        next(streams[name])

    def joined(first, second):
        return jnp.where(seq_at == 0, jnp.concatenate([first, second]), jnp.concatenate([second, first]))

    def main_steps():
        start("down", away_down, keep_down)
        start("up", away_up, keep_up)
        pooled_own = pooled.reshape(own_micro, row_count, SEGS, D)
        pooled_got = swap_seq(pooled_own)
        grads, sums_qkv = [], []
        for group in range(D // GROUP_WIDTH):
            grad, total = order.run(lambda g: run_attend_backward(group, g, qkv, lse, ids, out_weight), grad_attn_low)
            grads.append(grad)
            sums_qkv.append(total)
            yield
        flat = [g.reshape(tokens, 3 * GROUP_WIDTH) for g in grads]
        smalls = (sums1, sums2, ups, *sums_qkv)
        start("qkv", *order.run(lambda g: qkv_grads(links.sides, x_turned, [*flat[:-1], g], smalls), flat[-1]))
        yield
        back_own, back_send = order.run(lambda g: run_input_grad(seq_array, g, grads, qkv_weight), grad_h1)
        shape = (own_micro, row_count, piece, D)
        back_own, back_got = back_own.reshape(shape), swap_seq(back_send.reshape(shape))
        yield
        state["pooled"] = order.run(lambda g: joined(pooled_own, g), pooled_got)
        yield
        state["input"] = order.run(lambda g: joined(back_own, g), back_got)
        yield

    streams["main"] = main_steps()
    for name in map({"m": "main", "d": "down", "u": "up", "q": "qkv"}.get, SCHEDULE):
        if name in streams:
            next(streams[name], None)
    while streams:
        for name in list(streams):
            if next(streams[name], streams) is streams:
                del streams[name]
    pooled_local, input_local = state["pooled"], state["input"]
    (down_all,) = sums["down"][1]
    up_all, out_all = sums["up"][1]
    wide = 3 * GROUP_WIDTH
    columns = [(0, g * wide + c * GROUP_WIDTH, GROUP_WIDTH, c * D + g * GROUP_WIDTH) for g in range(D // GROUP_WIDTH) for c in range(3)]
    qkv_all, small_all = assemble(links.places, sums["qkv"], [columns, [(0, 3 * D, SMALLS, 0)]])
    lines = small_all[:, : 8 + FF // D].T
    return (
        pooled_local,
        input_local,
        qkv_all,
        lines[0],
        lines[1],
        out_all,
        lines[2],
        lines[3],
        lines[4],
        up_all,
        lines[8 : 8 + FF // D].reshape(FF),
        down_all,
        lines[5],
        lines[6],
        lines[7],
    )


def solution(mesh):
    rep = P()
    in_specs = (
        P(None, "dp", "seq", None),
        P(None, "dp", "seq"),
        P(None, "dp", None),
        P(None, "dp", None, None),
    ) + (rep,) * 13
    out_specs = (P(None, "dp", None, None), P(None, "dp", "seq", None)) + (rep,) * 13
    return jax.shard_map(local, mesh=mesh, in_specs=in_specs, out_specs=out_specs, check_vma=False)
```

time: 450 us -> 326 us (0.72)
  Pallas kernels: 228 us -> 162 us
  starting transfers between devices: 80.5 us -> 51.9 us
  waiting for transfers between devices: 110 us -> 83.8 us
  local copies, waits for them, and re-layouts: 19.9 us -> 11 us
    pallas_call x12 -> x9, Pallas kernels: 181 us -> 122 us  [the longest x1 51.8 us: run_feed_both(): pl.pallas_call(feed_both, grid_spec=pltpu.PrefetchScalarGridSpec(num_scal...]
    ppermute x33 -> x39, waiting for transfers between devices: 99 us -> 67.1 us  [send(): return lax.ppermute(value, ('dp', 'seq'), pairs)]
    ppermute x33 -> x39, starting transfers between devices: 74.1 us -> 46 us  [send(): return lax.ppermute(value, ('dp', 'seq'), pairs)]
    pallas_call x1, Pallas kernels: 38.2 us -> 21 us  [run_attend_forward(): pl.pallas_call(attend_forward, grid_spec=pltpu.PrefetchScalarGridSpec(num...]
    pallas_call x3 -> x6, Pallas kernels: 9.14 us -> 19.2 us  [add_split(): pl.pallas_call(add_split_body, grid_spec=pltpu.PrefetchScalarGridSpec(num...]
    ppermute x3, waiting for transfers between devices: 10.9 us -> 16.8 us  [swap_seq(): return lax.ppermute(value, 'seq', [(0, 1), (1, 0)])]
    convert_element_type x4 -> x7, other arithmetic: 0.1 us -> 5.67 us  [the longest x3 3.41 us: deal(): both(at ^ hop).astype(BF)]
  transfers between devices with their start and end apart: 36 -> 42, of which waited for: 15 -> 18; matrix products, arithmetic and copies ran while one was open for 5% -> 4% of each run, Pallas kernels for 26% -> 27%
where the time goes in v3:
time: 326 us; the launch traced here: 322 us
  Pallas kernels  162 us (50%)
  waiting for transfers between devices  83.8 us (26%)
  starting transfers between devices  51.9 us (16%)
  other arithmetic  11.3 us (3%)
  local copies, waits for them, and re-layouts  11 us (3%)
    ppermute x39, waiting for transfers between devices, send(): return lax.ppermute(value, ('dp', 'seq'), pairs)  67.1 us
    pallas_call x1, Pallas kernels, run_feed_both(): pl.pallas_call(feed_both, grid_spec=pltpu.PrefetchScalarGridSpec(num_scal...  51.8 us
    ppermute x39, starting transfers between devices, send(): return lax.ppermute(value, ('dp', 'seq'), pairs)  46 us
    pallas_call x3, Pallas kernels, run_attend_backward(): pl.pallas_call(attend_backward, grid=(rows,), in_specs=[row_spec(length,...  34.5 us
    pallas_call x1, Pallas kernels, run_attend_forward(): pl.pallas_call(attend_forward, grid_spec=pltpu.PrefetchScalarGridSpec(num...  21 us
    pallas_call x6, Pallas kernels, add_split(): pl.pallas_call(add_split_body, grid_spec=pltpu.PrefetchScalarGridSpec(num...  19.2 us
    pallas_call x3, Pallas kernels, assemble(): pl.pallas_call(functools.partial(assemble_body, steps, moves), grid_spec=...  19 us
    ppermute x3, waiting for transfers between devices, swap_seq(): return lax.ppermute(value, 'seq', [(0, 1), (1, 0)])  16.8 us
  transfers between devices with their start and end apart: 42, of which 18 were waited for; matrix products, arithmetic and copies ran while one was open for 4% of the time, Pallas kernels for 27%

profile of v3, /device:TPU:0, one launch (start us, length us, event | category | flops | bytes accessed | tf_op | source)
XLA Modules:
  0.0 321.5 jit_solution(15755832708296427899)
XLA Ops:
  0.8 2.2 constant_dynamic-slice_fusion.1
  3.0 3.0 collective-permute-start
  7.0 16.7 %collective-permute-done = bf16[2,1,256,768]{3,2,0,1:T(8,128)(2,1)S(1)} collective-permute-done((bf16[2,1,256,768]{3,2,0,1:T(8,128)(2,1)}, bf16[2,1,256,768]{3,2,0,1:T(8,128)(2,1)S(1)}, u32[]{:S(2)}, u32[]{:S(2)}) %collective-permute-start) | collective-permute-done | bytes 786464 | tf_op jit(solution)/shard_map/ppermute | solution.py:634
  23.7 2.0 copy-done.3
  25.7 1.4 copy-done.4
  27.1 21.0 %attend_forward.1 = (bf16[2,512,2304]{2,1,0:T(8,128)(2,1)}, bf16[768,1024]{1,0:T(8,128)(2,1)}, bf16[768,1024]{1,0:T(8,128)(2,1)}, f32[2,48,512]{2,1,0:T(8,128)},...) custom-call(s32[1]{0:T(128)} %bitcast.2.at_ref, bf16[4,256,768]{2,1,0:T(8,128)(2,1)S(1)} %bitcast.29, ...), custom_call_target="tpu_custom_call" | custom-call | flops 38000000 | tf_op jit(solution)/shard_map/attend_forward/pallas_call | solution.py:114
  48.1 1.7 copy-done.5
  49.8 51.8 %feed_both.1 = (bf16[1536,768]{1,0:T(8,128)(2,1)}, bf16[1536,768]{1,0:T(8,128)(2,1)}, bf16[384,3840]{1,0:T(8,128)(2,1)}, bf16[384,3840]{1,0:T(8,128)(2,1)}, f32[...) custom-call(s32[2]{0:T(128)S(1)} %pad_add_fusion.sides_ref, ...), custom_call_target="tpu_custom_call" | custom-call | flops 50000000 | tf_op jit(solution)/shard_map/feed_both/pallas_call | solution.py:274
  102.1 11.7 %attend_backward.3 = (bf16[2,512,768]{2,1,0:T(8,128)(2,1)}, f32[2,1,768]{2,1,0:T(1,128)S(1)}) custom-call(bf16[2,512,768]{2,1,0:T(8,128)(2,1)} %get-tuple-element.105.gal_ref, bf16[2,512,2304]{2,1,0:T(8,128)(2,1)} %get-tuple-element.93.q_ref.k_ref.v_ref, bf16[2,512,2304]{2,1,0:T(8,128)(2,1)} %get-tuple-element.93.q_ref.k_ref.v_ref, ...), custom_call_target="tpu_custom_call" | custom-call | flops 14000000 | tf_op jit(solution)/shard_map/attend_backward/pallas_call | solution.py:368
  113.8 3.2 %add_split.6 = (bf16[768,768]{1,0:T(8,128)(2,1)}, f32[768,768]{1,0:T(8,128)}) custom-call(s32[1]{0:T(128)} %bitcast.1.at_ref, bf16[1536,768]{1,0:T(8,128)(2,1)} %get-tuple-element.89.keep_away_ref.keep_here_ref, bf16[1536,768]{1,0:T(8,128)(2,1)} %get-tuple-element.89.keep_away_ref.keep_here_ref, ...), custom_call_target="tpu_custom_call" | custom-call | flops 3000000 | tf_op jit(solution)/shard_map/add_split/pallas_call | solution.py:477
  117.0 1.7 collective-permute-start.3
  118.8 3.7 %add_split.7 = (bf16[192,3840]{1,0:T(8,128)(2,1)}, f32[192,3840]{1,0:T(8,128)}) custom-call(s32[1]{0:T(128)} %bitcast.1.at_ref, bf16[384,3840]{1,0:T(8,128)(2,1)} %get-tuple-element.99.keep_away_ref.keep_here_ref, bf16[384,3840]{1,0:T(8,128)(2,1)} %get-tuple-element.99.keep_away_ref.keep_here_ref, ...), custom_call_target="tpu_custom_call" | custom-call | flops 3000000 | tf_op jit(solution)/shard_map/add_split/pallas_call | solution.py:477
  122.7 11.4 %attend_backward.4 = (bf16[2,512,768]{2,1,0:T(8,128)(2,1)}, f32[2,1,768]{2,1,0:T(1,128)S(1)}) custom-call(bf16[2,512,768]{2,1,0:T(8,128)(2,1)} %get-tuple-element.105.gal_ref, bf16[2,512,2304]{2,1,0:T(8,128)(2,1)} %get-tuple-element.93.q_ref.k_ref.v_ref, bf16[2,512,2304]{2,1,0:T(8,128)(2,1)} %get-tuple-element.93.q_ref.k_ref.v_ref, ...), custom_call_target="tpu_custom_call" | custom-call | flops 14000000 | tf_op jit(solution)/shard_map/attend_backward/pallas_call | solution.py:368
  134.1 11.4 %attend_backward.5 = (bf16[2,512,768]{2,1,0:T(8,128)(2,1)}, f32[2,1,768]{2,1,0:T(1,128)S(1)}) custom-call(bf16[2,512,768]{2,1,0:T(8,128)(2,1)} %get-tuple-element.105.gal_ref, bf16[2,512,2304]{2,1,0:T(8,128)(2,1)} %get-tuple-element.93.q_ref.k_ref.v_ref, bf16[2,512,2304]{2,1,0:T(8,128)(2,1)} %get-tuple-element.93.q_ref.k_ref.v_ref, ...), custom_call_target="tpu_custom_call" | custom-call | flops 14000000 | tf_op jit(solution)/shard_map/attend_backward/pallas_call | solution.py:368
  145.6 2.7 add_split.8
  148.3 8.9 %qkv_grads.1 = (bf16[384,2432]{1,0:T(8,128)(2,1)}, bf16[384,2432]{1,0:T(8,128)(2,1)}) custom-call(s32[2]{0:T(128)S(1)} %pad_add_fusion.sides_ref, bf16[768,1024]{1,0:T(8,128)(2,1)} %get-tuple-element.111.x_away_ref.x_here_ref, bf16[768,1024]{1,0:T(8,128)(2,1)} %get-tuple-element.111.x_away_ref.x_here_ref, bf16[1024,768]{1,0:T(8,128)(2,1)} %bitcast.36, ...), custom_call_target="tpu_custom_call" | custom-call | flops 7000000 | tf_op jit(solution)/shard_map/qkv_grads/pallas_call | solution.py:450
  157.2 1.7 collective-permute-start.5
  159.0 3.6 %add_split.9 = (bf16[96,3840]{1,0:T(8,128)(2,1)}, f32[96,3840]{1,0:T(8,128)}) custom-call(s32[1]{0:T(128)} %bitcast.12.at_ref, f32[192,3840]{1,0:T(8,128)} %get-tuple-element.110.keep_away_ref.keep_here_ref, f32[192,3840]{1,0:T(8,128)} %get-tuple-element.110.keep_away_ref.keep_here_ref, bf16[192,3840]{1,0:T(8,128)(2,1)} %collective-permute-done.6.got_away_ref.got_here_ref, ...), custom_call_target="tpu_custom_call" | custom-call | flops 3000000 | tf_op jit(solution)/shard_map/add_split/pallas_call | solution.py:477
  163.0 4.5 %collective-permute-done.5 = bf16[384,768]{1,0:T(8,128)(2,1)} collective-permute-done((bf16[384,768]{1,0:T(8,128)(2,1)}, bf16[384,768]{1,0:T(8,128)(2,1)}, u32[]{:S(2)}, u32[]{:S(2)}) %collective-permute-start.5) | collective-permute-done | bytes 589856 | tf_op jit(solution)/shard_map/ppermute | solution.py:562
  167.4 1.8 add_convert_fusion.7
  169.3 3.2 %add_split.10 = (bf16[192,2432]{1,0:T(8,128)(2,1)}, f32[192,2432]{1,0:T(8,128)}) custom-call(s32[1]{0:T(128)} %bitcast.1.at_ref, bf16[384,2432]{1,0:T(8,128)(2,1)} %get-tuple-element.125.keep_away_ref.keep_here_ref, bf16[384,2432]{1,0:T(8,128)(2,1)} %get-tuple-element.125.keep_away_ref.keep_here_ref, ...), custom_call_target="tpu_custom_call" | custom-call | flops 3000000 | tf_op jit(solution)/shard_map/add_split/pallas_call | solution.py:477
  172.5 1.7 collective-permute-start.14
  174.2 1.5 collective-permute-start.1
  175.7 1.6 collective-permute-start.7
  177.3 2.5 collective-permute-start.11
  179.9 1.5 add_convert_fusion.2
  181.4 7.6 %input_grad.1 = (bf16[2,256,768]{2,1,0:T(8,128)(2,1)S(1)}, bf16[2,256,768]{2,1,0:T(8,128)(2,1)S(1)}) custom-call(s32[1]{0:T(128)} %bitcast.2.at_ref, f32[2,512,768]{2,1,0:T(8,128)} %get-tuple-element.129.gh1_ref, bf16[2,512,768]{2,1,0:T(8,128)(2,1)} %get-tuple-element.95.refs_0_, bf16[2,512,768]{2,1,0:T(8,128)(2,1)} %get-tuple-element.104.refs_1_, ...), custom_call_target="tpu_custom_call" | custom-call | flops 6000000 | tf_op jit(solution)/shard_map/input_grad/pallas_call | solution.py:402
  189.0 1.9 collective-permute-start.13
  190.8 1.7 collective-permute-start.15
  192.5 1.9 collective-permute-start.16
  195.4 2.0 collective-permute-start.18
  197.4 2.7 add_split.11
  201.1 10.5 %collective-permute-done.15 = bf16[24,3840]{1,0:T(8,128)(2,1)S(1)} collective-permute-done((bf16[24,3840]{1,0:T(8,128)(2,1)S(1)}, bf16[24,3840]{1,0:T(8,128)(2,1)S(1)}, u32[]{:S(2)}, u32[]{:S(2)}) %collective-permute-start.15) | collective-permute-done | bytes 184352 | tf_op jit(solution)/shard_map/ppermute | solution.py:562
  211.6 1.5 collective-permute-start.19
  213.1 1.2 add_convert_fusion
  214.2 3.0 collective-permute-done.12
  217.2 3.8 %collective-permute-start.23 = (bf16[24,3840]{1,0:T(8,128)(2,1)S(1)}, bf16[24,3840]{1,0:T(8,128)(2,1)S(1)}, u32[]{:S(2)}, u32[]{:S(2)}) collective-permute-start(bf16[24,3840]{1,0:T(8,128)(2,1)S(1)} %add_convert_fusion), channel_id=1, source_target_pairs={{0,24},{1,25},{2,26},{3,27},{4,28},{5,29},{6,30},{7,31},{8,16},{9,... | collective-permute-start | bytes 552968 | tf_op jit(solution)/shard_map/ppermute | solution.py:562
  221.1 1.1 collective-permute-start.22
  222.2 6.0 %collective-permute-done.17 = bf16[96,768]{1,0:T(8,128)(2,1)S(1)} collective-permute-done((bf16[96,768]{1,0:T(8,128)(2,1)S(1)}, bf16[96,768]{1,0:T(8,128)(2,1)S(1)}, u32[]{:S(2)}, u32[]{:S(2)}) %collective-permute-start.17) | collective-permute-done | bytes 147488 | tf_op jit(solution)/shard_map/ppermute | solution.py:562
  228.2 2.3 collective-permute-start.21
  231.4 5.8 %collective-permute-done.21 = bf16[96,2432]{1,0:T(8,128)(2,1)S(1)} collective-permute-done((bf16[96,2432]{1,0:T(8,128)(2,1)}, bf16[96,2432]{1,0:T(8,128)(2,1)S(1)}, u32[]{:S(2)}, u32[]{:S(2)}) %collective-permute-start.21) | collective-permute-done | bytes 466976 | tf_op jit(solution)/shard_map/ppermute | solution.py:562
  237.2 2.0 collective-permute-start.25
  239.3 1.6 collective-permute-done.20
  240.9 3.8 %collective-permute-start.26 = (bf16[24,2432]{1,0:T(8,128)(2,1)S(1)}, bf16[24,2432]{1,0:T(8,128)(2,1)S(1)}, u32[]{:S(2)}, u32[]{:S(2)}) collective-permute-start(bf16[24,2432]{1,0:T(8,128)(2,1)S(1)} %get-tuple-element.239), channel_id=1, source_target_pairs={{0,16},{1,17},{2,18},{3,19},{4,20},{5,21},{6,22},{7,23},{8,24},{9,... | collective-permute-start | bytes 350216 | tf_op jit(solution)/shard_map/ppermute | solution.py:562
  245.5 1.6 collective-permute-start.29
  247.1 1.4 maximum_select_fusion
  248.8 2.4 collective-permute-done.26
  251.1 1.1 collective-permute-done.27
  252.3 2.9 collective-permute-start.31
  256.7 1.4 collective-permute-start.33
  258.1 6.8 %collective-permute-done.29 = bf16[96,3840]{1,0:T(8,128)(2,1)S(1)} collective-permute-done((bf16[96,3840]{1,0:T(8,128)(2,1)S(1)}, bf16[96,3840]{1,0:T(8,128)(2,1)S(1)}, u32[]{:S(2)}, u32[]{:S(2)}) %collective-permute-start.29) | collective-permute-done | bytes 737312 | tf_op jit(solution)/shard_map/ppermute | solution.py:562
  266.2 6.8 %collective-permute-done.33.refs_1_ = bf16[768,768]{1,0:T(8,128)(2,1)} collective-permute-done((bf16[768,768]{1,0:T(8,128)(2,1)S(1)}, bf16[768,768]{1,0:T(8,128)(2,1)}, u32[]{:S(2)}, u32[]{:S(2)}) %collective-permute-start.33) | collective-permute-done | bytes 1179680 | tf_op jit(solution)/shard_map/ppermute | solution.py:562
  273.6 2.0 collective-permute-start.32
  276.6 1.3 collective-permute-done.35.refs_3_
  277.9 8.7 %assemble.3 = f32[3072,768]{1,0:T(8,128)} custom-call(s32[4]{0:T(128)S(1)} %pad_add_fusion.1.place_ref, bf16[768,768]{1,0:T(8,128)(2,1)S(1)} %pad_maximum_fusion.1.refs_0_, bf16[768,768]{1,0:T(8,128)(2,1)} %collective-permute-done.33.refs_1_, bf16[768,768]{1,0:T(8,128)(2,1)} %collective-permute-done.34.refs_2_, bf16[768,768]{1,0:T(8,128)(2,1)} %collective-permute-done.35.refs_3_), custom_call_target="tpu_custom_call" | custom-call | flops 8000000 | tf_op jit(solution)/shard_map/assemble/pallas_call | solution.py:511
  287.4 1.2 broadcast_select_fusion.5
  288.7 8.6 %collective-permute-done.37.refs_1_ = bf16[192,3840]{1,0:T(8,128)(2,1)} collective-permute-done((bf16[192,3840]{1,0:T(8,128)(2,1)S(1)}, bf16[192,3840]{1,0:T(8,128)(2,1)}, u32[]{:S(2)}, u32[]{:S(2)}) %collective-permute-start.37) | collective-permute-done | bytes 1474592 | tf_op jit(solution)/shard_map/ppermute | solution.py:562
  298.0 1.2 collective-permute-start.36
  299.8 3.3 %collective-permute-done.39.refs_3_ = bf16[192,3840]{1,0:T(8,128)(2,1)S(1)} collective-permute-done((bf16[192,3840]{1,0:T(8,128)(2,1)}, bf16[192,3840]{1,0:T(8,128)(2,1)S(1)}, u32[]{:S(2)}, u32[]{:S(2)}) %collective-permute-start.39) | collective-permute-done | bytes 1474592 | tf_op jit(solution)/shard_map/ppermute | solution.py:562
  303.2 6.5 %assemble.4 = (f32[768,3072]{1,0:T(8,128)}, f32[768,768]{1,0:T(8,128)}) custom-call(s32[4]{0:T(128)S(1)} %pad_add_fusion.1.place_ref, bf16[192,3840]{1,0:T(8,128)(2,1)S(1)} %pad_maximum_fusion.refs_0_, bf16[192,3840]{1,0:T(8,128)(2,1)} %collective-permute-done.37.refs_1_, bf16[192,3840]{1,0:T(8,128)(2,1)S(1)} %collective-permute-done.38.refs_2_, ...), custom_call_target="tpu_custom_call" | custom-call | flops 8000000 | tf_op jit(solution)/shard_map/assemble/pallas_call | solution.py:511
  309.6 1.9 collective-permute-done.36.refs_1_
  311.6 2.5 collective-permute-done.41.refs_3_
  314.0 3.8 %assemble.5 = (f32[768,2304]{1,0:T(8,128)}, f32[768,128]{1,0:T(8,128)S(1)}) custom-call(s32[4]{0:T(128)S(1)} %pad_add_fusion.1.place_ref, bf16[192,2432]{1,0:T(8,128)(2,1)S(1)} %pad_maximum_fusion.2.refs_0_, bf16[192,2432]{1,0:T(8,128)(2,1)S(1)} %collective-permute-done.36.refs_1_, bf16[192,2432]{1,0:T(8,128)(2,1)S(1)} %collective-permute-done.40.refs_2_, ...), custom_call_target="tpu_custom_call" | custom-call | flops 8000000 | tf_op jit(solution)/shard_map/assemble/pallas_call | solution.py:511
  317.9 2.2 slice_reduce_fusion
  (118 shorter events, 14.1 us)
Async XLA Ops:
  0.6 6.3 %copy-start = (f32[4,1,32,768]{3,2,1,0:T(8,128)S(1)}, f32[4,1,32,768]{3,2,1,0:T(8,128)}, u32[]{:S(2)}) copy-start(f32[4,1,32,768]{3,2,1,0:T(8,128)} %param.19) | copy-start | bytes 1179652
  0.7 5.3 %copy-start.9 = (f32[768]{0:T(1024)S(1)}, f32[768]{0:T(1024)}, u32[]{:S(2)}) copy-start(f32[768]{0:T(1024)} %param.24) | copy-start | bytes 9220
  0.7 5.3 %copy-start.10 = (f32[768]{0:T(1024)S(1)}, f32[768]{0:T(1024)}, u32[]{:S(2)}) copy-start(f32[768]{0:T(1024)} %param.25) | copy-start | bytes 9220
  0.7 5.3 %copy-start.11 = (f32[768]{0:T(1024)S(1)}, f32[768]{0:T(1024)}, u32[]{:S(2)}) copy-start(f32[768]{0:T(1024)} %param.26) | copy-start | bytes 9220
  0.7 5.3 %copy-start.12 = (f32[768]{0:T(1024)S(1)}, f32[768]{0:T(1024)}, u32[]{:S(2)}) copy-start(f32[768]{0:T(1024)} %param.30) | copy-start | bytes 9220
  0.7 5.3 %copy-start.13 = (f32[768]{0:T(1024)S(1)}, f32[768]{0:T(1024)}, u32[]{:S(2)}) copy-start(f32[768]{0:T(1024)} %param.31) | copy-start | bytes 9220
  0.7 5.3 %copy-start.14 = (f32[768]{0:T(1024)S(1)}, f32[768]{0:T(1024)}, u32[]{:S(2)}) copy-start(f32[768]{0:T(1024)} %param.32) | copy-start | bytes 9220
  0.7 5.4 %copy-start.15 = (f32[768]{0:T(1024)S(1)}, f32[768]{0:T(1024)}, u32[]{:S(2)}) copy-start(f32[768]{0:T(1024)} %param.22) | copy-start | bytes 9220
  0.7 5.4 %copy-start.16 = (f32[768]{0:T(1024)S(1)}, f32[768]{0:T(1024)}, u32[]{:S(2)}) copy-start(f32[768]{0:T(1024)} %param.21) | copy-start | bytes 9220
  0.7 5.4 %copy-start.17 = (s32[4,1,32]{2,1,0:T(1,128)S(1)}, s32[4,1,32]{2,1,0:T(1,128)}, u32[]{:S(2)}) copy-start(s32[4,1,32]{2,1,0:T(1,128)} %param.18) | copy-start | bytes 1540
  0.8 23.0 %copy-start.2 = (bf16[768,768]{1,0:T(8,128)(2,1)S(1)}, bf16[768,768]{1,0:T(8,128)(2,1)}, u32[]{:S(2)}) copy-start(bf16[768,768]{1,0:T(8,128)(2,1)} %wo_ref.7) | copy-start | bytes 3538948
  3.0 20.7 %collective-permute-start = (bf16[2,1,256,768]{3,2,0,1:T(8,128)(2,1)}, bf16[2,1,256,768]{3,2,0,1:T(8,128)(2,1)S(1)}, u32[]{:S(2)}, u32[]{:S(2)}) collective-permute-start(bf16[2,1,256,768]{3,2,0,1:T(8,128)(2,1)} %constant_dynamic-slice_fusion.1), channel_id=1, source_target_pairs={{0,1},{1,0},{2,3},{3,2},{4,5},{5,4},{6,7},{7,6},{8,9},{9,8},{10,11... | collective-permute-start | bytes 2359304 | tf_op jit(solution)/shard_map/ppermute | solution.py:634
  23.7 2.0 copy-start.3
  25.7 1.4 copy-start.4
  27.1 22.7 %copy-start.6 = (f32[3072]{0:T(1024)S(1)}, f32[3072]{0:T(1024)}, u32[]{:S(2)}) copy-start(f32[3072]{0:T(1024)} %param.28) | copy-start | bytes 36868
  48.1 1.7 copy-start.5
  101.6 12.2 %collective-permute-start.2 = (bf16[1536,768]{1,0:T(8,128)(2,1)}, bf16[1536,768]{1,0:T(8,128)(2,1)S(1)}, u32[]{:S(2)}, u32[]{:S(2)}) collective-permute-start(bf16[1536,768]{1,0:T(8,128)(2,1)} %get-tuple-element.90), channel_id=1, source_target_pairs={{0,2},{1,3},{2,0},{3,1},{4,6},{5,7},{6,4},{7,5},{8,10},{9,11},{10,... | collective-permute-start | bytes 7077896 | tf_op jit(solution)/shard_map/ppermute | solution.py:562
  101.6 17.1 %collective-permute-start.4 = (bf16[384,3840]{1,0:T(8,128)(2,1)}, bf16[384,3840]{1,0:T(8,128)(2,1)S(1)}, u32[]{:S(2)}, u32[]{:S(2)}) collective-permute-start(bf16[384,3840]{1,0:T(8,128)(2,1)} %get-tuple-element.100), channel_id=1, source_target_pairs={{0,2},{1,3},{2,0},{3,1},{4,6},{5,7},{6,4},{7,5},{8,10},{9,11},{10,... | collective-permute-start | bytes 8847368 | tf_op jit(solution)/shard_map/ppermute | solution.py:562
  117.0 28.5 %collective-permute-start.3 = (bf16[768,768]{1,0:T(8,128)(2,1)}, bf16[768,768]{1,0:T(8,128)(2,1)S(1)}, u32[]{:S(2)}, u32[]{:S(2)}) collective-permute-start(bf16[768,768]{1,0:T(8,128)(2,1)} %get-tuple-element.98), channel_id=1, source_target_pairs={{0,4},{1,5},{2,3},{3,2},{4,0},{5,1},{6,7},{7,6},{8,12},{9,13},{10,... | collective-permute-start | bytes 3538952 | tf_op jit(solution)/shard_map/ppermute | solution.py:562
  122.4 36.5 %collective-permute-start.6 = (bf16[192,3840]{1,0:T(8,128)(2,1)}, bf16[192,3840]{1,0:T(8,128)(2,1)}, u32[]{:S(2)}, u32[]{:S(2)}) collective-permute-start(bf16[192,3840]{1,0:T(8,128)(2,1)} %get-tuple-element.102), channel_id=1, source_target_pairs={{0,4},{1,5},{2,3},{3,2},{4,0},{5,1},{6,7},{7,6},{8,12},{9,13},{10,... | collective-permute-start | bytes 4423688 | tf_op jit(solution)/shard_map/ppermute | solution.py:562
  157.2 12.0 %collective-permute-start.9 = (bf16[384,2432]{1,0:T(8,128)(2,1)}, bf16[384,2432]{1,0:T(8,128)(2,1)S(1)}, u32[]{:S(2)}, u32[]{:S(2)}) collective-permute-start(bf16[384,2432]{1,0:T(8,128)(2,1)} %get-tuple-element.119), channel_id=1, source_target_pairs={{0,2},{1,3},{2,0},{3,1},{4,6},{5,7},{6,4},{7,5},{8,10},{9,11},{10,... | collective-permute-start | bytes 5603336 | tf_op jit(solution)/shard_map/ppermute | solution.py:562
  157.2 10.2 %collective-permute-start.5 = (bf16[384,768]{1,0:T(8,128)(2,1)}, bf16[384,768]{1,0:T(8,128)(2,1)}, u32[]{:S(2)}, u32[]{:S(2)}) collective-permute-start(bf16[384,768]{1,0:T(8,128)(2,1)} %get-tuple-element.109), channel_id=1, source_target_pairs={{0,1},{1,0},{2,6},{3,7},{4,5},{5,4},{6,2},{7,3},{8,9},{9,8},{10,14... | collective-permute-start | bytes 1769480 | tf_op jit(solution)/shard_map/ppermute | solution.py:562
  159.0 8.5 %copy-start.7 = (f32[384,768]{1,0:T(8,128)S(1)}, f32[384,768]{1,0:T(8,128)}, u32[]{:S(2)}) copy-start(f32[384,768]{1,0:T(8,128)} %get-tuple-element.108) | copy-start | bytes 3538948
  162.6 17.2 %collective-permute-start.8 = (bf16[96,3840]{1,0:T(8,128)(2,1)}, bf16[96,3840]{1,0:T(8,128)(2,1)}, u32[]{:S(2)}, u32[]{:S(2)}) collective-permute-start(bf16[96,3840]{1,0:T(8,128)(2,1)} %get-tuple-element.121), channel_id=1, source_target_pairs={{0,1},{1,0},{2,6},{3,7},{4,5},{5,4},{6,2},{7,3},{8,9},{9,8},{10,14... | collective-permute-start | bytes 2211848 | tf_op jit(solution)/shard_map/ppermute | solution.py:562
  172.5 22.9 %collective-permute-start.14 = (bf16[192,2432]{1,0:T(8,128)(2,1)}, bf16[192,2432]{1,0:T(8,128)(2,1)S(1)}, u32[]{:S(2)}, u32[]{:S(2)}) collective-permute-start(bf16[192,2432]{1,0:T(8,128)(2,1)} %get-tuple-element.127), channel_id=1, source_target_pairs={{0,4},{1,5},{2,3},{3,2},{4,0},{5,1},{6,7},{7,6},{8,12},{9,13},{10,... | collective-permute-start | bytes 2801672 | tf_op jit(solution)/shard_map/ppermute | solution.py:562
  174.2 56.4 %collective-permute-start.1 = (f32[2,1,32,768]{3,2,0,1:T(8,128)S(1)}, f32[2,1,32,768]{3,2,0,1:T(8,128)S(1)}, u32[]{:S(2)}, u32[]{:S(2)}) collective-permute-start(f32[2,1,32,768]{3,2,0,1:T(8,128)S(1)} %bitcast.32), channel_id=1, source_target_pairs={{0,1},{1,0},{2,3},{3,2},{4,5},{5,4},{6,7},{7,6},{8,9},{9,8},{10,11... | collective-permute-start | bytes 589832 | tf_op jit(solution)/shard_map/ppermute | solution.py:634
  175.7 13.2 %collective-permute-start.7 = (bf16[96,768]{1,0:T(8,128)(2,1)}, bf16[96,768]{1,0:T(8,128)(2,1)S(1)}, u32[]{:S(2)}, u32[]{:S(2)}) collective-permute-start(bf16[96,768]{1,0:T(8,128)(2,1)} %get-tuple-element.234), channel_id=1, source_target_pairs={{0,8},{1,9},{2,10},{3,11},{4,12},{5,13},{6,14},{7,15},{8,0},{9,1},... | collective-permute-start | bytes 442376 | tf_op jit(solution)/shard_map/ppermute | solution.py:562
  177.3 13.5 %collective-permute-start.11 = (bf16[96,768]{1,0:T(8,128)(2,1)}, bf16[96,768]{1,0:T(8,128)(2,1)S(1)}, u32[]{:S(2)}, u32[]{:S(2)}) collective-permute-start(bf16[96,768]{1,0:T(8,128)(2,1)} %get-tuple-element.235), channel_id=1, source_target_pairs={{0,24},{1,25},{2,26},{3,27},{4,28},{5,29},{6,30},{7,31},{8,16},{9,... | collective-permute-start | bytes 442376 | tf_op jit(solution)/shard_map/ppermute | solution.py:562
  179.8 12.8 %collective-permute-start.10 = (bf16[96,768]{1,0:T(8,128)(2,1)S(1)}, bf16[96,768]{1,0:T(8,128)(2,1)S(1)}, u32[]{:S(2)}, u32[]{:S(2)}) collective-permute-start(bf16[96,768]{1,0:T(8,128)(2,1)S(1)} %get-tuple-element.236), channel_id=1, source_target_pairs={{0,16},{1,17},{2,18},{3,19},{4,20},{5,21},{6,22},{7,23},{8,24},{9,... | collective-permute-start | bytes 442376 | tf_op jit(solution)/shard_map/ppermute | solution.py:562
  189.0 11.4 %collective-permute-start.13 = (bf16[24,3840]{1,0:T(8,128)(2,1)S(1)}, bf16[24,3840]{1,0:T(8,128)(2,1)S(1)}, u32[]{:S(2)}, u32[]{:S(2)}) collective-permute-start(bf16[24,3840]{1,0:T(8,128)(2,1)S(1)} %get-tuple-element.233), channel_id=1, source_target_pairs={{0,8},{1,9},{2,10},{3,11},{4,12},{5,13},{6,14},{7,15},{8,0},{9,1},... | collective-permute-start | bytes 552968 | tf_op jit(solution)/shard_map/ppermute | solution.py:562
  190.8 20.8 %collective-permute-start.15 = (bf16[24,3840]{1,0:T(8,128)(2,1)S(1)}, bf16[24,3840]{1,0:T(8,128)(2,1)S(1)}, u32[]{:S(2)}, u32[]{:S(2)}) collective-permute-start(bf16[24,3840]{1,0:T(8,128)(2,1)S(1)} %get-tuple-element.231), channel_id=1, source_target_pairs={{0,16},{1,17},{2,18},{3,19},{4,20},{5,21},{6,22},{7,23},{8,24},{9,... | collective-permute-start | bytes 552968 | tf_op jit(solution)/shard_map/ppermute | solution.py:562
  192.5 19.1 %collective-permute-start.16 = (bf16[24,3840]{1,0:T(8,128)(2,1)S(1)}, bf16[24,3840]{1,0:T(8,128)(2,1)S(1)}, u32[]{:S(2)}, u32[]{:S(2)}) collective-permute-start(bf16[24,3840]{1,0:T(8,128)(2,1)S(1)} %get-tuple-element.232), channel_id=1, source_target_pairs={{0,24},{1,25},{2,26},{3,27},{4,28},{5,29},{6,30},{7,31},{8,16},{9,... | collective-permute-start | bytes 552968 | tf_op jit(solution)/shard_map/ppermute | solution.py:562
  195.4 25.7 %collective-permute-start.18 = (bf16[96,768]{1,0:T(8,128)(2,1)S(1)}, bf16[96,768]{1,0:T(8,128)(2,1)S(1)}, u32[]{:S(2)}, u32[]{:S(2)}) collective-permute-start(bf16[96,768]{1,0:T(8,128)(2,1)S(1)} %add_convert_fusion.4), channel_id=1, source_target_pairs={{0,24},{1,25},{2,26},{3,27},{4,28},{5,29},{6,30},{7,31},{8,16},{9,... | collective-permute-start | bytes 442376 | tf_op jit(solution)/shard_map/ppermute | solution.py:562
  200.4 27.8 %collective-permute-start.17 = (bf16[96,768]{1,0:T(8,128)(2,1)S(1)}, bf16[96,768]{1,0:T(8,128)(2,1)S(1)}, u32[]{:S(2)}, u32[]{:S(2)}) collective-permute-start(bf16[96,768]{1,0:T(8,128)(2,1)S(1)} %add_convert_fusion.4), channel_id=1, source_target_pairs={{0,16},{1,17},{2,18},{3,19},{4,20},{5,21},{6,22},{7,23},{8,24},{9,... | collective-permute-start | bytes 442376 | tf_op jit(solution)/shard_map/ppermute | solution.py:562
  211.6 5.6 %collective-permute-start.12 = (bf16[96,768]{1,0:T(8,128)(2,1)S(1)}, bf16[96,768]{1,0:T(8,128)(2,1)S(1)}, u32[]{:S(2)}, u32[]{:S(2)}) collective-permute-start(bf16[96,768]{1,0:T(8,128)(2,1)S(1)} %add_convert_fusion.4), channel_id=1, source_target_pairs={{0,8},{1,9},{2,10},{3,11},{4,12},{5,13},{6,14},{7,15},{8,0},{9,1},... | collective-permute-start | bytes 442376 | tf_op jit(solution)/shard_map/ppermute | solution.py:562
  211.6 33.8 %collective-permute-start.19 = (bf16[2,1,256,768]{3,2,0,1:T(8,128)(2,1)S(1)}, bf16[2,1,256,768]{3,2,0,1:T(8,128)(2,1)S(1)}, u32[]{:S(2)}, u32[]{:S(2)}) collective-permute-start(bf16[2,1,256,768]{3,2,0,1:T(8,128)(2,1)S(1)} %bitcast.35), channel_id=1, source_target_pairs={{0,1},{1,0},{2,3},{3,2},{4,5},{5,4},{6,7},{7,6},{8,9},{9,8},{10,11... | collective-permute-start | bytes 2359304 | tf_op jit(solution)/shard_map/ppermute | solution.py:634
  214.2 25.0 %copy-start.8 = (f32[96,2432]{1,0:T(8,128)S(1)}, f32[96,2432]{1,0:T(8,128)}, u32[]{:S(2)}) copy-start(f32[96,2432]{1,0:T(8,128)} %get-tuple-element.139) | copy-start | bytes 2801668
  217.2 23.7 %collective-permute-start.23 = (bf16[24,3840]{1,0:T(8,128)(2,1)S(1)}, bf16[24,3840]{1,0:T(8,128)(2,1)S(1)}, u32[]{:S(2)}, u32[]{:S(2)}) collective-permute-start(bf16[24,3840]{1,0:T(8,128)(2,1)S(1)} %add_convert_fusion), channel_id=1, source_target_pairs={{0,24},{1,25},{2,26},{3,27},{4,28},{5,29},{6,30},{7,31},{8,16},{9,... | collective-permute-start | bytes 552968 | tf_op jit(solution)/shard_map/ppermute | solution.py:562
  221.1 23.6 %collective-permute-start.22 = (bf16[24,3840]{1,0:T(8,128)(2,1)S(1)}, bf16[24,3840]{1,0:T(8,128)(2,1)S(1)}, u32[]{:S(2)}, u32[]{:S(2)}) collective-permute-start(bf16[24,3840]{1,0:T(8,128)(2,1)S(1)} %add_convert_fusion), channel_id=1, source_target_pairs={{0,16},{1,17},{2,18},{3,19},{4,20},{5,21},{6,22},{7,23},{8,24},{9,... | collective-permute-start | bytes 552968 | tf_op jit(solution)/shard_map/ppermute | solution.py:562
  228.2 9.1 %collective-permute-start.21 = (bf16[96,2432]{1,0:T(8,128)(2,1)}, bf16[96,2432]{1,0:T(8,128)(2,1)S(1)}, u32[]{:S(2)}, u32[]{:S(2)}) collective-permute-start(bf16[96,2432]{1,0:T(8,128)(2,1)} %get-tuple-element.134), channel_id=1, source_target_pairs={{0,1},{1,0},{2,6},{3,7},{4,5},{5,4},{6,2},{7,3},{8,9},{9,8},{10,14... | collective-permute-start | bytes 1400840 | tf_op jit(solution)/shard_map/ppermute | solution.py:562
  230.6 10.3 %collective-permute-start.20 = (bf16[24,3840]{1,0:T(8,128)(2,1)S(1)}, bf16[24,3840]{1,0:T(8,128)(2,1)S(1)}, u32[]{:S(2)}, u32[]{:S(2)}) collective-permute-start(bf16[24,3840]{1,0:T(8,128)(2,1)S(1)} %add_convert_fusion), channel_id=1, source_target_pairs={{0,8},{1,9},{2,10},{3,11},{4,12},{5,13},{6,14},{7,15},{8,0},{9,1},... | collective-permute-start | bytes 552968 | tf_op jit(solution)/shard_map/ppermute | solution.py:562
  237.2 11.3 %collective-permute-start.25 = (bf16[384,768]{1,0:T(8,128)(2,1)S(1)}, bf16[384,768]{1,0:T(8,128)(2,1)S(1)}, u32[]{:S(2)}, u32[]{:S(2)}) collective-permute-start(bf16[384,768]{1,0:T(8,128)(2,1)S(1)} %pad_maximum_fusion.4), channel_id=1, source_target_pairs={{0,1},{1,0},{2,6},{3,7},{4,5},{5,4},{6,2},{7,3},{8,9},{9,8},{10,14... | collective-permute-start | bytes 1769480 | tf_op jit(solution)/shard_map/ppermute | solution.py:562
  240.9 7.9 %collective-permute-start.24 = (bf16[24,2432]{1,0:T(8,128)(2,1)S(1)}, bf16[24,2432]{1,0:T(8,128)(2,1)S(1)}, u32[]{:S(2)}, u32[]{:S(2)}) collective-permute-start(bf16[24,2432]{1,0:T(8,128)(2,1)S(1)} %get-tuple-element.241), channel_id=1, source_target_pairs={{0,8},{1,9},{2,10},{3,11},{4,12},{5,13},{6,14},{7,15},{8,0},{9,1},... | collective-permute-start | bytes 350216 | tf_op jit(solution)/shard_map/ppermute | solution.py:562
  240.9 10.2 %collective-permute-start.26 = (bf16[24,2432]{1,0:T(8,128)(2,1)S(1)}, bf16[24,2432]{1,0:T(8,128)(2,1)S(1)}, u32[]{:S(2)}, u32[]{:S(2)}) collective-permute-start(bf16[24,2432]{1,0:T(8,128)(2,1)S(1)} %get-tuple-element.239), channel_id=1, source_target_pairs={{0,16},{1,17},{2,18},{3,19},{4,20},{5,21},{6,22},{7,23},{8,24},{9,... | collective-permute-start | bytes 350216 | tf_op jit(solution)/shard_map/ppermute | solution.py:562
  244.7 7.5 %collective-permute-start.27 = (bf16[24,2432]{1,0:T(8,128)(2,1)S(1)}, bf16[24,2432]{1,0:T(8,128)(2,1)S(1)}, u32[]{:S(2)}, u32[]{:S(2)}) collective-permute-start(bf16[24,2432]{1,0:T(8,128)(2,1)S(1)} %get-tuple-element.240), channel_id=1, source_target_pairs={{0,24},{1,25},{2,26},{3,27},{4,28},{5,29},{6,30},{7,31},{8,16},{9,... | collective-permute-start | bytes 350216 | tf_op jit(solution)/shard_map/ppermute | solution.py:562
  245.5 19.5 %collective-permute-start.29 = (bf16[96,3840]{1,0:T(8,128)(2,1)S(1)}, bf16[96,3840]{1,0:T(8,128)(2,1)S(1)}, u32[]{:S(2)}, u32[]{:S(2)}) collective-permute-start(bf16[96,3840]{1,0:T(8,128)(2,1)S(1)} %pad_maximum_fusion.3), channel_id=1, source_target_pairs={{0,1},{1,0},{2,6},{3,7},{4,5},{5,4},{6,2},{7,3},{8,9},{9,8},{10,14... | collective-permute-start | bytes 2211848 | tf_op jit(solution)/shard_map/ppermute | solution.py:562
  252.3 13.0 %collective-permute-start.31 = (bf16[24,2432]{1,0:T(8,128)(2,1)S(1)}, bf16[24,2432]{1,0:T(8,128)(2,1)S(1)}, u32[]{:S(2)}, u32[]{:S(2)}) collective-permute-start(bf16[24,2432]{1,0:T(8,128)(2,1)S(1)} %add_convert_fusion.8), channel_id=1, source_target_pairs={{0,24},{1,25},{2,26},{3,27},{4,28},{5,29},{6,30},{7,31},{8,16},{9,... | collective-permute-start | bytes 350216 | tf_op jit(solution)/shard_map/ppermute | solution.py:562
  255.2 10.1 %collective-permute-start.30 = (bf16[24,2432]{1,0:T(8,128)(2,1)S(1)}, bf16[24,2432]{1,0:T(8,128)(2,1)S(1)}, u32[]{:S(2)}, u32[]{:S(2)}) collective-permute-start(bf16[24,2432]{1,0:T(8,128)(2,1)S(1)} %add_convert_fusion.8), channel_id=1, source_target_pairs={{0,16},{1,17},{2,18},{3,19},{4,20},{5,21},{6,22},{7,23},{8,24},{9,... | collective-permute-start | bytes 350216 | tf_op jit(solution)/shard_map/ppermute | solution.py:562
  255.9 9.4 %collective-permute-start.28 = (bf16[24,2432]{1,0:T(8,128)(2,1)S(1)}, bf16[24,2432]{1,0:T(8,128)(2,1)S(1)}, u32[]{:S(2)}, u32[]{:S(2)}) collective-permute-start(bf16[24,2432]{1,0:T(8,128)(2,1)S(1)} %add_convert_fusion.8), channel_id=1, source_target_pairs={{0,8},{1,9},{2,10},{3,11},{4,12},{5,13},{6,14},{7,15},{8,0},{9,1},... | collective-permute-start | bytes 350216 | tf_op jit(solution)/shard_map/ppermute | solution.py:562
  256.7 16.3 %collective-permute-start.33 = (bf16[768,768]{1,0:T(8,128)(2,1)S(1)}, bf16[768,768]{1,0:T(8,128)(2,1)}, u32[]{:S(2)}, u32[]{:S(2)}) collective-permute-start(bf16[768,768]{1,0:T(8,128)(2,1)S(1)} %pad_maximum_fusion.1.refs_0_), channel_id=1, source_target_pairs={{0,4},{1,5},{2,3},{3,2},{4,0},{5,1},{6,7},{7,6},{8,12},{9,13},{10,... | collective-permute-start | bytes 3538952 | tf_op jit(solution)/shard_map/ppermute | solution.py:562
  273.1 4.8 %collective-permute-start.35 = (bf16[768,768]{1,0:T(8,128)(2,1)}, bf16[768,768]{1,0:T(8,128)(2,1)}, u32[]{:S(2)}, u32[]{:S(2)}) collective-permute-start(bf16[768,768]{1,0:T(8,128)(2,1)} %collective-permute-done.33.refs_1_), channel_id=1, source_target_pairs={{0,2},{1,3},{2,0},{3,1},{4,6},{5,7},{6,4},{7,5},{8,10},{9,11},{10,... | collective-permute-start | bytes 3538952 | tf_op jit(solution)/shard_map/ppermute | solution.py:562
  273.1 4.8 %collective-permute-start.34 = (bf16[768,768]{1,0:T(8,128)(2,1)S(1)}, bf16[768,768]{1,0:T(8,128)(2,1)}, u32[]{:S(2)}, u32[]{:S(2)}) collective-permute-start(bf16[768,768]{1,0:T(8,128)(2,1)S(1)} %pad_maximum_fusion.1.refs_0_), channel_id=1, source_target_pairs={{0,2},{1,3},{2,0},{3,1},{4,6},{5,7},{6,4},{7,5},{8,10},{9,11},{10,... | collective-permute-start | bytes 3538952 | tf_op jit(solution)/shard_map/ppermute | solution.py:562
  273.6 13.9 %collective-permute-start.32 = (bf16[96,2432]{1,0:T(8,128)(2,1)}, bf16[96,2432]{1,0:T(8,128)(2,1)}, u32[]{:S(2)}, u32[]{:S(2)}) collective-permute-start(bf16[96,2432]{1,0:T(8,128)(2,1)} %pad_maximum_fusion.5), channel_id=1, source_target_pairs={{0,1},{1,0},{2,6},{3,7},{4,5},{5,4},{6,2},{7,3},{8,9},{9,8},{10,14... | collective-permute-start | bytes 1400840 | tf_op jit(solution)/shard_map/ppermute | solution.py:562
  275.6 21.7 %collective-permute-start.37 = (bf16[192,3840]{1,0:T(8,128)(2,1)S(1)}, bf16[192,3840]{1,0:T(8,128)(2,1)}, u32[]{:S(2)}, u32[]{:S(2)}) collective-permute-start(bf16[192,3840]{1,0:T(8,128)(2,1)S(1)} %pad_maximum_fusion.refs_0_), channel_id=1, source_target_pairs={{0,4},{1,5},{2,3},{3,2},{4,0},{5,1},{6,7},{7,6},{8,12},{9,13},{10,... | collective-permute-start | bytes 4423688 | tf_op jit(solution)/shard_map/ppermute | solution.py:562
  297.3 5.9 %collective-permute-start.39 = (bf16[192,3840]{1,0:T(8,128)(2,1)}, bf16[192,3840]{1,0:T(8,128)(2,1)S(1)}, u32[]{:S(2)}, u32[]{:S(2)}) collective-permute-start(bf16[192,3840]{1,0:T(8,128)(2,1)} %collective-permute-done.37.refs_1_), channel_id=1, source_target_pairs={{0,2},{1,3},{2,0},{3,1},{4,6},{5,7},{6,4},{7,5},{8,10},{9,11},{10,... | collective-permute-start | bytes 4423688 | tf_op jit(solution)/shard_map/ppermute | solution.py:562
  298.0 5.2 %collective-permute-start.38 = (bf16[192,3840]{1,0:T(8,128)(2,1)S(1)}, bf16[192,3840]{1,0:T(8,128)(2,1)S(1)}, u32[]{:S(2)}, u32[]{:S(2)}) collective-permute-start(bf16[192,3840]{1,0:T(8,128)(2,1)S(1)} %pad_maximum_fusion.refs_0_), channel_id=1, source_target_pairs={{0,2},{1,3},{2,0},{3,1},{4,6},{5,7},{6,4},{7,5},{8,10},{9,11},{10,... | collective-permute-start | bytes 4423688 | tf_op jit(solution)/shard_map/ppermute | solution.py:562
  298.0 13.6 %collective-permute-start.36 = (bf16[192,2432]{1,0:T(8,128)(2,1)S(1)}, bf16[192,2432]{1,0:T(8,128)(2,1)S(1)}, u32[]{:S(2)}, u32[]{:S(2)}) collective-permute-start(bf16[192,2432]{1,0:T(8,128)(2,1)S(1)} %pad_maximum_fusion.2.refs_0_), channel_id=1, source_target_pairs={{0,4},{1,5},{2,3},{3,2},{4,0},{5,1},{6,7},{7,6},{8,12},{9,13},{10,... | collective-permute-start | bytes 2801672 | tf_op jit(solution)/shard_map/ppermute | solution.py:562
  299.2 12.4 %collective-permute-start.40 = (bf16[192,2432]{1,0:T(8,128)(2,1)S(1)}, bf16[192,2432]{1,0:T(8,128)(2,1)S(1)}, u32[]{:S(2)}, u32[]{:S(2)}) collective-permute-start(bf16[192,2432]{1,0:T(8,128)(2,1)S(1)} %pad_maximum_fusion.2.refs_0_), channel_id=1, source_target_pairs={{0,2},{1,3},{2,0},{3,1},{4,6},{5,7},{6,4},{7,5},{8,10},{9,11},{10,... | collective-permute-start | bytes 2801672 | tf_op jit(solution)/shard_map/ppermute | solution.py:562
  311.6 2.5 collective-permute-start.41
  317.9 3.2 copy-start.1
